TPU v7x, 32 devices: a whole 2x2x4 slice. The times are simulated.
32 devices in a mesh: grp: 2 (over x), tok: 16 (over z, y, core).
Axes of the slice: x: 2, y: 2, z: 4, core: 2. Of those that a mesh axis runs over, the one named last changes fastest.
Arguments:
- tokens: bfloat16 [4096, 2048], P(('grp', 'tok')), parts along dimension 0, may hold values from -6 to 6
- norm_gain: float32 [2048], replicated, may hold values from 0.1 to 1.9
- expert_ids: int32 [4096, 8], P(('grp', 'tok')), parts along dimension 0, may hold values from 0 to 15, as said below
- gate_weights: float32 [4096, 8], P(('grp', 'tok')), parts along dimension 0, may hold values from 0.05 to 1
- owner_map: int32 [16], replicated, may hold values from 0 to 15, each once
- in_q: bfloat16 [16, 2, 2048, 768], P('tok'), may hold values from -0.125 to 0.125
- in_scale: bfloat16 [16, 2, 768], P('tok'), may hold values from 0.5 to 2
- down_q: bfloat16 [16, 768, 2048], P('tok'), may hold values from -0.21875 to 0.21875
- down_scale: bfloat16 [16, 2048], P('tok'), may hold values from 0.5 to 2
Outputs:
- moe_out: bfloat16 [4096, 2048], P(('grp', 'tok')), parts along dimension 0
There are 2 independent parts, one for each index of `grp`. A program takes and returns all parts, laid end to end along the dimension named above; an argument that names none is the same for every part. Nothing has to cross between parts.
Inputs may be any that keep to these rules, and one draw needn't show every extreme that they name: `expert_ids`: each row names 8 different experts. One and the same expert is named by exactly 96 of the 128 rows of every device; every other expert is named by between 32 and 80 rows of each device, and 80 is reached on every device. `owner_map`: every slot holds exactly one expert.
All inputs are finite; a program needn't handle non-finite values.
Results may differ from a plain program's by a relative error of at most 0.0071.
Values may be sent and summed in bfloat16 or wider, within the bound.
No kernel may reach another device: no remote copies, remote signals or barrier semaphores. Data moves between devices by JAX's collectives and lax.ppermute only.
A program may use at most 128 MiB of HBM per device.

v0:
```python
import jax
import jax.numpy as jnp
from jax import lax
from jax.sharding import PartitionSpec as P


def expert_rows(batch_rows, in_blocks, in_scales, down_block, down_scales):
    gate_part = jnp.dot(batch_rows, in_blocks[0], preferred_element_type=jnp.float32) * in_scales[0]
    up_part = jnp.dot(batch_rows, in_blocks[1], preferred_element_type=jnp.float32) * in_scales[1]
    hidden = (jax.nn.silu(gate_part) * up_part).astype(jnp.bfloat16)
    return (jnp.dot(hidden, down_block, preferred_element_type=jnp.float32) * down_scales).astype(
        jnp.bfloat16
    )


def on_device(
    tokens, norm_gain, expert_ids, gate_weights, owner_map, in_q, in_scale, down_q, down_scale
):
    tok_rows, model_width = tokens.shape
    top_count = expert_ids.shape[1]
    experts = owner_map.shape[0]
    mean_load = tok_rows * top_count // experts
    capacity = mean_load + mean_load // 2
    in_blocks = in_q[0]
    in_scales = in_scale[0]
    down_block = down_q[0]
    down_scales = down_scale[0]
    values = tokens.astype(jnp.float32)
    row_scale = lax.rsqrt(jnp.mean(values * values, axis=1, keepdims=True) + 1e-06)
    normed = (values * row_scale * norm_gain).astype(jnp.bfloat16)
    weights = gate_weights / jnp.sum(gate_weights, axis=1, keepdims=True)
    labels = jnp.arange(experts, dtype=jnp.int32)
    slot_table = jnp.sum(jnp.where(expert_ids[:, :, None] == labels, owner_map, 0), axis=2)
    flat_slot = slot_table.reshape(-1)
    onehot = (flat_slot[:, None] == labels).astype(jnp.int32)
    slot_rank = jnp.sum((jnp.cumsum(onehot, axis=0) - onehot) * onehot, axis=1)
    repeated = jnp.repeat(normed, top_count, axis=0)
    outgoing = (
        jnp.zeros((experts, capacity, model_width), jnp.bfloat16)
        .at[flat_slot, slot_rank]
        .set(repeated)
    )
    received = lax.all_to_all(outgoing, "tok", split_axis=0, concat_axis=0, tiled=True)
    source_count, slot_count, unused_width = received.shape
    flat_rows = received.reshape(source_count * slot_count, model_width)
    served = expert_rows(flat_rows, in_blocks, in_scales, down_block, down_scales)
    served = served.reshape(source_count, slot_count, model_width)
    returned_rows = lax.all_to_all(served, "tok", split_axis=0, concat_axis=0, tiled=True)
    picked = returned_rows[flat_slot, slot_rank].reshape(tok_rows, top_count, model_width)
    mixed = jnp.sum(weights[:, :, None] * picked.astype(jnp.float32), axis=1)
    return mixed.astype(jnp.bfloat16)


def solution(mesh):
    in_specs = (
        P(("grp", "tok"), None),
        P(),
        P(("grp", "tok"), None),
        P(("grp", "tok"), None),
        P(),
        P("tok", None, None, None),
        P("tok", None, None),
        P("tok", None, None),
        P("tok", None),
    )
    out_specs = P(("grp", "tok"), None)
    return jax.shard_map(
        on_device, mesh=mesh, in_specs=in_specs, out_specs=out_specs, check_vma=False
    )
```

profile of v0, /device:TPU:13, one launch (start us, length us, event | category | flops | bytes accessed | tf_op | source)
XLA Modules:
  0.0 364.9 jit_solution(7678618837900742371)
XLA Ops:
  0.0 0.0 copy-start
  0.0 0.9 select_reduce_fusion
  0.9 0.1 copy.19
  1.0 0.1 eq.45
  1.1 0.1 eq.41
  1.2 0.1 reshape.107
  1.3 4.5 %reduce-window.6 = s32[16,8,128]{2,1,0:T(8,128)S(1)} reduce-window(s32[16,8,128]{2,1,0:T(8,128)S(1)} %fusion.17, s32[]{:T(128)} %constant.10.clone.1), window={size=1x1x128 pad=0_0x0_0x127_0}, to_apply=%region_2.3 | reduce-window | flops 2080768 | bytes 131076 | tf_op jit(solution)/shard_map/reduce-window
  5.9 0.1 slice.30
  5.9 0.1 copy.22
  6.1 0.1 copy.23
  6.2 0.1 broadcast_add_fusion
  6.3 0.7 multiply_reduce_fusion
  7.1 0.8 and_reduce_fusion
  7.8 1.2 fusion.11
  9.1 2.0 fusion.13
  11.1 10.6 %scatter_custom_fusion = bf16[1536,2048]{1,0:T(8,128)(2,1)} fusion(s32[1024]{0:T(1024)S(1)} %broadcast_select_fusion, bf16[]{:T(256)} %constant.5.clone.1, bf16[128,2048]{1,0:T(8,128)(2,1)} %fusion.13), kind=kCustom, calls=%fused_computation.6 | custom fusion | bytes 6815746
  21.8 0.0 copy-start.3
  21.8 0.0 copy-start.2
  21.8 6.7 %all-to-all-start = ((bf16[16,96,2048]{2,1,0:T(8,128)(2,1)}), bf16[16,96,2048]{2,1,0:T(8,128)(2,1)}, u32[]{:S(2)}, u32[]{:S(2)}) async-start(bf16[16,96,2048]{2,1,0:T(8,128)(2,1)} %bitcast.43), calls=%async_computation | async-start | bytes 12582912 | tf_op jit(solution)/shard_map/all_to_all | solution.py:43
  28.4 0.0 copy-done.3
  28.4 0.0 copy-done.2
  28.5 137.3 %all-to-all-done = bf16[16,96,2048]{2,1,0:T(8,128)(2,1)} async-done(((bf16[16,96,2048]{2,1,0:T(8,128)(2,1)}), bf16[16,96,2048]{2,1,0:T(8,128)(2,1)}, u32[]{:S(2)}, u32[]{:S(2)}) %all-to-all-start) | async-done | bytes 6291488 | tf_op jit(solution)/shard_map/all_to_all | solution.py:43
  165.8 8.1 %fusion.5 = f32[1536,768]{1,0:T(8,128)S(1)} fusion(bf16[1536,2048]{1,0:T(8,128)(2,1)} %bitcast.5, bf16[1,2,2048,768]{3,2,1,0:T(8,128)(2,1)} %param.14), kind=kOutput, calls=%fused_computation.10 | convolution fusion | flops 4831838208 | bytes 14155776 | tf_op jit(solution)/shard_map/dot_general | solution.py:8
  173.9 8.6 %multiply_convert_fusion.1 = bf16[1536,768]{1,0:T(8,128)(2,1)S(1)} fusion(f32[1536,768]{1,0:T(8,128)S(1)} %fusion.5, bf16[1536,2048]{1,0:T(8,128)(2,1)} %bitcast.5, bf16[1,2,2048,768]{3,2,1,0:T(8,128)(2,1)} %param.14, f32[768]{0:T(1024)S(1)} %get-tuple-element.6, f32[768]{0:T(1024)S(1)} %get-tuple-element.5), kind=kOutput, calls=%fused_computation.5 | convolution fusion | flops 4841275392 | bytes 16521216 | tf_op jit(solution)/shard_map/dot_general | solution.py:9
  182.5 0.0 copy-done
  182.6 7.1 %multiply_convert_fusion = bf16[1536,2048]{1,0:T(8,128)(2,1)} fusion(bf16[1536,768]{1,0:T(8,128)(2,1)S(1)} %multiply_convert_fusion.1, f32[2048]{0:T(1024)S(1)} %bitcast.48, bf16[1,768,2048]{2,1,0:T(8,128)(2,1)S(1)} %copy-done), kind=kOutput, calls=%fused_computation.2 | convolution fusion | flops 4838129664 | bytes 11804672 | tf_op jit(solution)/shard_map/dot_general | solution.py:11
  189.6 0.0 copy-start.1
  189.6 4.9 %all-to-all-start.1 = ((bf16[16,96,2048]{2,1,0:T(8,128)(2,1)}), bf16[16,96,2048]{2,1,0:T(8,128)(2,1)}, u32[]{:S(2)}, u32[]{:S(2)}) async-start(bf16[16,96,2048]{2,1,0:T(8,128)(2,1)} %bitcast.44), calls=%async_computation.1 | async-start | bytes 12582912 | tf_op jit(solution)/shard_map/all_to_all | solution.py:48
  194.6 0.0 copy-done.1
  194.6 0.1 copy.18
  194.7 137.3 %all-to-all-done.1 = bf16[16,96,2048]{2,1,0:T(8,128)(2,1)} async-done(((bf16[16,96,2048]{2,1,0:T(8,128)(2,1)}), bf16[16,96,2048]{2,1,0:T(8,128)(2,1)}, u32[]{:S(2)}, u32[]{:S(2)}) %all-to-all-start.1) | async-done | bytes 6291488 | tf_op jit(solution)/shard_map/all_to_all | solution.py:48
  332.0 25.6 %gather_fusion = bf16[1024,2048]{1,0:T(8,128)(2,1)} fusion(bf16[16,96,2048]{2,1,0:T(8,128)(2,1)} %all-to-all-done.1, s32[1024]{0:T(1024)S(1)} %bitcast.42), kind=kCustom, calls=%fused_computation | custom fusion | bytes 8396800 | tf_op jit(solution)/shard_map/gather | solution.py:49
  357.6 7.3 %fusion = bf16[128,2048]{1,0:T(8,128)(2,1)} fusion(bf16[1024,2048]{1,0:T(8,128)(2,1)} %gather_fusion, f32[128,8]{1,0:T(8,128)S(1)} %copy.18), kind=kLoop, calls=%fused_computation.4 | loop fusion | flops 6029312 | bytes 4722688 | tf_op jit(solution)/shard_map/reduce_sum | solution.py:50
  (11 shorter events, 0.2 us)
Async XLA Ops:
  0.0 182.5 %copy-start = (bf16[1,768,2048]{2,1,0:T(8,128)(2,1)S(1)}, bf16[1,768,2048]{2,1,0:T(8,128)(2,1)}, u32[]{:S(2)}) copy-start(bf16[1,768,2048]{2,1,0:T(8,128)(2,1)} %param.16) | copy-start | bytes 9437188
  21.8 6.7 %copy-start.3 = (bf16[1,2048]{1,0:T(2,128)(2,1)S(1)}, bf16[1,2048]{1,0:T(2,128)(2,1)}, u32[]{:S(2)}) copy-start(bf16[1,2048]{1,0:T(2,128)(2,1)} %param.17) | copy-start | bytes 12292
  21.8 6.7 %copy-start.2 = (bf16[1,2,768]{2,1,0:T(2,128)(2,1)S(1)}, bf16[1,2,768]{2,1,0:T(2,128)(2,1)}, u32[]{:S(2)}) copy-start(bf16[1,2,768]{2,1,0:T(2,128)(2,1)} %param.15) | copy-start | bytes 9220
  21.8 144.1 %all-to-all-start = ((bf16[16,96,2048]{2,1,0:T(8,128)(2,1)}), bf16[16,96,2048]{2,1,0:T(8,128)(2,1)}, u32[]{:S(2)}, u32[]{:S(2)}) async-start(bf16[16,96,2048]{2,1,0:T(8,128)(2,1)} %bitcast.43), calls=%async_computation | async-start | bytes 12582912 | tf_op jit(solution)/shard_map/all_to_all | solution.py:43
  189.6 4.9 %copy-start.1 = (f32[128,8]{0,1:T(8,128)S(1)}, f32[128,8]{0,1:T(8,128)}, u32[]{:S(2)}) copy-start(f32[128,8]{0,1:T(8,128)} %param.12) | copy-start | bytes 12292
  189.6 142.3 %all-to-all-start.1 = ((bf16[16,96,2048]{2,1,0:T(8,128)(2,1)}), bf16[16,96,2048]{2,1,0:T(8,128)(2,1)}, u32[]{:S(2)}, u32[]{:S(2)}) async-start(bf16[16,96,2048]{2,1,0:T(8,128)(2,1)} %bitcast.44), calls=%async_computation.1 | async-start | bytes 12582912 | tf_op jit(solution)/shard_map/all_to_all | solution.py:48
where the time goes:
time: 366 us; the launch traced here: 365 us
  waiting for transfers between devices  275 us (75%)
  local copies, waits for them, and re-layouts  37.1 us (10%)
  matrix products  23.8 us (7%)
  other arithmetic  17.8 us (5%)
  starting transfers between devices  11.6 us (3%)
    all_to_all x1, waiting for transfers between devices, on_device(): lax.all_to_all(outgoing, 'tok', split_axis=0, concat_axis=0, tiled=True)  137 us
    all_to_all x1, waiting for transfers between devices, on_device(): lax.all_to_all(served, 'tok', split_axis=0, concat_axis=0, tiled=True)  137 us
    gather x1, local copies, waits for them, and re-layouts, on_device(): returned_rows[flat_slot, slot_rank]  25.6 us
    unnamed x9, local copies, waits for them, and re-layouts  10.7 us
    dot_general x1, matrix products, expert_rows(): jnp.dot(batch_rows, in_blocks[1], preferred_element_type=jnp.float32)  8.64 us
    dot_general x1, matrix products, expert_rows(): jnp.dot(batch_rows, in_blocks[0], preferred_element_type=jnp.float32)  8.06 us
    reduce_sum x1, other arithmetic, on_device(): mixed = jnp.sum(weights[:, :, None] * picked.astype(jnp.float32), axis=1)  7.33 us
  transfers between devices with their start and end apart: 2, of which 2 were waited for; matrix products, arithmetic and copies ran while one was open for 0% of the time, Pallas kernels for 0%

commit v1 on v0

--- a/solution.py
+++ b/solution.py
@@ -8,12 +8,16 @@
     gate_part = jnp.dot(batch_rows, in_blocks[0], preferred_element_type=jnp.float32) * in_scales[0]
     up_part = jnp.dot(batch_rows, in_blocks[1], preferred_element_type=jnp.float32) * in_scales[1]
     hidden = (jax.nn.silu(gate_part) * up_part).astype(jnp.bfloat16)
-    return (jnp.dot(hidden, down_block, preferred_element_type=jnp.float32) * down_scales).astype(
-        jnp.bfloat16
-    )
+    return jnp.dot(hidden, down_block, preferred_element_type=jnp.float32) * down_scales
 
 
-def on_device(
+def normalized(tokens, norm_gain):
+    values = tokens.astype(jnp.float32)
+    row_scale = lax.rsqrt(jnp.mean(values * values, axis=1, keepdims=True) + 1e-06)
+    return (values * row_scale * norm_gain).astype(jnp.bfloat16)
+
+
+def exchanged(
     tokens, norm_gain, expert_ids, gate_weights, owner_map, in_q, in_scale, down_q, down_scale
 ):
     tok_rows, model_width = tokens.shape
@@ -21,13 +25,7 @@
     experts = owner_map.shape[0]
     mean_load = tok_rows * top_count // experts
     capacity = mean_load + mean_load // 2
-    in_blocks = in_q[0]
-    in_scales = in_scale[0]
-    down_block = down_q[0]
-    down_scales = down_scale[0]
-    values = tokens.astype(jnp.float32)
-    row_scale = lax.rsqrt(jnp.mean(values * values, axis=1, keepdims=True) + 1e-06)
-    normed = (values * row_scale * norm_gain).astype(jnp.bfloat16)
+    normed = normalized(tokens, norm_gain)
     weights = gate_weights / jnp.sum(gate_weights, axis=1, keepdims=True)
     labels = jnp.arange(experts, dtype=jnp.int32)
     slot_table = jnp.sum(jnp.where(expert_ids[:, :, None] == labels, owner_map, 0), axis=2)
@@ -43,15 +41,81 @@
     received = lax.all_to_all(outgoing, "tok", split_axis=0, concat_axis=0, tiled=True)
     source_count, slot_count, unused_width = received.shape
     flat_rows = received.reshape(source_count * slot_count, model_width)
-    served = expert_rows(flat_rows, in_blocks, in_scales, down_block, down_scales)
-    served = served.reshape(source_count, slot_count, model_width)
+    served = expert_rows(flat_rows, in_q[0], in_scale[0], down_q[0], down_scale[0])
+    served = served.astype(jnp.bfloat16).reshape(source_count, slot_count, model_width)
     returned_rows = lax.all_to_all(served, "tok", split_axis=0, concat_axis=0, tiled=True)
     picked = returned_rows[flat_slot, slot_rank].reshape(tok_rows, top_count, model_width)
     mixed = jnp.sum(weights[:, :, None] * picked.astype(jnp.float32), axis=1)
     return mixed.astype(jnp.bfloat16)
 
 
+def ring_pairs(devices):
+    chips = devices // 2
+    loop = list(range(0, chips, 2)) + list(range(chips - 1, 0, -2))
+    pairs = []
+    for place, chip in enumerate(loop):
+        after = loop[(place + 1) % chips]
+        pairs.append((2 * chip, 2 * after))
+        pairs.append((2 * after + 1, 2 * chip + 1))
+    return pairs, chips
+
+
+def circulated(
+    tokens, norm_gain, expert_ids, gate_weights, owner_map, in_q, in_scale, down_q, down_scale
+):
+    tok_rows, model_width = tokens.shape
+    experts = owner_map.shape[0]
+    devices = lax.axis_size("tok")
+    ring, chips = ring_pairs(devices)
+    swap = [(i, i ^ 1) for i in range(devices)]
+    me = lax.axis_index("tok")
+    lanes = -(-2 * experts // 128) * 128
+    labels = jnp.arange(experts, dtype=jnp.int32)
+    my_expert = jnp.sum(jnp.where(owner_map == me, labels, 0))
+
+    normed = normalized(tokens, norm_gain)
+    weights = gate_weights / jnp.sum(gate_weights, axis=1, keepdims=True)
+    named = expert_ids[:, :, None] == labels
+    table = jnp.sum(jnp.where(named, weights[:, :, None], 0.0), axis=1)
+    high = lax.reduce_precision(table, 8, 7)
+    low = table - high
+    fill = jnp.zeros((tok_rows, lanes - 2 * experts), jnp.float32)
+    extra = jnp.concatenate([high, low, fill], axis=1).astype(jnp.bfloat16)
+    block = jnp.concatenate([normed, extra], axis=1)
+    lane = jnp.arange(lanes, dtype=jnp.int32)
+    mine = (lane == my_expert) | (lane == my_expert + experts)
+
+    def served(rows):
+        share = jnp.sum(jnp.where(mine, rows[:, model_width:].astype(jnp.float32), 0.0), axis=1)
+        out = expert_rows(rows[:, :model_width], in_q[0], in_scale[0], down_q[0], down_scale[0])
+        return out * share[:, None]
+
+    total = None
+    for step in range(chips):
+        other = lax.ppermute(block, "tok", swap)
+        both = served(jnp.concatenate([block, other], axis=0))
+        if step < chips - 1:
+            block = lax.ppermute(block, "tok", ring)
+        lent = lax.ppermute(both[tok_rows:].astype(jnp.bfloat16), "tok", swap)
+        part = both[:tok_rows] + lent.astype(jnp.float32)
+        if step == 0:
+            own = part
+            continue
+        if total is not None:
+            part = part + total.astype(jnp.float32)
+        total = lax.ppermute(part.astype(jnp.bfloat16), "tok", ring)
+    return (own + total.astype(jnp.float32)).astype(jnp.bfloat16)
+
+
 def solution(mesh):
+    def on_device(tokens, norm_gain, expert_ids, gate_weights, owner_map, *blocks):
+        tok_rows, experts = tokens.shape[0], owner_map.shape[0]
+        mean_load = tok_rows * expert_ids.shape[1] // experts
+        routed = experts * (mean_load + mean_load // 2)
+        dense = tok_rows * mesh.shape["tok"]
+        form = circulated if dense <= 2 * routed and mesh.shape["tok"] % 4 == 0 else exchanged
+        return form(tokens, norm_gain, expert_ids, gate_weights, owner_map, *blocks)
+
     in_specs = (
         P(("grp", "tok"), None),
         P(),

time: 366 us -> 185 us (0.51)
  the two profiles are of different devices: /device:TPU:13 before, /device:TPU:0 now
where the time goes in v1:
time: 185 us; the launch traced here: 184 us
  matrix products  68.9 us (37%)
  waiting for transfers between devices  41.4 us (22%)
  starting transfers between devices  27.4 us (15%)
  other arithmetic  25.2 us (14%)
  local copies, waits for them, and re-layouts  20 us (11%)
    dot_general x8, matrix products, expert_rows(): jnp.dot(hidden, down_block, preferred_element_type=jnp.float32)  46.8 us
    ppermute x7, waiting for transfers between devices, circulated(): block = lax.ppermute(block, 'tok', ring)  33 us
    dot_general x8, matrix products, expert_rows(): jnp.dot(batch_rows, in_blocks[0], preferred_element_type=jnp.float32)  22 us
    convert_element_type x7, other arithmetic, circulated(): total = lax.ppermute(part.astype(jnp.bfloat16), 'tok', ring)  16.1 us
    slice x8, local copies, waits for them, and re-layouts, circulated(): lent = lax.ppermute(both[tok_rows:].astype(jnp.bfloat16), 'tok', swap)  16.1 us
    ppermute x7, starting transfers between devices, circulated(): block = lax.ppermute(block, 'tok', ring)  15.5 us
    ppermute x7, starting transfers between devices, circulated(): total = lax.ppermute(part.astype(jnp.bfloat16), 'tok', ring)  11.1 us
    ppermute x7, waiting for transfers between devices, circulated(): total = lax.ppermute(part.astype(jnp.bfloat16), 'tok', ring)  8.42 us
  transfers between devices with their start and end apart: 30, of which 11 were waited for; matrix products, arithmetic and copies ran while one was open for 52% of the time, Pallas kernels for 0%

profile of v1, /device:TPU:0, one launch (start us, length us, event | category | flops | bytes accessed | tf_op | source)
XLA Modules:
  0.0 184.0 jit_solution(15212123844766037458)
XLA Ops:
  0.0 0.9 reduce_sum.109
  0.9 0.8 broadcast_divide_fusion
  1.7 0.7 select_reduce_fusion.8
  2.7 1.2 fusion.145
  3.9 2.0 %fusion.147 = bf16[128,2048]{1,0:T(8,128)(2,1)} fusion(bf16[128,2048]{1,0:T(8,128)(2,1)} %param.9, f32[2048]{0:T(1024)} %param.10, f32[128]{0:T(128)S(1)} %add_rsqrt_fusion), kind=kLoop, calls=%fused_computation.87 | loop fusion | flops 1048576 | bytes 1057280 | tf_op jit(solution)/shard_map/convert_element_type | solution.py:17
  5.9 1.9 %concatenate.30 = bf16[128,2176]{1,0:T(8,128)(2,1)} concatenate(bf16[128,2048]{1,0:T(8,128)(2,1)} %fusion.147, bf16[128,16]{1,0:T(8,128)(2,1)S(1)} %copy.12, bf16[128,16]{1,0:T(8,128)(2,1)S(1)} %copy.13, bf16[128,96]{1,0:T(8,128)(2,1)S(1)} %broadcast_in_dim.42), dimensions={1} | concatenate | bytes 1114112 | tf_op jit(solution)/shard_map/concatenate | solution.py:84
  7.8 3.1 %collective-permute-start.2 = (bf16[128,2176]{1,0:T(8,128)(2,1)}, bf16[128,2176]{1,0:T(8,128)(2,1)}, u32[]{:S(2)}, u32[]{:S(2)}) collective-permute-start(bf16[128,2176]{1,0:T(8,128)(2,1)} %concatenate.30), channel_id=1, source_target_pairs={{0,4},{5,1},{4,8},{9,5},{8,12},{13,9},{12,14},{15,13},{14,10},{11,... | collective-permute-start | bytes 1671176 | tf_op jit(solution)/shard_map/ppermute | solution.py:98
  10.9 0.6 fusion.270
  12.2 0.7 compare_or_fusion
  12.9 5.8 %collective-permute-done.2 = bf16[128,2176]{1,0:T(8,128)(2,1)} collective-permute-done((bf16[128,2176]{1,0:T(8,128)(2,1)}, bf16[128,2176]{1,0:T(8,128)(2,1)}, u32[]{:S(2)}, u32[]{:S(2)}) %collective-permute-start.2) | collective-permute-done | bytes 557088 | tf_op jit(solution)/shard_map/ppermute | solution.py:98
  18.6 2.1 %collective-permute-start.3 = (bf16[128,2176]{1,0:T(8,128)(2,1)}, bf16[128,2176]{1,0:T(8,128)(2,1)S(1)}, u32[]{:S(2)}, u32[]{:S(2)}) collective-permute-start(bf16[128,2176]{1,0:T(8,128)(2,1)} %collective-permute-done.2), channel_id=1, source_target_pairs={{0,4},{5,1},{4,8},{9,5},{8,12},{13,9},{12,14},{15,13},{14,10},{11,... | collective-permute-start | bytes 1671176 | tf_op jit(solution)/shard_map/ppermute | solution.py:98
  20.7 1.1 constant_dynamic-update-slice_fusion.13
  21.8 4.1 %fusion.96 = f32[256,768]{1,0:T(8,128)} fusion(bf16[1,2,2048,768]{3,2,1,0:T(8,128)(2,1)} %param.14, f32[768]{0:T(1024)S(1)} %get-tuple-element.6, bf16[128,2176]{1,0:T(8,128)(2,1)} %concatenate.30, bf16[128,2176]{1,0:T(8,128)(2,1)} %collective-permute-done), kind=kOutput, calls=%fused_computation.66 | convolution fusion | flops 807600128 | bytes 5049344 | tf_op jit(solution)/shard_map/dot_general | solution.py:8
  25.9 2.4 %collective-permute-done.3 = bf16[128,2176]{1,0:T(8,128)(2,1)S(1)} collective-permute-done((bf16[128,2176]{1,0:T(8,128)(2,1)}, bf16[128,2176]{1,0:T(8,128)(2,1)S(1)}, u32[]{:S(2)}, u32[]{:S(2)}) %collective-permute-start.3) | collective-permute-done | bytes 557088 | tf_op jit(solution)/shard_map/ppermute | solution.py:98
  28.4 2.1 %collective-permute-start.4 = (bf16[128,2176]{1,0:T(8,128)(2,1)S(1)}, bf16[128,2176]{1,0:T(8,128)(2,1)S(1)}, u32[]{:S(2)}, u32[]{:S(2)}) collective-permute-start(bf16[128,2176]{1,0:T(8,128)(2,1)S(1)} %collective-permute-done.3), channel_id=1, source_target_pairs={{0,4},{5,1},{4,8},{9,5},{8,12},{13,9},{12,14},{15,13},{14,10},{11,... | collective-permute-start | bytes 1671176 | tf_op jit(solution)/shard_map/ppermute | solution.py:98
  30.5 4.3 %fusion.117 = f32[256,768]{1,0:T(8,128)} fusion(bf16[256,2176]{1,0:T(8,128)(2,1)S(1)} %constant_dynamic-update-slice_fusion.12, bf16[1,2,2048,768]{3,2,1,0:T(8,128)(2,1)} %param.14, f32[768]{0:T(1024)S(1)} %get-tuple-element.6), kind=kOutput, calls=%fused_computation.73 | convolution fusion | flops 805502976 | bytes 4984832 | tf_op jit(solution)/shard_map/dot_general | solution.py:8
  34.9 3.0 %collective-permute-done.4 = bf16[128,2176]{1,0:T(8,128)(2,1)S(1)} collective-permute-done((bf16[128,2176]{1,0:T(8,128)(2,1)S(1)}, bf16[128,2176]{1,0:T(8,128)(2,1)S(1)}, u32[]{:S(2)}, u32[]{:S(2)}) %collective-permute-start.4) | collective-permute-done | bytes 557088 | tf_op jit(solution)/shard_map/ppermute | solution.py:98
  37.9 2.1 %collective-permute-start.5 = (bf16[128,2176]{1,0:T(8,128)(2,1)S(1)}, bf16[128,2176]{1,0:T(8,128)(2,1)S(1)}, u32[]{:S(2)}, u32[]{:S(2)}) collective-permute-start(bf16[128,2176]{1,0:T(8,128)(2,1)S(1)} %collective-permute-done.4), channel_id=1, source_target_pairs={{0,4},{5,1},{4,8},{9,5},{8,12},{13,9},{12,14},{15,13},{14,10},{11,... | collective-permute-start | bytes 1671176 | tf_op jit(solution)/shard_map/ppermute | solution.py:98
  40.1 1.9 %fusion.114 = f32[256,768]{1,0:T(8,128)} fusion(bf16[256,2176]{1,0:T(8,128)(2,1)S(1)} %constant_dynamic-update-slice_fusion.10, bf16[1,2,2048,768]{3,2,1,0:T(8,128)(2,1)S(1)} %bitcast.157, f32[768]{0:T(1024)S(1)} %get-tuple-element.6), kind=kOutput, calls=%fused_computation.72 | convolution fusion | flops 805502976 | bytes 4984832 | tf_op jit(solution)/shard_map/dot_general | solution.py:8
  42.0 5.4 %collective-permute-done.5 = bf16[128,2176]{1,0:T(8,128)(2,1)S(1)} collective-permute-done((bf16[128,2176]{1,0:T(8,128)(2,1)S(1)}, bf16[128,2176]{1,0:T(8,128)(2,1)S(1)}, u32[]{:S(2)}, u32[]{:S(2)}) %collective-permute-start.5) | collective-permute-done | bytes 557088 | tf_op jit(solution)/shard_map/ppermute | solution.py:98
  47.4 2.1 %collective-permute-start.6 = (bf16[128,2176]{1,0:T(8,128)(2,1)S(1)}, bf16[128,2176]{1,0:T(8,128)(2,1)S(1)}, u32[]{:S(2)}, u32[]{:S(2)}) collective-permute-start(bf16[128,2176]{1,0:T(8,128)(2,1)S(1)} %collective-permute-done.5), channel_id=1, source_target_pairs={{0,4},{5,1},{4,8},{9,5},{8,12},{13,9},{12,14},{15,13},{14,10},{11,... | collective-permute-start | bytes 1671176 | tf_op jit(solution)/shard_map/ppermute | solution.py:98
  49.6 1.9 %fusion.111 = f32[256,768]{1,0:T(8,128)} fusion(bf16[256,2176]{1,0:T(8,128)(2,1)S(1)} %constant_dynamic-update-slice_fusion.8, bf16[1,2,2048,768]{3,2,1,0:T(8,128)(2,1)S(1)} %bitcast.157, f32[768]{0:T(1024)S(1)} %get-tuple-element.6), kind=kOutput, calls=%fused_computation.71 | convolution fusion | flops 805502976 | bytes 4984832 | tf_op jit(solution)/shard_map/dot_general | solution.py:8
  51.5 5.5 %collective-permute-done.6 = bf16[128,2176]{1,0:T(8,128)(2,1)S(1)} collective-permute-done((bf16[128,2176]{1,0:T(8,128)(2,1)S(1)}, bf16[128,2176]{1,0:T(8,128)(2,1)S(1)}, u32[]{:S(2)}, u32[]{:S(2)}) %collective-permute-start.6) | collective-permute-done | bytes 557088 | tf_op jit(solution)/shard_map/ppermute | solution.py:98
  57.0 2.1 %collective-permute-start.7 = (bf16[128,2176]{1,0:T(8,128)(2,1)S(1)}, bf16[128,2176]{1,0:T(8,128)(2,1)S(1)}, u32[]{:S(2)}, u32[]{:S(2)}) collective-permute-start(bf16[128,2176]{1,0:T(8,128)(2,1)S(1)} %collective-permute-done.6), channel_id=1, source_target_pairs={{0,4},{5,1},{4,8},{9,5},{8,12},{13,9},{12,14},{15,13},{14,10},{11,... | collective-permute-start | bytes 1671176 | tf_op jit(solution)/shard_map/ppermute | solution.py:98
  59.2 1.9 %fusion.108 = f32[256,768]{1,0:T(8,128)} fusion(bf16[256,2176]{1,0:T(8,128)(2,1)S(1)} %constant_dynamic-update-slice_fusion.6, bf16[1,2,2048,768]{3,2,1,0:T(8,128)(2,1)S(1)} %bitcast.157, f32[768]{0:T(1024)S(1)} %get-tuple-element.6), kind=kOutput, calls=%fused_computation.70 | convolution fusion | flops 805502976 | bytes 4984832 | tf_op jit(solution)/shard_map/dot_general | solution.py:8
  61.0 5.4 %collective-permute-done.7 = bf16[128,2176]{1,0:T(8,128)(2,1)S(1)} collective-permute-done((bf16[128,2176]{1,0:T(8,128)(2,1)S(1)}, bf16[128,2176]{1,0:T(8,128)(2,1)S(1)}, u32[]{:S(2)}, u32[]{:S(2)}) %collective-permute-start.7) | collective-permute-done | bytes 557088 | tf_op jit(solution)/shard_map/ppermute | solution.py:98
  66.5 2.1 %collective-permute-start.8 = (bf16[128,2176]{1,0:T(8,128)(2,1)S(1)}, bf16[128,2176]{1,0:T(8,128)(2,1)S(1)}, u32[]{:S(2)}, u32[]{:S(2)}) collective-permute-start(bf16[128,2176]{1,0:T(8,128)(2,1)S(1)} %collective-permute-done.7), channel_id=1, source_target_pairs={{0,4},{5,1},{4,8},{9,5},{8,12},{13,9},{12,14},{15,13},{14,10},{11,... | collective-permute-start | bytes 1671176 | tf_op jit(solution)/shard_map/ppermute | solution.py:98
  68.7 1.9 %fusion.105 = f32[256,768]{1,0:T(8,128)} fusion(bf16[256,2176]{1,0:T(8,128)(2,1)S(1)} %constant_dynamic-update-slice_fusion.4, bf16[1,2,2048,768]{3,2,1,0:T(8,128)(2,1)S(1)} %bitcast.157, f32[768]{0:T(1024)S(1)} %get-tuple-element.6), kind=kOutput, calls=%fused_computation.69 | convolution fusion | flops 805502976 | bytes 4984832 | tf_op jit(solution)/shard_map/dot_general | solution.py:8
  70.6 5.4 %collective-permute-done.8 = bf16[128,2176]{1,0:T(8,128)(2,1)S(1)} collective-permute-done((bf16[128,2176]{1,0:T(8,128)(2,1)S(1)}, bf16[128,2176]{1,0:T(8,128)(2,1)S(1)}, u32[]{:S(2)}, u32[]{:S(2)}) %collective-permute-start.8) | collective-permute-done | bytes 557088 | tf_op jit(solution)/shard_map/ppermute | solution.py:98
  76.2 1.9 %fusion.102 = f32[256,768]{1,0:T(8,128)} fusion(bf16[256,2176]{1,0:T(8,128)(2,1)S(1)} %constant_dynamic-update-slice_fusion.2, bf16[1,2,2048,768]{3,2,1,0:T(8,128)(2,1)S(1)} %bitcast.157, f32[768]{0:T(1024)S(1)} %get-tuple-element.6), kind=kOutput, calls=%fused_computation.68 | convolution fusion | flops 805502976 | bytes 4984832 | tf_op jit(solution)/shard_map/dot_general | solution.py:8
  78.2 1.0 select_reduce_fusion
  79.2 5.8 %fusion.93 = f32[256,2048]{1,0:T(8,128)} fusion(bf16[1,768,2048]{2,1,0:T(8,128)(2,1)S(1)} %copy-done, f32[256]{0:T(256)S(1)} %get-tuple-element.7, f32[2048]{0:T(1024)S(1)} %bitcast.148, f32[256,768]{1,0:T(8,128)} %fusion.117, bf16[1,2,2048,768]{3,2,1,0:T(8,128)(2,1)} %param.14, bf16[256,2176]{1,0:T(8,128)(2,1)} %copy-done.6, f32[768]{0:T(1024)S(1)} %get-tuple-element.5), kind=kOutput, calls=%fused_computation.63 | convolution fusion | flops 1613037568 | bytes 10235904 | tf_op jit(solution)/shard_map/dot_general | solution.py:11
  85.1 2.1 %slice.435 = bf16[128,2048]{1,0:T(8,128)(2,1)} slice(f32[256,2048]{1,0:T(8,128)} %fusion.93), slice={[128:256], [0:2048]} | slice | bytes 1048576 | tf_op jit(solution)/shard_map/slice | solution.py:99
  87.7 5.9 %fusion.87 = f32[256,2048]{1,0:T(8,128)} fusion(bf16[1,768,2048]{2,1,0:T(8,128)(2,1)S(1)} %copy-done, f32[256]{0:T(256)S(1)} %get-tuple-element.13, f32[2048]{0:T(1024)S(1)} %bitcast.149, f32[256,768]{1,0:T(8,128)} %fusion.114, bf16[1,2,2048,768]{3,2,1,0:T(8,128)(2,1)} %param.14, bf16[256,2176]{1,0:T(8,128)(2,1)} %copy-done.7, f32[768]{0:T(1024)S(1)} %get-tuple-element.5), kind=kOutput, calls=%fused_computation.61 | convolution fusion | flops 1613037568 | bytes 10235904 | tf_op jit(solution)/shard_map/dot_general | solution.py:11
  93.5 2.1 %slice.436 = bf16[128,2048]{1,0:T(8,128)(2,1)} slice(f32[256,2048]{1,0:T(8,128)} %fusion.87), slice={[128:256], [0:2048]} | slice | bytes 1048576 | tf_op jit(solution)/shard_map/slice | solution.py:99
  95.6 2.3 %fusion.148 = bf16[128,2048]{1,0:T(8,128)(2,1)} fusion(f32[256,2048]{1,0:T(8,128)} %fusion.93, bf16[128,2048]{1,0:T(8,128)(2,1)} %collective-permute-done.22), kind=kLoop, calls=%fused_computation.90 | loop fusion | flops 786432 | bytes 2097152 | tf_op jit(solution)/shard_map/convert_element_type | solution.py:106
  97.9 2.1 %collective-permute-start.23 = (bf16[128,2048]{1,0:T(8,128)(2,1)}, bf16[128,2048]{1,0:T(8,128)(2,1)}, u32[]{:S(2)}, u32[]{:S(2)}) collective-permute-start(bf16[128,2048]{1,0:T(8,128)(2,1)} %fusion.148), channel_id=1, source_target_pairs={{0,4},{5,1},{4,8},{9,5},{8,12},{13,9},{12,14},{15,13},{14,10},{11,... | collective-permute-start | bytes 1572872 | tf_op jit(solution)/shard_map/ppermute | solution.py:106
  100.0 5.8 %fusion.81 = f32[256,2048]{1,0:T(8,128)} fusion(bf16[1,768,2048]{2,1,0:T(8,128)(2,1)S(1)} %copy-done, f32[256]{0:T(256)S(1)} %get-tuple-element.12, f32[2048]{0:T(1024)S(1)} %bitcast.150, f32[256,768]{1,0:T(8,128)} %fusion.111, bf16[1,2,2048,768]{3,2,1,0:T(8,128)(2,1)} %param.14, bf16[256,2176]{1,0:T(8,128)(2,1)} %copy-done.4, f32[768]{0:T(1024)S(1)} %get-tuple-element.5), kind=kOutput, calls=%fused_computation.59 | convolution fusion | flops 1613037568 | bytes 10235904 | tf_op jit(solution)/shard_map/dot_general | solution.py:11
  105.8 2.1 %slice.437 = bf16[128,2048]{1,0:T(8,128)(2,1)} slice(f32[256,2048]{1,0:T(8,128)} %fusion.81), slice={[128:256], [0:2048]} | slice | bytes 1048576 | tf_op jit(solution)/shard_map/slice | solution.py:99
  108.1 2.5 %fusion.150 = bf16[128,2048]{1,0:T(8,128)(2,1)} fusion(f32[256,2048]{1,0:T(8,128)} %fusion.87, bf16[128,2048]{1,0:T(8,128)(2,1)} %collective-permute-done.23, bf16[128,2048]{1,0:T(8,128)(2,1)} %collective-permute-done.20), kind=kLoop, calls=%fused_computation.94 | loop fusion | flops 1310720 | bytes 2621440 | tf_op jit(solution)/shard_map/convert_element_type | solution.py:106
  110.6 1.4 collective-permute-start.24
  112.0 5.9 %fusion.75 = f32[256,2048]{1,0:T(8,128)} fusion(bf16[1,768,2048]{2,1,0:T(8,128)(2,1)S(1)} %copy-done, f32[256]{0:T(256)S(1)} %get-tuple-element.11, f32[2048]{0:T(1024)S(1)} %bitcast.151, f32[256,768]{1,0:T(8,128)} %fusion.108, bf16[1,2,2048,768]{3,2,1,0:T(8,128)(2,1)} %param.14, bf16[256,2176]{1,0:T(8,128)(2,1)} %copy-done.8, f32[768]{0:T(1024)S(1)} %get-tuple-element.5), kind=kOutput, calls=%fused_computation.57 | convolution fusion | flops 1613037568 | bytes 10235904 | tf_op jit(solution)/shard_map/dot_general | solution.py:11
  117.9 2.1 %slice.438 = bf16[128,2048]{1,0:T(8,128)(2,1)} slice(f32[256,2048]{1,0:T(8,128)} %fusion.75), slice={[128:256], [0:2048]} | slice | bytes 1048576 | tf_op jit(solution)/shard_map/slice | solution.py:99
  120.1 2.5 %fusion.152 = bf16[128,2048]{1,0:T(8,128)(2,1)} fusion(f32[256,2048]{1,0:T(8,128)} %fusion.81, bf16[128,2048]{1,0:T(8,128)(2,1)} %collective-permute-done.24, bf16[128,2048]{1,0:T(8,128)(2,1)} %collective-permute-done.18), kind=kLoop, calls=%fused_computation.98 | loop fusion | flops 1310720 | bytes 2621440 | tf_op jit(solution)/shard_map/convert_element_type | solution.py:106
  122.6 1.5 collective-permute-start.25
  124.1 5.8 %fusion.69 = f32[256,2048]{1,0:T(8,128)} fusion(bf16[1,768,2048]{2,1,0:T(8,128)(2,1)S(1)} %copy-done, f32[256]{0:T(256)S(1)} %get-tuple-element.10, f32[2048]{0:T(1024)S(1)} %bitcast.152, f32[256,768]{1,0:T(8,128)} %fusion.105, bf16[1,2,2048,768]{3,2,1,0:T(8,128)(2,1)} %param.14, bf16[256,2176]{1,0:T(8,128)(2,1)} %copy-done.5, f32[768]{0:T(1024)S(1)} %get-tuple-element.5), kind=kOutput, calls=%fused_computation.55 | convolution fusion | flops 1613037568 | bytes 10235904 | tf_op jit(solution)/shard_map/dot_general | solution.py:11
  129.9 2.1 %slice.439 = bf16[128,2048]{1,0:T(8,128)(2,1)} slice(f32[256,2048]{1,0:T(8,128)} %fusion.69), slice={[128:256], [0:2048]} | slice | bytes 1048576 | tf_op jit(solution)/shard_map/slice | solution.py:99
  132.1 2.5 %fusion.154 = bf16[128,2048]{1,0:T(8,128)(2,1)} fusion(f32[256,2048]{1,0:T(8,128)} %fusion.75, bf16[128,2048]{1,0:T(8,128)(2,1)} %collective-permute-done.25, bf16[128,2048]{1,0:T(8,128)(2,1)} %collective-permute-done.16), kind=kLoop, calls=%fused_computation.102 | loop fusion | flops 1310720 | bytes 2621440 | tf_op jit(solution)/shard_map/convert_element_type | solution.py:106
  134.6 1.5 collective-permute-start.26
  136.1 5.9 %fusion.63 = f32[256,2048]{1,0:T(8,128)} fusion(bf16[1,768,2048]{2,1,0:T(8,128)(2,1)S(1)} %copy-done, f32[256]{0:T(256)S(1)} %get-tuple-element.9, f32[2048]{0:T(1024)S(1)} %bitcast.153, f32[256,768]{1,0:T(8,128)} %fusion.102, bf16[1,2,2048,768]{3,2,1,0:T(8,128)(2,1)} %param.14, bf16[256,2176]{1,0:T(8,128)(2,1)} %copy-done.9, f32[768]{0:T(1024)S(1)} %get-tuple-element.5), kind=kOutput, calls=%fused_computation.53 | convolution fusion | flops 1613037568 | bytes 10235904 | tf_op jit(solution)/shard_map/dot_general | solution.py:11
  142.0 2.1 %slice.440 = bf16[128,2048]{1,0:T(8,128)(2,1)} slice(f32[256,2048]{1,0:T(8,128)} %fusion.63), slice={[128:256], [0:2048]} | slice | bytes 1048576 | tf_op jit(solution)/shard_map/slice | solution.py:99
  144.1 4.3 %fusion.99 = f32[256,768]{1,0:T(8,128)} fusion(bf16[256,2176]{1,0:T(8,128)(2,1)} %copy-done.10, bf16[1,2,2048,768]{3,2,1,0:T(8,128)(2,1)} %param.14, f32[768]{0:T(1024)S(1)} %get-tuple-element.6), kind=kOutput, calls=%fused_computation.67 | convolution fusion | flops 805502976 | bytes 4983808 | tf_op jit(solution)/shard_map/dot_general | solution.py:8
  148.3 2.2 %fusion.156 = bf16[128,2048]{1,0:T(8,128)(2,1)} fusion(f32[256,2048]{1,0:T(8,128)S(1)} %copy-done.2, bf16[128,2048]{1,0:T(8,128)(2,1)} %collective-permute-done.26, bf16[128,2048]{1,0:T(8,128)(2,1)} %collective-permute-done.14), kind=kLoop, calls=%fused_computation.106 | loop fusion | flops 1310720 | bytes 2621440 | tf_op jit(solution)/shard_map/convert_element_type | solution.py:106
  150.6 1.5 collective-permute-start.27
  152.1 5.8 %fusion.57 = f32[256,2048]{1,0:T(8,128)} fusion(bf16[1,768,2048]{2,1,0:T(8,128)(2,1)S(1)} %copy-done, f32[256]{0:T(256)S(1)} %get-tuple-element.8, f32[2048]{0:T(1024)S(1)} %bitcast.154, f32[256,768]{1,0:T(8,128)} %fusion.99, bf16[1,2,2048,768]{3,2,1,0:T(8,128)(2,1)} %param.14, bf16[256,2176]{1,0:T(8,128)(2,1)} %copy-done.10, f32[768]{0:T(1024)S(1)} %get-tuple-element.5), kind=kOutput, calls=%fused_computation.51 | convolution fusion | flops 1613037568 | bytes 10235904 | tf_op jit(solution)/shard_map/dot_general | solution.py:11
  157.9 2.1 %slice.441 = bf16[128,2048]{1,0:T(8,128)(2,1)} slice(f32[256,2048]{1,0:T(8,128)} %fusion.57), slice={[128:256], [0:2048]} | slice | bytes 1048576 | tf_op jit(solution)/shard_map/slice | solution.py:99
  160.0 2.5 %fusion.158 = bf16[128,2048]{1,0:T(8,128)(2,1)} fusion(f32[256,2048]{1,0:T(8,128)} %fusion.63, bf16[128,2048]{1,0:T(8,128)(2,1)} %collective-permute-done.27, bf16[128,2048]{1,0:T(8,128)(2,1)} %collective-permute-done.12), kind=kLoop, calls=%fused_computation.110 | loop fusion | flops 1310720 | bytes 2621440 | tf_op jit(solution)/shard_map/convert_element_type | solution.py:106
  162.5 1.5 collective-permute-start.28
  164.1 5.9 %fusion.51 = f32[256,2048]{1,0:T(8,128)} fusion(bf16[1,768,2048]{2,1,0:T(8,128)(2,1)S(1)} %copy-done, f32[256]{0:T(256)S(1)} %get-tuple-element.14, f32[2048]{0:T(1024)S(1)} %bitcast.155, f32[256,768]{1,0:T(8,128)} %fusion.96, bf16[1,2,2048,768]{3,2,1,0:T(8,128)(2,1)} %param.14, f32[768]{0:T(1024)S(1)} %get-tuple-element.5, ...), kind=kOutput, calls=%fused_computation.49 | convolution fusion | flops 1615134720 | bytes 10301440 | tf_op jit(solution)/shard_map/dot_general | solution.py:11
  169.9 1.4 slice.442
  172.0 1.7 fusion.160
  173.7 1.6 collective-permute-start.29
  175.3 7.7 %collective-permute-done.29 = bf16[128,2048]{1,0:T(8,128)(2,1)S(1)} collective-permute-done((bf16[128,2048]{1,0:T(8,128)(2,1)S(1)}, bf16[128,2048]{1,0:T(8,128)(2,1)S(1)}, u32[]{:S(2)}, u32[]{:S(2)}) %collective-permute-start.29) | collective-permute-done | bytes 524320 | tf_op jit(solution)/shard_map/ppermute | solution.py:106
  183.0 1.0 fusion.162
  (91 shorter events, 2.6 us)
Async XLA Ops:
  0.0 79.2 %copy-start = (bf16[1,768,2048]{2,1,0:T(8,128)(2,1)S(1)}, bf16[1,768,2048]{2,1,0:T(8,128)(2,1)}, u32[]{:S(2)}) copy-start(bf16[1,768,2048]{2,1,0:T(8,128)(2,1)} %param.16) | copy-start | bytes 9437188
  0.0 10.9 %copy-start.12 = (bf16[1,2048]{1,0:T(2,128)(2,1)S(1)}, bf16[1,2048]{1,0:T(2,128)(2,1)}, u32[]{:S(2)}) copy-start(bf16[1,2048]{1,0:T(2,128)(2,1)} %param.17) | copy-start | bytes 12292
  0.0 10.9 %copy-start.13 = (s32[16]{0:T(128)S(1)}, s32[16]{0:T(128)}, u32[]{:S(2)}) copy-start(s32[16]{0:T(128)} %param.13) | copy-start | bytes 196
  0.0 12.8 %copy-start.11 = (bf16[1,2,768]{2,1,0:T(2,128)(2,1)S(1)}, bf16[1,2,768]{2,1,0:T(2,128)(2,1)}, u32[]{:S(2)}) copy-start(bf16[1,2,768]{2,1,0:T(2,128)(2,1)} %param.15) | copy-start | bytes 9220
  7.8 10.8 %collective-permute-start.2 = (bf16[128,2176]{1,0:T(8,128)(2,1)}, bf16[128,2176]{1,0:T(8,128)(2,1)}, u32[]{:S(2)}, u32[]{:S(2)}) collective-permute-start(bf16[128,2176]{1,0:T(8,128)(2,1)} %concatenate.30), channel_id=1, source_target_pairs={{0,4},{5,1},{4,8},{9,5},{8,12},{13,9},{12,14},{15,13},{14,10},{11,... | collective-permute-start | bytes 1671176 | tf_op jit(solution)/shard_map/ppermute | solution.py:98
  10.9 11.0 %collective-permute-start = (bf16[128,2176]{1,0:T(8,128)(2,1)}, bf16[128,2176]{1,0:T(8,128)(2,1)}, u32[]{:S(2)}, u32[]{:S(2)}) collective-permute-start(bf16[128,2176]{1,0:T(8,128)(2,1)} %concatenate.30), channel_id=1, source_target_pairs={{0,1},{1,0},{2,3},{3,2},{4,5},{5,4},{6,7},{7,6},{8,9},{9,8},{10,11... | collective-permute-start | bytes 1671176 | tf_op jit(solution)/shard_map/ppermute | solution.py:95
  18.6 9.7 %collective-permute-start.3 = (bf16[128,2176]{1,0:T(8,128)(2,1)}, bf16[128,2176]{1,0:T(8,128)(2,1)S(1)}, u32[]{:S(2)}, u32[]{:S(2)}) collective-permute-start(bf16[128,2176]{1,0:T(8,128)(2,1)} %collective-permute-done.2), channel_id=1, source_target_pairs={{0,4},{5,1},{4,8},{9,5},{8,12},{13,9},{12,14},{15,13},{14,10},{11,... | collective-permute-start | bytes 1671176 | tf_op jit(solution)/shard_map/ppermute | solution.py:98
  20.7 9.7 %collective-permute-start.21 = (bf16[128,2176]{1,0:T(8,128)(2,1)}, bf16[128,2176]{1,0:T(8,128)(2,1)S(1)}, u32[]{:S(2)}, u32[]{:S(2)}) collective-permute-start(bf16[128,2176]{1,0:T(8,128)(2,1)} %collective-permute-done.2), channel_id=1, source_target_pairs={{0,1},{1,0},{2,3},{3,2},{4,5},{5,4},{6,7},{7,6},{8,9},{9,8},{10,11... | collective-permute-start | bytes 1671176 | tf_op jit(solution)/shard_map/ppermute | solution.py:95
  28.4 9.5 %collective-permute-start.4 = (bf16[128,2176]{1,0:T(8,128)(2,1)S(1)}, bf16[128,2176]{1,0:T(8,128)(2,1)S(1)}, u32[]{:S(2)}, u32[]{:S(2)}) collective-permute-start(bf16[128,2176]{1,0:T(8,128)(2,1)S(1)} %collective-permute-done.3), channel_id=1, source_target_pairs={{0,4},{5,1},{4,8},{9,5},{8,12},{13,9},{12,14},{15,13},{14,10},{11,... | collective-permute-start | bytes 1671176 | tf_op jit(solution)/shard_map/ppermute | solution.py:98
  30.4 9.6 %collective-permute-start.19 = (bf16[128,2176]{1,0:T(8,128)(2,1)S(1)}, bf16[128,2176]{1,0:T(8,128)(2,1)S(1)}, u32[]{:S(2)}, u32[]{:S(2)}) collective-permute-start(bf16[128,2176]{1,0:T(8,128)(2,1)S(1)} %collective-permute-done.3), channel_id=1, source_target_pairs={{0,1},{1,0},{2,3},{3,2},{4,5},{5,4},{6,7},{7,6},{8,9},{9,8},{10,11... | collective-permute-start | bytes 1671176 | tf_op jit(solution)/shard_map/ppermute | solution.py:95
  30.5 9.7 %slice-start = ((s8[6291456]{0:T(1024)(128)(4,1)}), s8[4194304]{0:T(1024)(128)(4,1)S(1)}, s32[]{:S(2)}) async-start(s8[6291456]{0:T(1024)(128)(4,1)} %bitcast.156), calls=%async_computation | async-start | bytes 8388608
  30.5 47.6 %copy-start.6 = (bf16[256,2176]{1,0:T(8,128)(2,1)}, bf16[256,2176]{1,0:T(8,128)(2,1)S(1)}, u32[]{:S(2)}) copy-start(bf16[256,2176]{1,0:T(8,128)(2,1)S(1)} %constant_dynamic-update-slice_fusion.12) | copy-start | bytes 3342340
  30.5 9.6 %slice-start.1 = ((s8[6291456]{0:T(1024)(128)(4,1)}), s8[2097152]{0:T(1024)(128)(4,1)S(1)}, s32[]{:S(2)}) async-start(s8[6291456]{0:T(1024)(128)(4,1)} %bitcast.156), calls=%async_computation.1 | async-start | bytes 4194304
  37.9 9.5 %collective-permute-start.5 = (bf16[128,2176]{1,0:T(8,128)(2,1)S(1)}, bf16[128,2176]{1,0:T(8,128)(2,1)S(1)}, u32[]{:S(2)}, u32[]{:S(2)}) collective-permute-start(bf16[128,2176]{1,0:T(8,128)(2,1)S(1)} %collective-permute-done.4), channel_id=1, source_target_pairs={{0,4},{5,1},{4,8},{9,5},{8,12},{13,9},{12,14},{15,13},{14,10},{11,... | collective-permute-start | bytes 1671176 | tf_op jit(solution)/shard_map/ppermute | solution.py:98
  40.0 9.5 %collective-permute-start.17 = (bf16[128,2176]{1,0:T(8,128)(2,1)S(1)}, bf16[128,2176]{1,0:T(8,128)(2,1)S(1)}, u32[]{:S(2)}, u32[]{:S(2)}) collective-permute-start(bf16[128,2176]{1,0:T(8,128)(2,1)S(1)} %collective-permute-done.4), channel_id=1, source_target_pairs={{0,1},{1,0},{2,3},{3,2},{4,5},{5,4},{6,7},{7,6},{8,9},{9,8},{10,11... | collective-permute-start | bytes 1671176 | tf_op jit(solution)/shard_map/ppermute | solution.py:95
  40.1 38.0 %copy-start.7 = (bf16[256,2176]{1,0:T(8,128)(2,1)}, bf16[256,2176]{1,0:T(8,128)(2,1)S(1)}, u32[]{:S(2)}) copy-start(bf16[256,2176]{1,0:T(8,128)(2,1)S(1)} %constant_dynamic-update-slice_fusion.10) | copy-start | bytes 3342340
  47.4 9.5 %collective-permute-start.6 = (bf16[128,2176]{1,0:T(8,128)(2,1)S(1)}, bf16[128,2176]{1,0:T(8,128)(2,1)S(1)}, u32[]{:S(2)}, u32[]{:S(2)}) collective-permute-start(bf16[128,2176]{1,0:T(8,128)(2,1)S(1)} %collective-permute-done.5), channel_id=1, source_target_pairs={{0,4},{5,1},{4,8},{9,5},{8,12},{13,9},{12,14},{15,13},{14,10},{11,... | collective-permute-start | bytes 1671176 | tf_op jit(solution)/shard_map/ppermute | solution.py:98
  49.5 9.6 %collective-permute-start.15 = (bf16[128,2176]{1,0:T(8,128)(2,1)S(1)}, bf16[128,2176]{1,0:T(8,128)(2,1)S(1)}, u32[]{:S(2)}, u32[]{:S(2)}) collective-permute-start(bf16[128,2176]{1,0:T(8,128)(2,1)S(1)} %collective-permute-done.5), channel_id=1, source_target_pairs={{0,1},{1,0},{2,3},{3,2},{4,5},{5,4},{6,7},{7,6},{8,9},{9,8},{10,11... | collective-permute-start | bytes 1671176 | tf_op jit(solution)/shard_map/ppermute | solution.py:95
  49.6 28.6 %copy-start.4 = (bf16[256,2176]{1,0:T(8,128)(2,1)}, bf16[256,2176]{1,0:T(8,128)(2,1)S(1)}, u32[]{:S(2)}) copy-start(bf16[256,2176]{1,0:T(8,128)(2,1)S(1)} %constant_dynamic-update-slice_fusion.8) | copy-start | bytes 3342340
  57.0 9.5 %collective-permute-start.7 = (bf16[128,2176]{1,0:T(8,128)(2,1)S(1)}, bf16[128,2176]{1,0:T(8,128)(2,1)S(1)}, u32[]{:S(2)}, u32[]{:S(2)}) collective-permute-start(bf16[128,2176]{1,0:T(8,128)(2,1)S(1)} %collective-permute-done.6), channel_id=1, source_target_pairs={{0,4},{5,1},{4,8},{9,5},{8,12},{13,9},{12,14},{15,13},{14,10},{11,... | collective-permute-start | bytes 1671176 | tf_op jit(solution)/shard_map/ppermute | solution.py:98
  59.0 9.5 %collective-permute-start.13 = (bf16[128,2176]{1,0:T(8,128)(2,1)S(1)}, bf16[128,2176]{1,0:T(8,128)(2,1)S(1)}, u32[]{:S(2)}, u32[]{:S(2)}) collective-permute-start(bf16[128,2176]{1,0:T(8,128)(2,1)S(1)} %collective-permute-done.6), channel_id=1, source_target_pairs={{0,1},{1,0},{2,3},{3,2},{4,5},{5,4},{6,7},{7,6},{8,9},{9,8},{10,11... | collective-permute-start | bytes 1671176 | tf_op jit(solution)/shard_map/ppermute | solution.py:95
  59.2 19.0 %copy-start.8 = (bf16[256,2176]{1,0:T(8,128)(2,1)}, bf16[256,2176]{1,0:T(8,128)(2,1)S(1)}, u32[]{:S(2)}) copy-start(bf16[256,2176]{1,0:T(8,128)(2,1)S(1)} %constant_dynamic-update-slice_fusion.6) | copy-start | bytes 3342340
  66.5 9.5 %collective-permute-start.8 = (bf16[128,2176]{1,0:T(8,128)(2,1)S(1)}, bf16[128,2176]{1,0:T(8,128)(2,1)S(1)}, u32[]{:S(2)}, u32[]{:S(2)}) collective-permute-start(bf16[128,2176]{1,0:T(8,128)(2,1)S(1)} %collective-permute-done.7), channel_id=1, source_target_pairs={{0,4},{5,1},{4,8},{9,5},{8,12},{13,9},{12,14},{15,13},{14,10},{11,... | collective-permute-start | bytes 1671176 | tf_op jit(solution)/shard_map/ppermute | solution.py:98
  68.6 7.5 %collective-permute-start.11 = (bf16[128,2176]{1,0:T(8,128)(2,1)S(1)}, bf16[128,2176]{1,0:T(8,128)(2,1)S(1)}, u32[]{:S(2)}, u32[]{:S(2)}) collective-permute-start(bf16[128,2176]{1,0:T(8,128)(2,1)S(1)} %collective-permute-done.7), channel_id=1, source_target_pairs={{0,1},{1,0},{2,3},{3,2},{4,5},{5,4},{6,7},{7,6},{8,9},{9,8},{10,11... | collective-permute-start | bytes 1671176 | tf_op jit(solution)/shard_map/ppermute | solution.py:95
  68.6 9.5 %copy-start.5 = (bf16[256,2176]{1,0:T(8,128)(2,1)}, bf16[256,2176]{1,0:T(8,128)(2,1)S(1)}, u32[]{:S(2)}) copy-start(bf16[256,2176]{1,0:T(8,128)(2,1)S(1)} %constant_dynamic-update-slice_fusion.4) | copy-start | bytes 3342340
  76.0 2.0 %collective-permute-start.9 = (bf16[128,2176]{1,0:T(8,128)(2,1)S(1)}, bf16[128,2176]{1,0:T(8,128)(2,1)S(1)}, u32[]{:S(2)}, u32[]{:S(2)}) collective-permute-start(bf16[128,2176]{1,0:T(8,128)(2,1)S(1)} %collective-permute-done.8), channel_id=1, source_target_pairs={{0,1},{1,0},{2,3},{3,2},{4,5},{5,4},{6,7},{7,6},{8,9},{9,8},{10,11... | collective-permute-start | bytes 1671176 | tf_op jit(solution)/shard_map/ppermute | solution.py:95
  76.2 2.0 %copy-start.9 = (bf16[256,2176]{1,0:T(8,128)(2,1)}, bf16[256,2176]{1,0:T(8,128)(2,1)S(1)}, u32[]{:S(2)}) copy-start(bf16[256,2176]{1,0:T(8,128)(2,1)S(1)} %constant_dynamic-update-slice_fusion.2) | copy-start | bytes 3342340
  76.2 2.0 %copy-start.1 = (bf16[128,2176]{1,0:T(8,128)(2,1)S(1)}, bf16[128,2176]{1,0:T(8,128)(2,1)}, u32[]{:S(2)}) copy-start(bf16[128,2176]{1,0:T(8,128)(2,1)} %concatenate.30) | copy-start | bytes 1671172
  78.2 1.0 copy-start.10
  87.2 8.5 %collective-permute-start.22 = (bf16[128,2048]{1,0:T(8,128)(2,1)}, bf16[128,2048]{1,0:T(8,128)(2,1)}, u32[]{:S(2)}, u32[]{:S(2)}) collective-permute-start(bf16[128,2048]{1,0:T(8,128)(2,1)} %slice.435), channel_id=1, source_target_pairs={{0,1},{1,0},{2,3},{3,2},{4,5},{5,4},{6,7},{7,6},{8,9},{9,8},{10,11... | collective-permute-start | bytes 1572872 | tf_op jit(solution)/shard_map/ppermute | solution.py:99
  95.6 12.5 %collective-permute-start.20 = (bf16[128,2048]{1,0:T(8,128)(2,1)}, bf16[128,2048]{1,0:T(8,128)(2,1)}, u32[]{:S(2)}, u32[]{:S(2)}) collective-permute-start(bf16[128,2048]{1,0:T(8,128)(2,1)} %slice.436), channel_id=1, source_target_pairs={{0,1},{1,0},{2,3},{3,2},{4,5},{5,4},{6,7},{7,6},{8,9},{9,8},{10,11... | collective-permute-start | bytes 1572872 | tf_op jit(solution)/shard_map/ppermute | solution.py:99
  97.9 10.2 %collective-permute-start.23 = (bf16[128,2048]{1,0:T(8,128)(2,1)}, bf16[128,2048]{1,0:T(8,128)(2,1)}, u32[]{:S(2)}, u32[]{:S(2)}) collective-permute-start(bf16[128,2048]{1,0:T(8,128)(2,1)} %fusion.148), channel_id=1, source_target_pairs={{0,4},{5,1},{4,8},{9,5},{8,12},{13,9},{12,14},{15,13},{14,10},{11,... | collective-permute-start | bytes 1572872 | tf_op jit(solution)/shard_map/ppermute | solution.py:106
  107.9 12.1 %collective-permute-start.18 = (bf16[128,2048]{1,0:T(8,128)(2,1)}, bf16[128,2048]{1,0:T(8,128)(2,1)}, u32[]{:S(2)}, u32[]{:S(2)}) collective-permute-start(bf16[128,2048]{1,0:T(8,128)(2,1)} %slice.437), channel_id=1, source_target_pairs={{0,1},{1,0},{2,3},{3,2},{4,5},{5,4},{6,7},{7,6},{8,9},{9,8},{10,11... | collective-permute-start | bytes 1572872 | tf_op jit(solution)/shard_map/ppermute | solution.py:99
  110.6 9.5 %collective-permute-start.24 = (bf16[128,2048]{1,0:T(8,128)(2,1)}, bf16[128,2048]{1,0:T(8,128)(2,1)}, u32[]{:S(2)}, u32[]{:S(2)}) collective-permute-start(bf16[128,2048]{1,0:T(8,128)(2,1)} %fusion.150), channel_id=1, source_target_pairs={{0,4},{5,1},{4,8},{9,5},{8,12},{13,9},{12,14},{15,13},{14,10},{11,... | collective-permute-start | bytes 1572872 | tf_op jit(solution)/shard_map/ppermute | solution.py:106
  120.0 12.0 %collective-permute-start.16 = (bf16[128,2048]{1,0:T(8,128)(2,1)}, bf16[128,2048]{1,0:T(8,128)(2,1)}, u32[]{:S(2)}, u32[]{:S(2)}) collective-permute-start(bf16[128,2048]{1,0:T(8,128)(2,1)} %slice.438), channel_id=1, source_target_pairs={{0,1},{1,0},{2,3},{3,2},{4,5},{5,4},{6,7},{7,6},{8,9},{9,8},{10,11... | collective-permute-start | bytes 1572872 | tf_op jit(solution)/shard_map/ppermute | solution.py:99
  122.6 9.5 %collective-permute-start.25 = (bf16[128,2048]{1,0:T(8,128)(2,1)}, bf16[128,2048]{1,0:T(8,128)(2,1)}, u32[]{:S(2)}, u32[]{:S(2)}) collective-permute-start(bf16[128,2048]{1,0:T(8,128)(2,1)} %fusion.152), channel_id=1, source_target_pairs={{0,4},{5,1},{4,8},{9,5},{8,12},{13,9},{12,14},{15,13},{14,10},{11,... | collective-permute-start | bytes 1572872 | tf_op jit(solution)/shard_map/ppermute | solution.py:106
  132.0 16.3 %collective-permute-start.14 = (bf16[128,2048]{1,0:T(8,128)(2,1)}, bf16[128,2048]{1,0:T(8,128)(2,1)}, u32[]{:S(2)}, u32[]{:S(2)}) collective-permute-start(bf16[128,2048]{1,0:T(8,128)(2,1)} %slice.439), channel_id=1, source_target_pairs={{0,1},{1,0},{2,3},{3,2},{4,5},{5,4},{6,7},{7,6},{8,9},{9,8},{10,11... | collective-permute-start | bytes 1572872 | tf_op jit(solution)/shard_map/ppermute | solution.py:99
  134.6 13.7 %collective-permute-start.26 = (bf16[128,2048]{1,0:T(8,128)(2,1)}, bf16[128,2048]{1,0:T(8,128)(2,1)}, u32[]{:S(2)}, u32[]{:S(2)}) collective-permute-start(bf16[128,2048]{1,0:T(8,128)(2,1)} %fusion.154), channel_id=1, source_target_pairs={{0,4},{5,1},{4,8},{9,5},{8,12},{13,9},{12,14},{15,13},{14,10},{11,... | collective-permute-start | bytes 1572872 | tf_op jit(solution)/shard_map/ppermute | solution.py:106
  144.1 4.3 %copy-start.2 = (f32[256,2048]{1,0:T(8,128)S(1)}, f32[256,2048]{1,0:T(8,128)}, u32[]{:S(2)}) copy-start(f32[256,2048]{1,0:T(8,128)} %fusion.69) | copy-start | bytes 6291460
  144.1 15.9 %collective-permute-start.12 = (bf16[128,2048]{1,0:T(8,128)(2,1)}, bf16[128,2048]{1,0:T(8,128)(2,1)}, u32[]{:S(2)}, u32[]{:S(2)}) collective-permute-start(bf16[128,2048]{1,0:T(8,128)(2,1)} %slice.440), channel_id=1, source_target_pairs={{0,1},{1,0},{2,3},{3,2},{4,5},{5,4},{6,7},{7,6},{8,9},{9,8},{10,11... | collective-permute-start | bytes 1572872 | tf_op jit(solution)/shard_map/ppermute | solution.py:99
  150.6 9.5 %collective-permute-start.27 = (bf16[128,2048]{1,0:T(8,128)(2,1)}, bf16[128,2048]{1,0:T(8,128)(2,1)}, u32[]{:S(2)}, u32[]{:S(2)}) collective-permute-start(bf16[128,2048]{1,0:T(8,128)(2,1)} %fusion.156), channel_id=1, source_target_pairs={{0,4},{5,1},{4,8},{9,5},{8,12},{13,9},{12,14},{15,13},{14,10},{11,... | collective-permute-start | bytes 1572872 | tf_op jit(solution)/shard_map/ppermute | solution.py:106
  160.0 11.5 %collective-permute-start.10 = (bf16[128,2048]{1,0:T(8,128)(2,1)}, bf16[128,2048]{1,0:T(8,128)(2,1)}, u32[]{:S(2)}, u32[]{:S(2)}) collective-permute-start(bf16[128,2048]{1,0:T(8,128)(2,1)} %slice.441), channel_id=1, source_target_pairs={{0,1},{1,0},{2,3},{3,2},{4,5},{5,4},{6,7},{7,6},{8,9},{9,8},{10,11... | collective-permute-start | bytes 1572872 | tf_op jit(solution)/shard_map/ppermute | solution.py:99
  162.5 9.5 %collective-permute-start.28 = (bf16[128,2048]{1,0:T(8,128)(2,1)}, bf16[128,2048]{1,0:T(8,128)(2,1)}, u32[]{:S(2)}, u32[]{:S(2)}) collective-permute-start(bf16[128,2048]{1,0:T(8,128)(2,1)} %fusion.158), channel_id=1, source_target_pairs={{0,4},{5,1},{4,8},{9,5},{8,12},{13,9},{12,14},{15,13},{14,10},{11,... | collective-permute-start | bytes 1572872 | tf_op jit(solution)/shard_map/ppermute | solution.py:106
  169.9 13.0 %copy-start.3 = (f32[256,2048]{1,0:T(8,128)S(1)}, f32[256,2048]{1,0:T(8,128)}, u32[]{:S(2)}) copy-start(f32[256,2048]{1,0:T(8,128)} %fusion.51) | copy-start | bytes 6291460
  171.4 3.9 %collective-permute-start.1 = (bf16[128,2048]{1,0:T(8,128)(2,1)S(1)}, bf16[128,2048]{1,0:T(8,128)(2,1)S(1)}, u32[]{:S(2)}, u32[]{:S(2)}) collective-permute-start(bf16[128,2048]{1,0:T(8,128)(2,1)S(1)} %slice.442), channel_id=1, source_target_pairs={{0,1},{1,0},{2,3},{3,2},{4,5},{5,4},{6,7},{7,6},{8,9},{9,8},{10,11... | collective-permute-start | bytes 1572872 | tf_op jit(solution)/shard_map/ppermute | solution.py:99
  173.7 9.2 %collective-permute-start.29 = (bf16[128,2048]{1,0:T(8,128)(2,1)S(1)}, bf16[128,2048]{1,0:T(8,128)(2,1)S(1)}, u32[]{:S(2)}, u32[]{:S(2)}) collective-permute-start(bf16[128,2048]{1,0:T(8,128)(2,1)S(1)} %fusion.160), channel_id=1, source_target_pairs={{0,4},{5,1},{4,8},{9,5},{8,12},{13,9},{12,14},{15,13},{14,10},{11,... | collective-permute-start | bytes 1572872 | tf_op jit(solution)/shard_map/ppermute | solution.py:106

commit v2 on v1

--- a/solution.py
+++ b/solution.py
@@ -1,7 +1,15 @@
+import functools
+
 import jax
 import jax.numpy as jnp
 from jax import lax
+from jax.experimental import pallas as pl
+from jax.experimental.pallas import tpu as pltpu
 from jax.sharding import PartitionSpec as P
+
+TILE = 256
+SMALL = 8 << 20
+LARGE = 20 << 20
 
 
 def expert_rows(batch_rows, in_blocks, in_scales, down_block, down_scales):
@@ -60,44 +68,113 @@
     return pairs, chips
 
 
+def packed_kernel(experts, tokens_ref, gain_ref, ids_ref, gates_ref, out_ref):
+    tok_rows, model_width = tokens_ref.shape
+    values = tokens_ref[...].astype(jnp.float32)
+    row_scale = lax.rsqrt(jnp.mean(values * values, axis=1, keepdims=True) + 1e-06)
+    out_ref[:, :model_width] = (values * row_scale * gain_ref[...]).astype(jnp.bfloat16)
+    gates = gates_ref[...]
+    weights = gates / jnp.sum(gates, axis=1, keepdims=True)
+    lanes = out_ref.shape[1] - model_width
+    lane = lax.broadcasted_iota(jnp.int32, (tok_rows, lanes), 1)
+    label = jnp.where(lane < experts, lane, lane - experts)
+    table = jnp.zeros((tok_rows, lanes), jnp.float32)
+    for k in range(ids_ref.shape[1]):
+        table += jnp.where(label == ids_ref[:, k : k + 1], weights[:, k : k + 1], 0.0)
+    high = table.astype(jnp.bfloat16).astype(jnp.float32)
+    out_ref[:, model_width:] = jnp.where(lane < experts, high, table - high).astype(jnp.bfloat16)
+
+
+def packed(tokens, norm_gain, expert_ids, gate_weights, experts):
+    tok_rows, model_width = tokens.shape
+    lanes = -(-2 * experts // 128) * 128
+    return pl.pallas_call(
+        functools.partial(packed_kernel, experts),
+        out_shape=jax.ShapeDtypeStruct((tok_rows, model_width + lanes), jnp.bfloat16),
+        in_specs=[pl.BlockSpec(memory_space=pltpu.VMEM)] * 4,
+        out_specs=pl.BlockSpec(memory_space=pltpu.VMEM),
+        compiler_params=pltpu.CompilerParams(vmem_limit_bytes=SMALL),
+        name="packed",
+    )(tokens, norm_gain[None, :], expert_ids, gate_weights)
+
+
+def visit_kernel(
+    experts, mine_ref, near_ref, far_ref, in_ref, in_scale_ref, down_ref, down_scale_ref,
+    part_ref, lent_ref, rows_ref, hidden_ref,
+):
+    tok_rows, model_width = part_ref.shape
+    hidden_width = hidden_ref.shape[1]
+    rows_ref[:tok_rows] = near_ref[:, :model_width]
+    rows_ref[tok_rows:] = far_ref[:, :model_width]
+    rows = rows_ref[...]
+    for start in range(0, hidden_width, TILE):
+        cols = slice(start, start + TILE)
+        gate = jnp.dot(rows, in_ref[0, 0, :, cols], preferred_element_type=jnp.float32)
+        up = jnp.dot(rows, in_ref[0, 1, :, cols], preferred_element_type=jnp.float32)
+        gate = gate * in_scale_ref[0, 0:1, cols].astype(jnp.float32)
+        up = up * in_scale_ref[0, 1:2, cols].astype(jnp.float32)
+        hidden_ref[:, cols] = (gate / (1.0 + jnp.exp(-gate)) * up).astype(jnp.bfloat16)
+    lane = lax.broadcasted_iota(jnp.int32, (tok_rows, far_ref.shape[1] - model_width), 1)
+    chosen = (lane == mine_ref[0]) | (lane == mine_ref[0] + experts)
+    near = near_ref[:, model_width:].astype(jnp.float32)
+    far = far_ref[:, model_width:].astype(jnp.float32)
+    near_share = jnp.sum(jnp.where(chosen, near, 0.0), axis=1, keepdims=True)
+    far_share = jnp.sum(jnp.where(chosen, far, 0.0), axis=1, keepdims=True)
+    hidden = hidden_ref[...]
+    for start in range(0, model_width, TILE):
+        cols = slice(start, start + TILE)
+        out = jnp.dot(hidden, down_ref[0, :, cols], preferred_element_type=jnp.float32)
+        out = out * down_scale_ref[:, cols].astype(jnp.float32)
+        part_ref[:, cols] = out[:tok_rows] * near_share
+        lent_ref[:, cols] = (out[tok_rows:] * far_share).astype(jnp.bfloat16)
+
+
+def visit(my_expert, near, far, experts, in_q, in_scale, down_q, down_scale):
+    tok_rows = near.shape[0]
+    hidden_width, model_width = down_q.shape[1:]
+    flops = 2 * 2 * tok_rows * 3 * hidden_width * model_width
+    return pl.pallas_call(
+        functools.partial(visit_kernel, experts),
+        out_shape=(
+            jax.ShapeDtypeStruct((tok_rows, model_width), jnp.float32),
+            jax.ShapeDtypeStruct((tok_rows, model_width), jnp.bfloat16),
+        ),
+        in_specs=[pl.BlockSpec(memory_space=pltpu.SMEM)]
+        + [pl.BlockSpec(memory_space=pltpu.VMEM)] * 6,
+        out_specs=(pl.BlockSpec(memory_space=pltpu.VMEM),) * 2,
+        scratch_shapes=[
+            pltpu.VMEM((2 * tok_rows, model_width), jnp.bfloat16),
+            pltpu.VMEM((2 * tok_rows, hidden_width), jnp.bfloat16),
+        ],
+        compiler_params=pltpu.CompilerParams(vmem_limit_bytes=LARGE),
+        cost_estimate=pl.CostEstimate(
+            flops=flops, bytes_accessed=6 * tok_rows * model_width, transcendentals=0
+        ),
+        name="visit",
+    )(my_expert, near, far, in_q, in_scale, down_q, down_scale)
+
+
 def circulated(
     tokens, norm_gain, expert_ids, gate_weights, owner_map, in_q, in_scale, down_q, down_scale
 ):
-    tok_rows, model_width = tokens.shape
     experts = owner_map.shape[0]
     devices = lax.axis_size("tok")
     ring, chips = ring_pairs(devices)
     swap = [(i, i ^ 1) for i in range(devices)]
     me = lax.axis_index("tok")
-    lanes = -(-2 * experts // 128) * 128
     labels = jnp.arange(experts, dtype=jnp.int32)
-    my_expert = jnp.sum(jnp.where(owner_map == me, labels, 0))
-
-    normed = normalized(tokens, norm_gain)
-    weights = gate_weights / jnp.sum(gate_weights, axis=1, keepdims=True)
-    named = expert_ids[:, :, None] == labels
-    table = jnp.sum(jnp.where(named, weights[:, :, None], 0.0), axis=1)
-    high = lax.reduce_precision(table, 8, 7)
-    low = table - high
-    fill = jnp.zeros((tok_rows, lanes - 2 * experts), jnp.float32)
-    extra = jnp.concatenate([high, low, fill], axis=1).astype(jnp.bfloat16)
-    block = jnp.concatenate([normed, extra], axis=1)
-    lane = jnp.arange(lanes, dtype=jnp.int32)
-    mine = (lane == my_expert) | (lane == my_expert + experts)
-
-    def served(rows):
-        share = jnp.sum(jnp.where(mine, rows[:, model_width:].astype(jnp.float32), 0.0), axis=1)
-        out = expert_rows(rows[:, :model_width], in_q[0], in_scale[0], down_q[0], down_scale[0])
-        return out * share[:, None]
+    my_expert = jnp.sum(jnp.where(owner_map == me, labels, 0), keepdims=True)
+    block = packed(tokens, norm_gain, expert_ids, gate_weights, experts)
 
     total = None
     for step in range(chips):
         other = lax.ppermute(block, "tok", swap)
-        both = served(jnp.concatenate([block, other], axis=0))
+        here = block
         if step < chips - 1:
             block = lax.ppermute(block, "tok", ring)
-        lent = lax.ppermute(both[tok_rows:].astype(jnp.bfloat16), "tok", swap)
-        part = both[:tok_rows] + lent.astype(jnp.float32)
+        part, lent = visit(my_expert, here, other, experts, in_q, in_scale, down_q, down_scale)
+        lent = lax.ppermute(lent, "tok", swap)
+        part = part + lent.astype(jnp.float32)
         if step == 0:
             own = part
             continue

time: 185 us -> 110 us (0.59)
  matrix products: 68.9 us -> 0 us
  Pallas kernels: 0 us -> 27.2 us
  other arithmetic: 25.2 us -> 3.58 us
  local copies, waits for them, and re-layouts: 20 us -> 9.37 us
    dot_general x16 -> x0, matrix products: 68.9 us -> none  [the longest x8 46.8 us: expert_rows(): jnp.dot(hidden, down_block, preferred_element_type=jnp.float32)]
    pallas_call x0 -> x9, Pallas kernels: none -> 27.2 us  [the longest x8 26.7 us: visit(): pl.pallas_call(functools.partial(visit_kernel, experts), out_shape=(jax.S...]
    ppermute x7, waiting for transfers between devices: 8.42 us -> 29.2 us  [circulated(): total = lax.ppermute(part.astype(jnp.bfloat16), 'tok', ring)]
    ppermute x7, waiting for transfers between devices: 33 us -> 12.9 us  [circulated(): block = lax.ppermute(block, 'tok', ring)]
    slice x8 -> x0, local copies, waits for them, and re-layouts: 16.1 us -> none  [circulated(): lent = lax.ppermute(both[tok_rows:].astype(jnp.bfloat16), 'tok', swap)]
    convert_element_type x7, other arithmetic: 16.1 us -> 1.29 us  [circulated(): total = lax.ppermute(part.astype(jnp.bfloat16), 'tok', ring)]
    unnamed x39 -> x20, local copies, waits for them, and re-layouts: 1.43 us -> 9.37 us
    reduce_sum x5 -> x1, other arithmetic: 4.46 us -> 1.29 us  [circulated(): my_expert = jnp.sum(jnp.where(owner_map == me, labels, 0), keepdims=True)]
  transfers between devices with their start and end apart: 30 -> 30, of which waited for: 11 -> 13; matrix products, arithmetic and copies ran while one was open for 52% -> 2% of each run, Pallas kernels for 0% -> 24%
where the time goes in v2:
time: 110 us; the launch traced here: 109 us
  waiting for transfers between devices  42.2 us (38%)
  Pallas kernels  27.2 us (25%)
  starting transfers between devices  26.7 us (24%)
  local copies, waits for them, and re-layouts  9.37 us (9%)
  other arithmetic  3.58 us (3%)
    ppermute x7, waiting for transfers between devices, circulated(): total = lax.ppermute(part.astype(jnp.bfloat16), 'tok', ring)  29.2 us
    pallas_call x8, Pallas kernels, visit(): pl.pallas_call(functools.partial(visit_kernel, experts), out_shape=(jax.S...  26.7 us
    ppermute x7, starting transfers between devices, circulated(): block = lax.ppermute(block, 'tok', ring)  13.1 us
    ppermute x7, waiting for transfers between devices, circulated(): block = lax.ppermute(block, 'tok', ring)  12.9 us
    ppermute x7, starting transfers between devices, circulated(): total = lax.ppermute(part.astype(jnp.bfloat16), 'tok', ring)  11.6 us
    unnamed x20, local copies, waits for them, and re-layouts  9.37 us
  transfers between devices with their start and end apart: 30, of which 13 were waited for; matrix products, arithmetic and copies ran while one was open for 2% of the time, Pallas kernels for 24%

profile of v2, /device:TPU:0, one launch (start us, length us, event | category | flops | bytes accessed | tf_op | source)
XLA Modules:
  0.0 109.3 jit_solution(4415812270551455261)
XLA Ops:
  0.0 0.8 copy.10.ids_ref
  0.8 0.8 copy.11.gates_ref
  1.6 1.0 copy-done.4
  2.6 0.7 copy-done.8
  3.3 0.6 packed.1.near_ref
  3.9 3.1 %collective-permute-start.2 = (bf16[128,2176]{1,0:T(8,128)(2,1)S(1)}, bf16[128,2176]{1,0:T(8,128)(2,1)S(1)}, u32[]{:S(2)}, u32[]{:S(2)}) collective-permute-start(bf16[128,2176]{1,0:T(8,128)(2,1)S(1)} %packed.1.near_ref), channel_id=1, source_target_pairs={{0,4},{5,1},{4,8},{9,5},{8,12},{13,9},{12,14},{15,13},{14,10},{11,... | collective-permute-start | bytes 1671176 | tf_op jit(solution)/shard_map/ppermute | solution.py:174
  7.0 7.5 %collective-permute-done.2.near_ref = bf16[128,2176]{1,0:T(8,128)(2,1)S(1)} collective-permute-done((bf16[128,2176]{1,0:T(8,128)(2,1)S(1)}, bf16[128,2176]{1,0:T(8,128)(2,1)S(1)}, u32[]{:S(2)}, u32[]{:S(2)}) %collective-permute-start.2) | collective-permute-done | bytes 557088 | tf_op jit(solution)/shard_map/ppermute | solution.py:174
  14.4 0.0 collective-permute-start.21
  14.5 1.3 %fusion = s32[]{:T(128)} fusion(s32[16]{0:T(128)} %param.13, s32[]{:T(128)S(6)} %axis_index.12), kind=kLoop, calls=%fused_computation.9 | loop fusion | flops 47 | bytes 72 | tf_op jit(solution)/shard_map/reduce_sum | solution.py:166
  15.7 2.1 %collective-permute-start.3 = (bf16[128,2176]{1,0:T(8,128)(2,1)S(1)}, bf16[128,2176]{1,0:T(8,128)(2,1)S(1)}, u32[]{:S(2)}, u32[]{:S(2)}) collective-permute-start(bf16[128,2176]{1,0:T(8,128)(2,1)S(1)} %collective-permute-done.2.near_ref), channel_id=1, source_target_pairs={{0,4},{5,1},{4,8},{9,5},{8,12},{13,9},{12,14},{15,13},{14,10},{11,... | collective-permute-start | bytes 1671176 | tf_op jit(solution)/shard_map/ppermute | solution.py:174
  17.8 2.8 %copy-done = bf16[1,2,2048,768]{3,2,1,0:T(8,128)(2,1)S(1)} copy-done((bf16[1,2,2048,768]{3,2,1,0:T(8,128)(2,1)S(1)}, bf16[1,2,2048,768]{3,2,1,0:T(8,128)(2,1)}, u32[]{:S(2)}) %copy-start) | copy-done | bytes 6291480
  20.6 1.9 %copy-done.2 = bf16[1,768,2048]{2,1,0:T(8,128)(2,1)S(1)} copy-done((bf16[1,768,2048]{2,1,0:T(8,128)(2,1)S(1)}, bf16[1,768,2048]{2,1,0:T(8,128)(2,1)}, u32[]{:S(2)}) %copy-start.2) | copy-done | bytes 3145752
  22.5 0.7 copy-done.5
  23.2 0.7 copy-done.6
  23.9 3.5 %visit.15 = (f32[128,2048]{1,0:T(8,128)S(1)}, bf16[128,2048]{1,0:T(8,128)(2,1)S(1)}) custom-call(s32[1]{0:T(128)} %bitcast.mine_ref, bf16[128,2176]{1,0:T(8,128)(2,1)S(1)} %collective-permute-done.2.near_ref, bf16[128,2176]{1,0:T(8,128)(2,1)S(1)} %collective-permute-done.21.far_ref, bf16[1,2,2048,768]{3,2,1,0:T(8,128)(2,1)S(1)} %copy-done, ...), custom_call_target="tpu_custom_call" | custom-call | flops 2415919104 | bytes 1572864 | tf_op jit(solution)/shard_map/visit/pallas_call | solution.py:136
  27.4 0.2 collective-permute-start.22
  27.6 0.3 collective-permute-start.19
  28.0 1.6 %collective-permute-start.4 = (bf16[128,2176]{1,0:T(8,128)(2,1)S(1)}, bf16[128,2176]{1,0:T(8,128)(2,1)S(1)}, u32[]{:S(2)}, u32[]{:S(2)}) collective-permute-start(bf16[128,2176]{1,0:T(8,128)(2,1)S(1)} %collective-permute-done.3.near_ref), channel_id=1, source_target_pairs={{0,4},{5,1},{4,8},{9,5},{8,12},{13,9},{12,14},{15,13},{14,10},{11,... | collective-permute-start | bytes 1671176 | tf_op jit(solution)/shard_map/ppermute | solution.py:174
  29.5 0.1 add_convert_fusion.7
  29.7 1.6 %collective-permute-start.23 = (bf16[128,2048]{1,0:T(8,128)(2,1)S(1)}, bf16[128,2048]{1,0:T(8,128)(2,1)S(1)}, u32[]{:S(2)}, u32[]{:S(2)}) collective-permute-start(bf16[128,2048]{1,0:T(8,128)(2,1)S(1)} %add_convert_fusion.7), channel_id=1, source_target_pairs={{0,4},{5,1},{4,8},{9,5},{8,12},{13,9},{12,14},{15,13},{14,10},{11,... | collective-permute-start | bytes 1572872 | tf_op jit(solution)/shard_map/ppermute | solution.py:183
  31.3 3.3 %visit.14 = (f32[128,2048]{1,0:T(8,128)S(1)}, bf16[128,2048]{1,0:T(8,128)(2,1)S(1)}) custom-call(s32[1]{0:T(128)} %bitcast.mine_ref, bf16[128,2176]{1,0:T(8,128)(2,1)S(1)} %collective-permute-done.3.near_ref, bf16[128,2176]{1,0:T(8,128)(2,1)S(1)} %collective-permute-done.19.far_ref, bf16[1,2,2048,768]{3,2,1,0:T(8,128)(2,1)S(1)} %copy-done.1, ...), custom_call_target="tpu_custom_call" | custom-call | flops 2415919104 | bytes 1572864 | tf_op jit(solution)/shard_map/visit/pallas_call | solution.py:136
  34.6 0.1 collective-permute-start.20
  34.7 2.8 %collective-permute-done.4.near_ref = bf16[128,2176]{1,0:T(8,128)(2,1)S(1)} collective-permute-done((bf16[128,2176]{1,0:T(8,128)(2,1)S(1)}, bf16[128,2176]{1,0:T(8,128)(2,1)S(1)}, u32[]{:S(2)}, u32[]{:S(2)}) %collective-permute-start.4) | collective-permute-done | bytes 557088 | tf_op jit(solution)/shard_map/ppermute | solution.py:174
  37.5 1.6 %collective-permute-start.5 = (bf16[128,2176]{1,0:T(8,128)(2,1)S(1)}, bf16[128,2176]{1,0:T(8,128)(2,1)S(1)}, u32[]{:S(2)}, u32[]{:S(2)}) collective-permute-start(bf16[128,2176]{1,0:T(8,128)(2,1)S(1)} %collective-permute-done.4.near_ref), channel_id=1, source_target_pairs={{0,4},{5,1},{4,8},{9,5},{8,12},{13,9},{12,14},{15,13},{14,10},{11,... | collective-permute-start | bytes 1671176 | tf_op jit(solution)/shard_map/ppermute | solution.py:174
  39.1 4.0 %collective-permute-done.23 = bf16[128,2048]{1,0:T(8,128)(2,1)S(1)} collective-permute-done((bf16[128,2048]{1,0:T(8,128)(2,1)S(1)}, bf16[128,2048]{1,0:T(8,128)(2,1)S(1)}, u32[]{:S(2)}, u32[]{:S(2)}) %collective-permute-start.23) | collective-permute-done | bytes 524320 | tf_op jit(solution)/shard_map/ppermute | solution.py:183
  43.1 0.2 add_convert_fusion.6
  43.3 1.6 %collective-permute-start.24 = (bf16[128,2048]{1,0:T(8,128)(2,1)S(1)}, bf16[128,2048]{1,0:T(8,128)(2,1)S(1)}, u32[]{:S(2)}, u32[]{:S(2)}) collective-permute-start(bf16[128,2048]{1,0:T(8,128)(2,1)S(1)} %add_convert_fusion.6), channel_id=1, source_target_pairs={{0,4},{5,1},{4,8},{9,5},{8,12},{13,9},{12,14},{15,13},{14,10},{11,... | collective-permute-start | bytes 1572872 | tf_op jit(solution)/shard_map/ppermute | solution.py:183
  44.9 3.3 %visit.13 = (f32[128,2048]{1,0:T(8,128)S(1)}, bf16[128,2048]{1,0:T(8,128)(2,1)S(1)}) custom-call(s32[1]{0:T(128)} %bitcast.mine_ref, bf16[128,2176]{1,0:T(8,128)(2,1)S(1)} %collective-permute-done.4.near_ref, bf16[128,2176]{1,0:T(8,128)(2,1)S(1)} %collective-permute-done.17.far_ref, bf16[1,2,2048,768]{3,2,1,0:T(8,128)(2,1)S(1)} %copy-done.1, ...), custom_call_target="tpu_custom_call" | custom-call | flops 2415919104 | bytes 1572864 | tf_op jit(solution)/shard_map/visit/pallas_call | solution.py:136
  48.3 0.1 collective-permute-start.18
  48.4 0.7 collective-permute-done.5.near_ref
  49.1 1.6 %collective-permute-start.6 = (bf16[128,2176]{1,0:T(8,128)(2,1)S(1)}, bf16[128,2176]{1,0:T(8,128)(2,1)S(1)}, u32[]{:S(2)}, u32[]{:S(2)}) collective-permute-start(bf16[128,2176]{1,0:T(8,128)(2,1)S(1)} %collective-permute-done.5.near_ref), channel_id=1, source_target_pairs={{0,4},{5,1},{4,8},{9,5},{8,12},{13,9},{12,14},{15,13},{14,10},{11,... | collective-permute-start | bytes 1671176 | tf_op jit(solution)/shard_map/ppermute | solution.py:174
  50.7 4.0 %collective-permute-done.24 = bf16[128,2048]{1,0:T(8,128)(2,1)S(1)} collective-permute-done((bf16[128,2048]{1,0:T(8,128)(2,1)S(1)}, bf16[128,2048]{1,0:T(8,128)(2,1)S(1)}, u32[]{:S(2)}, u32[]{:S(2)}) %collective-permute-start.24) | collective-permute-done | bytes 524320 | tf_op jit(solution)/shard_map/ppermute | solution.py:183
  54.7 0.2 add_convert_fusion.5
  54.9 1.6 %collective-permute-start.25 = (bf16[128,2048]{1,0:T(8,128)(2,1)S(1)}, bf16[128,2048]{1,0:T(8,128)(2,1)S(1)}, u32[]{:S(2)}, u32[]{:S(2)}) collective-permute-start(bf16[128,2048]{1,0:T(8,128)(2,1)S(1)} %add_convert_fusion.5), channel_id=1, source_target_pairs={{0,4},{5,1},{4,8},{9,5},{8,12},{13,9},{12,14},{15,13},{14,10},{11,... | collective-permute-start | bytes 1572872 | tf_op jit(solution)/shard_map/ppermute | solution.py:183
  56.5 3.3 %visit.12 = (f32[128,2048]{1,0:T(8,128)S(1)}, bf16[128,2048]{1,0:T(8,128)(2,1)S(1)}) custom-call(s32[1]{0:T(128)} %bitcast.mine_ref, bf16[128,2176]{1,0:T(8,128)(2,1)S(1)} %collective-permute-done.5.near_ref, bf16[128,2176]{1,0:T(8,128)(2,1)S(1)} %collective-permute-done.15.far_ref, bf16[1,2,2048,768]{3,2,1,0:T(8,128)(2,1)S(1)} %copy-done.1, ...), custom_call_target="tpu_custom_call" | custom-call | flops 2415919104 | bytes 1572864 | tf_op jit(solution)/shard_map/visit/pallas_call | solution.py:136
  59.9 0.1 collective-permute-start.16
  59.9 0.7 collective-permute-done.6.near_ref
  60.7 1.6 %collective-permute-start.7 = (bf16[128,2176]{1,0:T(8,128)(2,1)S(1)}, bf16[128,2176]{1,0:T(8,128)(2,1)S(1)}, u32[]{:S(2)}, u32[]{:S(2)}) collective-permute-start(bf16[128,2176]{1,0:T(8,128)(2,1)S(1)} %collective-permute-done.6.near_ref), channel_id=1, source_target_pairs={{0,4},{5,1},{4,8},{9,5},{8,12},{13,9},{12,14},{15,13},{14,10},{11,... | collective-permute-start | bytes 1671176 | tf_op jit(solution)/shard_map/ppermute | solution.py:174
  62.2 4.0 %collective-permute-done.25 = bf16[128,2048]{1,0:T(8,128)(2,1)S(1)} collective-permute-done((bf16[128,2048]{1,0:T(8,128)(2,1)S(1)}, bf16[128,2048]{1,0:T(8,128)(2,1)S(1)}, u32[]{:S(2)}, u32[]{:S(2)}) %collective-permute-start.25) | collective-permute-done | bytes 524320 | tf_op jit(solution)/shard_map/ppermute | solution.py:183
  66.3 0.2 add_convert_fusion.4
  66.5 1.8 %collective-permute-start.26 = (bf16[128,2048]{1,0:T(8,128)(2,1)S(1)}, bf16[128,2048]{1,0:T(8,128)(2,1)S(1)}, u32[]{:S(2)}, u32[]{:S(2)}) collective-permute-start(bf16[128,2048]{1,0:T(8,128)(2,1)S(1)} %add_convert_fusion.4), channel_id=1, source_target_pairs={{0,4},{5,1},{4,8},{9,5},{8,12},{13,9},{12,14},{15,13},{14,10},{11,... | collective-permute-start | bytes 1572872 | tf_op jit(solution)/shard_map/ppermute | solution.py:183
  68.3 3.3 %visit.11 = (f32[128,2048]{1,0:T(8,128)S(1)}, bf16[128,2048]{1,0:T(8,128)(2,1)S(1)}) custom-call(s32[1]{0:T(128)} %bitcast.mine_ref, bf16[128,2176]{1,0:T(8,128)(2,1)S(1)} %collective-permute-done.6.near_ref, bf16[128,2176]{1,0:T(8,128)(2,1)S(1)} %collective-permute-done.13.far_ref, bf16[1,2,2048,768]{3,2,1,0:T(8,128)(2,1)S(1)} %copy-done.1, ...), custom_call_target="tpu_custom_call" | custom-call | flops 2415919104 | bytes 1572864 | tf_op jit(solution)/shard_map/visit/pallas_call | solution.py:136
  71.6 0.1 collective-permute-start.14
  71.7 0.5 collective-permute-done.7.near_ref
  72.2 1.6 %collective-permute-start.8 = (bf16[128,2176]{1,0:T(8,128)(2,1)S(1)}, bf16[128,2176]{1,0:T(8,128)(2,1)S(1)}, u32[]{:S(2)}, u32[]{:S(2)}) collective-permute-start(bf16[128,2176]{1,0:T(8,128)(2,1)S(1)} %collective-permute-done.7.near_ref), channel_id=1, source_target_pairs={{0,4},{5,1},{4,8},{9,5},{8,12},{13,9},{12,14},{15,13},{14,10},{11,... | collective-permute-start | bytes 1671176 | tf_op jit(solution)/shard_map/ppermute | solution.py:174
  73.8 4.0 %collective-permute-done.26 = bf16[128,2048]{1,0:T(8,128)(2,1)S(1)} collective-permute-done((bf16[128,2048]{1,0:T(8,128)(2,1)S(1)}, bf16[128,2048]{1,0:T(8,128)(2,1)S(1)}, u32[]{:S(2)}, u32[]{:S(2)}) %collective-permute-start.26) | collective-permute-done | bytes 524320 | tf_op jit(solution)/shard_map/ppermute | solution.py:183
  77.9 0.2 add_convert_fusion.3
  78.1 1.6 %collective-permute-start.27 = (bf16[128,2048]{1,0:T(8,128)(2,1)S(1)}, bf16[128,2048]{1,0:T(8,128)(2,1)S(1)}, u32[]{:S(2)}, u32[]{:S(2)}) collective-permute-start(bf16[128,2048]{1,0:T(8,128)(2,1)S(1)} %add_convert_fusion.3), channel_id=1, source_target_pairs={{0,4},{5,1},{4,8},{9,5},{8,12},{13,9},{12,14},{15,13},{14,10},{11,... | collective-permute-start | bytes 1572872 | tf_op jit(solution)/shard_map/ppermute | solution.py:183
  79.7 3.3 %visit.10 = (f32[128,2048]{1,0:T(8,128)S(1)}, bf16[128,2048]{1,0:T(8,128)(2,1)S(1)}) custom-call(s32[1]{0:T(128)} %bitcast.mine_ref, bf16[128,2176]{1,0:T(8,128)(2,1)S(1)} %collective-permute-done.7.near_ref, bf16[128,2176]{1,0:T(8,128)(2,1)S(1)} %collective-permute-done.11.far_ref, bf16[1,2,2048,768]{3,2,1,0:T(8,128)(2,1)S(1)} %copy-done.1, ...), custom_call_target="tpu_custom_call" | custom-call | flops 2415919104 | bytes 1572864 | tf_op jit(solution)/shard_map/visit/pallas_call | solution.py:136
  83.0 0.1 collective-permute-start.12
  83.1 0.7 collective-permute-done.8.near_ref
  83.8 0.5 collective-permute-start
  84.3 5.1 %collective-permute-done.27 = bf16[128,2048]{1,0:T(8,128)(2,1)S(1)} collective-permute-done((bf16[128,2048]{1,0:T(8,128)(2,1)S(1)}, bf16[128,2048]{1,0:T(8,128)(2,1)S(1)}, u32[]{:S(2)}, u32[]{:S(2)}) %collective-permute-start.27) | collective-permute-done | bytes 524320 | tf_op jit(solution)/shard_map/ppermute | solution.py:183
  89.5 0.2 add_convert_fusion.2
  89.7 1.6 %collective-permute-start.28 = (bf16[128,2048]{1,0:T(8,128)(2,1)S(1)}, bf16[128,2048]{1,0:T(8,128)(2,1)S(1)}, u32[]{:S(2)}, u32[]{:S(2)}) collective-permute-start(bf16[128,2048]{1,0:T(8,128)(2,1)S(1)} %add_convert_fusion.2), channel_id=1, source_target_pairs={{0,4},{5,1},{4,8},{9,5},{8,12},{13,9},{12,14},{15,13},{14,10},{11,... | collective-permute-start | bytes 1572872 | tf_op jit(solution)/shard_map/ppermute | solution.py:183
  91.3 3.3 %visit.9 = (f32[128,2048]{1,0:T(8,128)S(1)}, bf16[128,2048]{1,0:T(8,128)(2,1)S(1)}) custom-call(s32[1]{0:T(128)} %bitcast.mine_ref, bf16[128,2176]{1,0:T(8,128)(2,1)S(1)} %collective-permute-done.8.near_ref, bf16[128,2176]{1,0:T(8,128)(2,1)S(1)} %collective-permute-done.9.far_ref, bf16[1,2,2048,768]{3,2,1,0:T(8,128)(2,1)S(1)} %copy-done.1, ...), custom_call_target="tpu_custom_call" | custom-call | flops 2415919104 | bytes 1572864 | tf_op jit(solution)/shard_map/visit/pallas_call | solution.py:136
  94.6 0.1 collective-permute-start.10
  94.7 3.3 %visit.8 = (f32[128,2048]{1,0:T(8,128)S(1)}, bf16[128,2048]{1,0:T(8,128)(2,1)S(1)}) custom-call(s32[1]{0:T(128)} %bitcast.mine_ref, bf16[128,2176]{1,0:T(8,128)(2,1)S(1)} %packed.1.near_ref, bf16[128,2176]{1,0:T(8,128)(2,1)S(1)} %collective-permute-done.far_ref, bf16[1,2,2048,768]{3,2,1,0:T(8,128)(2,1)S(1)} %copy-done.1, bf16[1,2,768]{2,1,0:T(2,128)(2,1)S(1)} %copy-done.7, ...), custom_call_target="tpu_custom_call" | custom-call | flops 2415919104 | bytes 1572864 | tf_op jit(solution)/shard_map/visit/pallas_call | solution.py:136
  98.0 0.6 collective-permute-start.1
  98.6 0.3 collective-permute-done.28
  98.9 0.2 add_convert_fusion.1
  99.1 1.6 %collective-permute-start.29 = (bf16[128,2048]{1,0:T(8,128)(2,1)S(1)}, bf16[128,2048]{1,0:T(8,128)(2,1)S(1)}, u32[]{:S(2)}, u32[]{:S(2)}) collective-permute-start(bf16[128,2048]{1,0:T(8,128)(2,1)S(1)} %add_convert_fusion.1), channel_id=1, source_target_pairs={{0,4},{5,1},{4,8},{9,5},{8,12},{13,9},{12,14},{15,13},{14,10},{11,... | collective-permute-start | bytes 1572872 | tf_op jit(solution)/shard_map/ppermute | solution.py:183
  100.7 7.6 %collective-permute-done.29 = bf16[128,2048]{1,0:T(8,128)(2,1)S(1)} collective-permute-done((bf16[128,2048]{1,0:T(8,128)(2,1)S(1)}, bf16[128,2048]{1,0:T(8,128)(2,1)S(1)}, u32[]{:S(2)}, u32[]{:S(2)}) %collective-permute-start.29) | collective-permute-done | bytes 524320 | tf_op jit(solution)/shard_map/ppermute | solution.py:183
  108.3 1.0 add_convert_fusion
  (34 shorter events, 0.1 us)
Async XLA Ops:
  1.6 1.0 copy-start.4
  2.6 0.7 copy-start.8
  3.9 10.6 %collective-permute-start.2 = (bf16[128,2176]{1,0:T(8,128)(2,1)S(1)}, bf16[128,2176]{1,0:T(8,128)(2,1)S(1)}, u32[]{:S(2)}, u32[]{:S(2)}) collective-permute-start(bf16[128,2176]{1,0:T(8,128)(2,1)S(1)} %packed.1.near_ref), channel_id=1, source_target_pairs={{0,4},{5,1},{4,8},{9,5},{8,12},{13,9},{12,14},{15,13},{14,10},{11,... | collective-permute-start | bytes 1671176 | tf_op jit(solution)/shard_map/ppermute | solution.py:174
  14.4 3.4 %collective-permute-start.21 = (bf16[128,2176]{1,0:T(8,128)(2,1)S(1)}, bf16[128,2176]{1,0:T(8,128)(2,1)S(1)}, u32[]{:S(2)}, u32[]{:S(2)}) collective-permute-start(bf16[128,2176]{1,0:T(8,128)(2,1)S(1)} %collective-permute-done.2.near_ref), channel_id=1, source_target_pairs={{0,1},{1,0},{2,3},{3,2},{4,5},{5,4},{6,7},{7,6},{8,9},{9,8},{10,11... | collective-permute-start | bytes 1671176 | tf_op jit(solution)/shard_map/ppermute | solution.py:171
  15.7 11.9 %collective-permute-start.3 = (bf16[128,2176]{1,0:T(8,128)(2,1)S(1)}, bf16[128,2176]{1,0:T(8,128)(2,1)S(1)}, u32[]{:S(2)}, u32[]{:S(2)}) collective-permute-start(bf16[128,2176]{1,0:T(8,128)(2,1)S(1)} %collective-permute-done.2.near_ref), channel_id=1, source_target_pairs={{0,4},{5,1},{4,8},{9,5},{8,12},{13,9},{12,14},{15,13},{14,10},{11,... | collective-permute-start | bytes 1671176 | tf_op jit(solution)/shard_map/ppermute | solution.py:174
  17.8 2.8 %copy-start = (bf16[1,2,2048,768]{3,2,1,0:T(8,128)(2,1)S(1)}, bf16[1,2,2048,768]{3,2,1,0:T(8,128)(2,1)}, u32[]{:S(2)}) copy-start(bf16[1,2,2048,768]{3,2,1,0:T(8,128)(2,1)} %in_ref.15) | copy-start | bytes 18874372
  20.6 1.9 %copy-start.2 = (bf16[1,768,2048]{2,1,0:T(8,128)(2,1)S(1)}, bf16[1,768,2048]{2,1,0:T(8,128)(2,1)}, u32[]{:S(2)}) copy-start(bf16[1,768,2048]{2,1,0:T(8,128)(2,1)} %down_ref.15) | copy-start | bytes 9437188
  22.5 0.7 copy-start.5
  23.2 0.7 copy-start.6
  23.9 7.4 %copy-start.1 = (bf16[1,2,2048,768]{3,2,1,0:T(8,128)(2,1)S(1)}, bf16[1,2,2048,768]{3,2,1,0:T(8,128)(2,1)}, u32[]{:S(2)}) copy-start(bf16[1,2,2048,768]{3,2,1,0:T(8,128)(2,1)} %in_ref.15) | copy-start | bytes 18874372
  23.9 7.4 %copy-start.3 = (bf16[1,768,2048]{2,1,0:T(8,128)(2,1)S(1)}, bf16[1,768,2048]{2,1,0:T(8,128)(2,1)}, u32[]{:S(2)}) copy-start(bf16[1,768,2048]{2,1,0:T(8,128)(2,1)} %down_ref.15) | copy-start | bytes 9437188
  23.9 7.4 %copy-start.7 = (bf16[1,2,768]{2,1,0:T(2,128)(2,1)S(1)}, bf16[1,2,768]{2,1,0:T(2,128)(2,1)}, u32[]{:S(2)}) copy-start(bf16[1,2,768]{2,1,0:T(2,128)(2,1)} %in_scale_ref.15) | copy-start | bytes 9220
  27.4 2.2 %collective-permute-start.22 = (bf16[128,2048]{1,0:T(8,128)(2,1)S(1)}, bf16[128,2048]{1,0:T(8,128)(2,1)S(1)}, u32[]{:S(2)}, u32[]{:S(2)}) collective-permute-start(bf16[128,2048]{1,0:T(8,128)(2,1)S(1)} %get-tuple-element.36), channel_id=1, source_target_pairs={{0,1},{1,0},{2,3},{3,2},{4,5},{5,4},{6,7},{7,6},{8,9},{9,8},{10,11... | collective-permute-start | bytes 1572872 | tf_op jit(solution)/shard_map/ppermute | solution.py:176
  27.6 3.7 %collective-permute-start.19 = (bf16[128,2176]{1,0:T(8,128)(2,1)S(1)}, bf16[128,2176]{1,0:T(8,128)(2,1)S(1)}, u32[]{:S(2)}, u32[]{:S(2)}) collective-permute-start(bf16[128,2176]{1,0:T(8,128)(2,1)S(1)} %collective-permute-done.3.near_ref), channel_id=1, source_target_pairs={{0,1},{1,0},{2,3},{3,2},{4,5},{5,4},{6,7},{7,6},{8,9},{9,8},{10,11... | collective-permute-start | bytes 1671176 | tf_op jit(solution)/shard_map/ppermute | solution.py:171
  28.0 9.5 %collective-permute-start.4 = (bf16[128,2176]{1,0:T(8,128)(2,1)S(1)}, bf16[128,2176]{1,0:T(8,128)(2,1)S(1)}, u32[]{:S(2)}, u32[]{:S(2)}) collective-permute-start(bf16[128,2176]{1,0:T(8,128)(2,1)S(1)} %collective-permute-done.3.near_ref), channel_id=1, source_target_pairs={{0,4},{5,1},{4,8},{9,5},{8,12},{13,9},{12,14},{15,13},{14,10},{11,... | collective-permute-start | bytes 1671176 | tf_op jit(solution)/shard_map/ppermute | solution.py:174
  29.7 13.4 %collective-permute-start.23 = (bf16[128,2048]{1,0:T(8,128)(2,1)S(1)}, bf16[128,2048]{1,0:T(8,128)(2,1)S(1)}, u32[]{:S(2)}, u32[]{:S(2)}) collective-permute-start(bf16[128,2048]{1,0:T(8,128)(2,1)S(1)} %add_convert_fusion.7), channel_id=1, source_target_pairs={{0,4},{5,1},{4,8},{9,5},{8,12},{13,9},{12,14},{15,13},{14,10},{11,... | collective-permute-start | bytes 1572872 | tf_op jit(solution)/shard_map/ppermute | solution.py:183
  34.6 8.5 %collective-permute-start.20 = (bf16[128,2048]{1,0:T(8,128)(2,1)S(1)}, bf16[128,2048]{1,0:T(8,128)(2,1)S(1)}, u32[]{:S(2)}, u32[]{:S(2)}) collective-permute-start(bf16[128,2048]{1,0:T(8,128)(2,1)S(1)} %get-tuple-element.34), channel_id=1, source_target_pairs={{0,1},{1,0},{2,3},{3,2},{4,5},{5,4},{6,7},{7,6},{8,9},{9,8},{10,11... | collective-permute-start | bytes 1572872 | tf_op jit(solution)/shard_map/ppermute | solution.py:176
  37.5 7.5 %collective-permute-start.17 = (bf16[128,2176]{1,0:T(8,128)(2,1)S(1)}, bf16[128,2176]{1,0:T(8,128)(2,1)S(1)}, u32[]{:S(2)}, u32[]{:S(2)}) collective-permute-start(bf16[128,2176]{1,0:T(8,128)(2,1)S(1)} %collective-permute-done.4.near_ref), channel_id=1, source_target_pairs={{0,1},{1,0},{2,3},{3,2},{4,5},{5,4},{6,7},{7,6},{8,9},{9,8},{10,11... | collective-permute-start | bytes 1671176 | tf_op jit(solution)/shard_map/ppermute | solution.py:171
  37.5 11.6 %collective-permute-start.5 = (bf16[128,2176]{1,0:T(8,128)(2,1)S(1)}, bf16[128,2176]{1,0:T(8,128)(2,1)S(1)}, u32[]{:S(2)}, u32[]{:S(2)}) collective-permute-start(bf16[128,2176]{1,0:T(8,128)(2,1)S(1)} %collective-permute-done.4.near_ref), channel_id=1, source_target_pairs={{0,4},{5,1},{4,8},{9,5},{8,12},{13,9},{12,14},{15,13},{14,10},{11,... | collective-permute-start | bytes 1671176 | tf_op jit(solution)/shard_map/ppermute | solution.py:174
  43.3 11.4 %collective-permute-start.24 = (bf16[128,2048]{1,0:T(8,128)(2,1)S(1)}, bf16[128,2048]{1,0:T(8,128)(2,1)S(1)}, u32[]{:S(2)}, u32[]{:S(2)}) collective-permute-start(bf16[128,2048]{1,0:T(8,128)(2,1)S(1)} %add_convert_fusion.6), channel_id=1, source_target_pairs={{0,4},{5,1},{4,8},{9,5},{8,12},{13,9},{12,14},{15,13},{14,10},{11,... | collective-permute-start | bytes 1572872 | tf_op jit(solution)/shard_map/ppermute | solution.py:183
  48.3 6.4 %collective-permute-start.18 = (bf16[128,2048]{1,0:T(8,128)(2,1)S(1)}, bf16[128,2048]{1,0:T(8,128)(2,1)S(1)}, u32[]{:S(2)}, u32[]{:S(2)}) collective-permute-start(bf16[128,2048]{1,0:T(8,128)(2,1)S(1)} %get-tuple-element.32), channel_id=1, source_target_pairs={{0,1},{1,0},{2,3},{3,2},{4,5},{5,4},{6,7},{7,6},{8,9},{9,8},{10,11... | collective-permute-start | bytes 1572872 | tf_op jit(solution)/shard_map/ppermute | solution.py:176
  49.1 7.5 %collective-permute-start.15 = (bf16[128,2176]{1,0:T(8,128)(2,1)S(1)}, bf16[128,2176]{1,0:T(8,128)(2,1)S(1)}, u32[]{:S(2)}, u32[]{:S(2)}) collective-permute-start(bf16[128,2176]{1,0:T(8,128)(2,1)S(1)} %collective-permute-done.5.near_ref), channel_id=1, source_target_pairs={{0,1},{1,0},{2,3},{3,2},{4,5},{5,4},{6,7},{7,6},{8,9},{9,8},{10,11... | collective-permute-start | bytes 1671176 | tf_op jit(solution)/shard_map/ppermute | solution.py:171
  49.1 11.6 %collective-permute-start.6 = (bf16[128,2176]{1,0:T(8,128)(2,1)S(1)}, bf16[128,2176]{1,0:T(8,128)(2,1)S(1)}, u32[]{:S(2)}, u32[]{:S(2)}) collective-permute-start(bf16[128,2176]{1,0:T(8,128)(2,1)S(1)} %collective-permute-done.5.near_ref), channel_id=1, source_target_pairs={{0,4},{5,1},{4,8},{9,5},{8,12},{13,9},{12,14},{15,13},{14,10},{11,... | collective-permute-start | bytes 1671176 | tf_op jit(solution)/shard_map/ppermute | solution.py:174
  54.9 11.4 %collective-permute-start.25 = (bf16[128,2048]{1,0:T(8,128)(2,1)S(1)}, bf16[128,2048]{1,0:T(8,128)(2,1)S(1)}, u32[]{:S(2)}, u32[]{:S(2)}) collective-permute-start(bf16[128,2048]{1,0:T(8,128)(2,1)S(1)} %add_convert_fusion.5), channel_id=1, source_target_pairs={{0,4},{5,1},{4,8},{9,5},{8,12},{13,9},{12,14},{15,13},{14,10},{11,... | collective-permute-start | bytes 1572872 | tf_op jit(solution)/shard_map/ppermute | solution.py:183
  59.9 6.4 %collective-permute-start.16 = (bf16[128,2048]{1,0:T(8,128)(2,1)S(1)}, bf16[128,2048]{1,0:T(8,128)(2,1)S(1)}, u32[]{:S(2)}, u32[]{:S(2)}) collective-permute-start(bf16[128,2048]{1,0:T(8,128)(2,1)S(1)} %get-tuple-element.30), channel_id=1, source_target_pairs={{0,1},{1,0},{2,3},{3,2},{4,5},{5,4},{6,7},{7,6},{8,9},{9,8},{10,11... | collective-permute-start | bytes 1572872 | tf_op jit(solution)/shard_map/ppermute | solution.py:176
  60.7 7.6 %collective-permute-start.13 = (bf16[128,2176]{1,0:T(8,128)(2,1)S(1)}, bf16[128,2176]{1,0:T(8,128)(2,1)S(1)}, u32[]{:S(2)}, u32[]{:S(2)}) collective-permute-start(bf16[128,2176]{1,0:T(8,128)(2,1)S(1)} %collective-permute-done.6.near_ref), channel_id=1, source_target_pairs={{0,1},{1,0},{2,3},{3,2},{4,5},{5,4},{6,7},{7,6},{8,9},{9,8},{10,11... | collective-permute-start | bytes 1671176 | tf_op jit(solution)/shard_map/ppermute | solution.py:171
  60.7 11.6 %collective-permute-start.7 = (bf16[128,2176]{1,0:T(8,128)(2,1)S(1)}, bf16[128,2176]{1,0:T(8,128)(2,1)S(1)}, u32[]{:S(2)}, u32[]{:S(2)}) collective-permute-start(bf16[128,2176]{1,0:T(8,128)(2,1)S(1)} %collective-permute-done.6.near_ref), channel_id=1, source_target_pairs={{0,4},{5,1},{4,8},{9,5},{8,12},{13,9},{12,14},{15,13},{14,10},{11,... | collective-permute-start | bytes 1671176 | tf_op jit(solution)/shard_map/ppermute | solution.py:174
  66.5 11.4 %collective-permute-start.26 = (bf16[128,2048]{1,0:T(8,128)(2,1)S(1)}, bf16[128,2048]{1,0:T(8,128)(2,1)S(1)}, u32[]{:S(2)}, u32[]{:S(2)}) collective-permute-start(bf16[128,2048]{1,0:T(8,128)(2,1)S(1)} %add_convert_fusion.4), channel_id=1, source_target_pairs={{0,4},{5,1},{4,8},{9,5},{8,12},{13,9},{12,14},{15,13},{14,10},{11,... | collective-permute-start | bytes 1572872 | tf_op jit(solution)/shard_map/ppermute | solution.py:183
  71.6 6.2 %collective-permute-start.14 = (bf16[128,2048]{1,0:T(8,128)(2,1)S(1)}, bf16[128,2048]{1,0:T(8,128)(2,1)S(1)}, u32[]{:S(2)}, u32[]{:S(2)}) collective-permute-start(bf16[128,2048]{1,0:T(8,128)(2,1)S(1)} %get-tuple-element.28), channel_id=1, source_target_pairs={{0,1},{1,0},{2,3},{3,2},{4,5},{5,4},{6,7},{7,6},{8,9},{9,8},{10,11... | collective-permute-start | bytes 1572872 | tf_op jit(solution)/shard_map/ppermute | solution.py:176
  72.2 7.4 %collective-permute-start.11 = (bf16[128,2176]{1,0:T(8,128)(2,1)S(1)}, bf16[128,2176]{1,0:T(8,128)(2,1)S(1)}, u32[]{:S(2)}, u32[]{:S(2)}) collective-permute-start(bf16[128,2176]{1,0:T(8,128)(2,1)S(1)} %collective-permute-done.7.near_ref), channel_id=1, source_target_pairs={{0,1},{1,0},{2,3},{3,2},{4,5},{5,4},{6,7},{7,6},{8,9},{9,8},{10,11... | collective-permute-start | bytes 1671176 | tf_op jit(solution)/shard_map/ppermute | solution.py:171
  72.2 11.6 %collective-permute-start.8 = (bf16[128,2176]{1,0:T(8,128)(2,1)S(1)}, bf16[128,2176]{1,0:T(8,128)(2,1)S(1)}, u32[]{:S(2)}, u32[]{:S(2)}) collective-permute-start(bf16[128,2176]{1,0:T(8,128)(2,1)S(1)} %collective-permute-done.7.near_ref), channel_id=1, source_target_pairs={{0,4},{5,1},{4,8},{9,5},{8,12},{13,9},{12,14},{15,13},{14,10},{11,... | collective-permute-start | bytes 1671176 | tf_op jit(solution)/shard_map/ppermute | solution.py:174
  78.1 11.4 %collective-permute-start.27 = (bf16[128,2048]{1,0:T(8,128)(2,1)S(1)}, bf16[128,2048]{1,0:T(8,128)(2,1)S(1)}, u32[]{:S(2)}, u32[]{:S(2)}) collective-permute-start(bf16[128,2048]{1,0:T(8,128)(2,1)S(1)} %add_convert_fusion.3), channel_id=1, source_target_pairs={{0,4},{5,1},{4,8},{9,5},{8,12},{13,9},{12,14},{15,13},{14,10},{11,... | collective-permute-start | bytes 1572872 | tf_op jit(solution)/shard_map/ppermute | solution.py:183
  83.0 6.4 %collective-permute-start.12 = (bf16[128,2048]{1,0:T(8,128)(2,1)S(1)}, bf16[128,2048]{1,0:T(8,128)(2,1)S(1)}, u32[]{:S(2)}, u32[]{:S(2)}) collective-permute-start(bf16[128,2048]{1,0:T(8,128)(2,1)S(1)} %get-tuple-element.26), channel_id=1, source_target_pairs={{0,1},{1,0},{2,3},{3,2},{4,5},{5,4},{6,7},{7,6},{8,9},{9,8},{10,11... | collective-permute-start | bytes 1572872 | tf_op jit(solution)/shard_map/ppermute | solution.py:176
  83.8 7.5 %collective-permute-start.9 = (bf16[128,2176]{1,0:T(8,128)(2,1)S(1)}, bf16[128,2176]{1,0:T(8,128)(2,1)S(1)}, u32[]{:S(2)}, u32[]{:S(2)}) collective-permute-start(bf16[128,2176]{1,0:T(8,128)(2,1)S(1)} %collective-permute-done.8.near_ref), channel_id=1, source_target_pairs={{0,1},{1,0},{2,3},{3,2},{4,5},{5,4},{6,7},{7,6},{8,9},{9,8},{10,11... | collective-permute-start | bytes 1671176 | tf_op jit(solution)/shard_map/ppermute | solution.py:171
  83.8 10.9 %collective-permute-start = (bf16[128,2176]{1,0:T(8,128)(2,1)S(1)}, bf16[128,2176]{1,0:T(8,128)(2,1)S(1)}, u32[]{:S(2)}, u32[]{:S(2)}) collective-permute-start(bf16[128,2176]{1,0:T(8,128)(2,1)S(1)} %packed.1.near_ref), channel_id=1, source_target_pairs={{0,1},{1,0},{2,3},{3,2},{4,5},{5,4},{6,7},{7,6},{8,9},{9,8},{10,11... | collective-permute-start | bytes 1671176 | tf_op jit(solution)/shard_map/ppermute | solution.py:171
  89.7 9.2 %collective-permute-start.28 = (bf16[128,2048]{1,0:T(8,128)(2,1)S(1)}, bf16[128,2048]{1,0:T(8,128)(2,1)S(1)}, u32[]{:S(2)}, u32[]{:S(2)}) collective-permute-start(bf16[128,2048]{1,0:T(8,128)(2,1)S(1)} %add_convert_fusion.2), channel_id=1, source_target_pairs={{0,4},{5,1},{4,8},{9,5},{8,12},{13,9},{12,14},{15,13},{14,10},{11,... | collective-permute-start | bytes 1572872 | tf_op jit(solution)/shard_map/ppermute | solution.py:183
  94.6 4.3 %collective-permute-start.10 = (bf16[128,2048]{1,0:T(8,128)(2,1)S(1)}, bf16[128,2048]{1,0:T(8,128)(2,1)S(1)}, u32[]{:S(2)}, u32[]{:S(2)}) collective-permute-start(bf16[128,2048]{1,0:T(8,128)(2,1)S(1)} %get-tuple-element.24), channel_id=1, source_target_pairs={{0,1},{1,0},{2,3},{3,2},{4,5},{5,4},{6,7},{7,6},{8,9},{9,8},{10,11... | collective-permute-start | bytes 1572872 | tf_op jit(solution)/shard_map/ppermute | solution.py:176
  98.0 2.7 %collective-permute-start.1 = (bf16[128,2048]{1,0:T(8,128)(2,1)S(1)}, bf16[128,2048]{1,0:T(8,128)(2,1)S(1)}, u32[]{:S(2)}, u32[]{:S(2)}) collective-permute-start(bf16[128,2048]{1,0:T(8,128)(2,1)S(1)} %get-tuple-element.22), channel_id=1, source_target_pairs={{0,1},{1,0},{2,3},{3,2},{4,5},{5,4},{6,7},{7,6},{8,9},{9,8},{10,11... | collective-permute-start | bytes 1572872 | tf_op jit(solution)/shard_map/ppermute | solution.py:176
  99.1 9.2 %collective-permute-start.29 = (bf16[128,2048]{1,0:T(8,128)(2,1)S(1)}, bf16[128,2048]{1,0:T(8,128)(2,1)S(1)}, u32[]{:S(2)}, u32[]{:S(2)}) collective-permute-start(bf16[128,2048]{1,0:T(8,128)(2,1)S(1)} %add_convert_fusion.1), channel_id=1, source_target_pairs={{0,4},{5,1},{4,8},{9,5},{8,12},{13,9},{12,14},{15,13},{14,10},{11,... | collective-permute-start | bytes 1572872 | tf_op jit(solution)/shard_map/ppermute | solution.py:183

commit v3 on v2

--- a/solution.py
+++ b/solution.py
@@ -6,6 +6,7 @@
 from jax.experimental import pallas as pl
 from jax.experimental.pallas import tpu as pltpu
 from jax.sharding import PartitionSpec as P
+
 
 TILE = 256
 SMALL = 8 << 20
@@ -47,7 +48,7 @@
         .set(repeated)
     )
     received = lax.all_to_all(outgoing, "tok", split_axis=0, concat_axis=0, tiled=True)
-    source_count, slot_count, unused_width = received.shape
+    source_count, slot_count, _ = received.shape
     flat_rows = received.reshape(source_count * slot_count, model_width)
     served = expert_rows(flat_rows, in_q[0], in_scale[0], down_q[0], down_scale[0])
     served = served.astype(jnp.bfloat16).reshape(source_count, slot_count, model_width)
@@ -68,34 +69,95 @@
     return pairs, chips
 
 
-def packed_kernel(experts, tokens_ref, gain_ref, ids_ref, gates_ref, out_ref):
-    tok_rows, model_width = tokens_ref.shape
-    values = tokens_ref[...].astype(jnp.float32)
+def in_hbm(array):
+    return pltpu.with_memory_space_constraint(array, pltpu.HBM)
+
+
+def packed_kernel(experts, tokens_hbm, gain_hbm, ids_hbm, gates_hbm, out_ref, tokens, gain, ids, gates, sems):
+    moves = [
+        pltpu.make_async_copy(source, target, sems.at[i])
+        for i, (source, target) in enumerate(
+            ((ids_hbm, ids), (gates_hbm, gates), (tokens_hbm, tokens), (gain_hbm, gain))
+        )
+    ]
+    for move in moves:
+        move.start()
+    tok_rows, model_width = tokens.shape
+    lanes = out_ref.shape[1] - model_width
+    moves[0].wait()
+    moves[1].wait()
+    weights = gates[...] / jnp.sum(gates[...], axis=0, keepdims=True)
+    row = lax.broadcasted_iota(jnp.int32, (lanes, tok_rows), 0)
+    label = jnp.where(row < experts, row, row - experts)
+    table = jnp.zeros((lanes, tok_rows), jnp.float32)
+    for k in range(ids.shape[0]):
+        table += jnp.where(label == ids[k : k + 1, :], weights[k : k + 1, :], 0.0)
+    high = table.astype(jnp.bfloat16).astype(jnp.float32)
+    halves = jnp.where(row < experts, high, table - high)
+    out_ref[:, model_width:] = jnp.transpose(halves).astype(jnp.bfloat16)
+    moves[2].wait()
+    moves[3].wait()
+    values = tokens[...].astype(jnp.float32)
     row_scale = lax.rsqrt(jnp.mean(values * values, axis=1, keepdims=True) + 1e-06)
-    out_ref[:, :model_width] = (values * row_scale * gain_ref[...]).astype(jnp.bfloat16)
-    gates = gates_ref[...]
-    weights = gates / jnp.sum(gates, axis=1, keepdims=True)
-    lanes = out_ref.shape[1] - model_width
-    lane = lax.broadcasted_iota(jnp.int32, (tok_rows, lanes), 1)
-    label = jnp.where(lane < experts, lane, lane - experts)
-    table = jnp.zeros((tok_rows, lanes), jnp.float32)
-    for k in range(ids_ref.shape[1]):
-        table += jnp.where(label == ids_ref[:, k : k + 1], weights[:, k : k + 1], 0.0)
-    high = table.astype(jnp.bfloat16).astype(jnp.float32)
-    out_ref[:, model_width:] = jnp.where(lane < experts, high, table - high).astype(jnp.bfloat16)
+    out_ref[:, :model_width] = (values * row_scale * gain[...]).astype(jnp.bfloat16)
 
 
 def packed(tokens, norm_gain, expert_ids, gate_weights, experts):
     tok_rows, model_width = tokens.shape
+    top_count = expert_ids.shape[1]
     lanes = -(-2 * experts // 128) * 128
     return pl.pallas_call(
         functools.partial(packed_kernel, experts),
         out_shape=jax.ShapeDtypeStruct((tok_rows, model_width + lanes), jnp.bfloat16),
-        in_specs=[pl.BlockSpec(memory_space=pltpu.VMEM)] * 4,
+        in_specs=[pl.BlockSpec(memory_space=pltpu.HBM)] * 4,
         out_specs=pl.BlockSpec(memory_space=pltpu.VMEM),
+        scratch_shapes=[
+            pltpu.VMEM((tok_rows, model_width), jnp.bfloat16),
+            pltpu.VMEM((1, model_width), jnp.float32),
+            pltpu.VMEM((top_count, tok_rows), jnp.int32),
+            pltpu.VMEM((top_count, tok_rows), jnp.float32),
+            pltpu.SemaphoreType.DMA((4,)),
+        ],
         compiler_params=pltpu.CompilerParams(vmem_limit_bytes=SMALL),
         name="packed",
-    )(tokens, norm_gain[None, :], expert_ids, gate_weights)
+    )(*map(in_hbm, (tokens, norm_gain[None, :], expert_ids.T, gate_weights.T)))
+
+
+def loaded_kernel(
+    owner_ref, in_hbm, in_scale_hbm, down_hbm, down_scale_hbm,
+    mine_ref, in_ref, in_scale_ref, down_ref, down_scale_ref, sems,
+):
+    pairs = (
+        (in_hbm, in_ref), (in_scale_hbm, in_scale_ref), (down_hbm, down_ref), (down_scale_hbm, down_scale_ref),
+    )
+    moves = [
+        pltpu.make_async_copy(source, target, sems.at[i]) for i, (source, target) in enumerate(pairs)
+    ]
+    for move in moves:
+        move.start()
+    me = lax.axis_index("tok")
+    mine_ref[0] = lax.fori_loop(
+        0, owner_ref.shape[0], lambda i, found: jnp.where(owner_ref[i] == me, i, found), 0
+    )
+    for move in moves:
+        move.wait()
+
+
+def loaded(owner_map, in_q, in_scale, down_q, down_scale):
+    blocks = (in_q, in_scale, down_q, down_scale)
+    return pl.pallas_call(
+        loaded_kernel,
+        out_shape=(jax.ShapeDtypeStruct((1,), jnp.int32),)
+        + tuple(jax.ShapeDtypeStruct(x.shape, x.dtype) for x in blocks),
+        in_specs=[pl.BlockSpec(memory_space=pltpu.SMEM)] + [pl.BlockSpec(memory_space=pltpu.HBM)] * 4,
+        out_specs=(pl.BlockSpec(memory_space=pltpu.SMEM),) + (pl.BlockSpec(memory_space=pltpu.VMEM),) * 4,
+        scratch_shapes=[pltpu.SemaphoreType.DMA((4,))],
+        compiler_params=pltpu.CompilerParams(vmem_limit_bytes=SMALL),
+        cost_estimate=pl.CostEstimate(
+            flops=0, bytes_accessed=2 * (in_q.size + down_q.size), transcendentals=0
+        ),
+        name="loaded",
+    )(owner_map, *map(in_hbm, blocks))
 
 
 def visit_kernel(
@@ -161,50 +223,61 @@
     devices = lax.axis_size("tok")
     ring, chips = ring_pairs(devices)
     swap = [(i, i ^ 1) for i in range(devices)]
-    me = lax.axis_index("tok")
-    labels = jnp.arange(experts, dtype=jnp.int32)
-    my_expert = jnp.sum(jnp.where(owner_map == me, labels, 0), keepdims=True)
+    half = tokens.shape[0] // 2
     block = packed(tokens, norm_gain, expert_ids, gate_weights, experts)
-
-    total = None
+    mine, *blocks = loaded(owner_map, in_q, in_scale, down_q, down_scale)
+
+    parts = []
     for step in range(chips):
         other = lax.ppermute(block, "tok", swap)
         here = block
         if step < chips - 1:
             block = lax.ppermute(block, "tok", ring)
-        part, lent = visit(my_expert, here, other, experts, in_q, in_scale, down_q, down_scale)
-        lent = lax.ppermute(lent, "tok", swap)
-        part = part + lent.astype(jnp.float32)
-        if step == 0:
-            own = part
-            continue
+        part, lent = visit(mine, here, other, experts, *blocks)
+        parts.append((part, lax.ppermute(lent, "tok", swap)))
+
+    total = None
+    for step in range(1, chips):
+        part, lent = parts[step]
+        cuts = (slice(None),) if step < chips - 2 else (slice(0, half), slice(half, None))
+        if total is not None and len(total) < len(cuts):
+            total = [total[0][cut] for cut in cuts]
+        sums = [part[cut] + lent[cut].astype(jnp.float32) for cut in cuts]
         if total is not None:
-            part = part + total.astype(jnp.float32)
-        total = lax.ppermute(part.astype(jnp.bfloat16), "tok", ring)
-    return (own + total.astype(jnp.float32)).astype(jnp.bfloat16)
+            sums = [x + y.astype(jnp.float32) for x, y in zip(sums, total)]
+        total = [lax.ppermute(x.astype(jnp.bfloat16), "tok", ring) for x in sums]
+    part, lent = parts[0]
+    return jnp.concatenate(
+        [
+            (part[cut] + lent[cut].astype(jnp.float32) + x.astype(jnp.float32)).astype(jnp.bfloat16)
+            for cut, x in zip((slice(0, half), slice(half, None)), total)
+        ]
+    )
 
 
 def solution(mesh):
-    def on_device(tokens, norm_gain, expert_ids, gate_weights, owner_map, *blocks):
-        tok_rows, experts = tokens.shape[0], owner_map.shape[0]
+    devices = mesh.shape["tok"]
+    row = P(("grp", "tok"), None)
+    slot = [P("tok", *(None,) * extra) for extra in (3, 2, 2, 1)]
+
+    def placed(body):
+        return jax.shard_map(
+            body,
+            mesh=mesh,
+            in_specs=(row, P(), row, row, P(), *slot),
+            out_specs=row,
+            check_vma=False,
+        )
+
+
+    def step(tokens, norm_gain, expert_ids, gate_weights, owner_map, *blocks):
+        tok_rows = tokens.shape[0] // mesh.size
+        experts = owner_map.shape[0]
         mean_load = tok_rows * expert_ids.shape[1] // experts
         routed = experts * (mean_load + mean_load // 2)
-        dense = tok_rows * mesh.shape["tok"]
-        form = circulated if dense <= 2 * routed and mesh.shape["tok"] % 4 == 0 else exchanged
-        return form(tokens, norm_gain, expert_ids, gate_weights, owner_map, *blocks)
-
-    in_specs = (
-        P(("grp", "tok"), None),
-        P(),
-        P(("grp", "tok"), None),
-        P(("grp", "tok"), None),
-        P(),
-        P("tok", None, None, None),
-        P("tok", None, None),
-        P("tok", None, None),
-        P("tok", None),
-    )
-    out_specs = P(("grp", "tok"), None)
-    return jax.shard_map(
-        on_device, mesh=mesh, in_specs=in_specs, out_specs=out_specs, check_vma=False
-    )
+        arguments = (tokens, norm_gain, expert_ids, gate_weights, owner_map, *blocks)
+        if tok_rows * devices > 2 * routed or devices % 4:
+            return placed(exchanged)(*arguments)
+        return placed(circulated)(*arguments)
+
+    return step

time: 110 us -> 113 us (1.027)
  local copies, waits for them, and re-layouts: 9.37 us -> 0.66 us
  starting transfers between devices: 26.7 us -> 34.3 us
  Pallas kernels: 27.2 us -> 32.7 us
  other arithmetic: 3.58 us -> 2.3 us
    ppermute x7, waiting for transfers between devices: 12.9 us -> 23.3 us  [circulated(): block = lax.ppermute(block, 'tok', ring)]
    ppermute x15 -> x17, waiting for transfers between devices: 29.2 us -> 19 us  [the longest x9 19 us: circulated(): total = [lax.ppermute(x.astype(jnp.bfloat16), 'tok', ring) for x in sums]]
    unnamed x20 -> x2, local copies, waits for them, and re-layouts: 9.37 us -> 0.66 us
    ppermute x15 -> x17, starting transfers between devices: 12.8 us -> 17.9 us  [the longest x9 16.8 us: circulated(): total = [lax.ppermute(x.astype(jnp.bfloat16), 'tok', ring) for x in sums]]
    pallas_call x0 -> x1, Pallas kernels: none -> 4.82 us  [loaded(): pl.pallas_call(loaded_kernel, out_shape=(jax.ShapeDtypeStruct((1,), jnp.i...]
    ppermute x7, starting transfers between devices: 13.1 us -> 15.3 us  [circulated(): block = lax.ppermute(block, 'tok', ring)]
    reduce_sum x1 -> x0, other arithmetic: 1.29 us -> none  [circulated(): my_expert = jnp.sum(jnp.where(owner_map == me, labels, 0), keepdims=True)]
  transfers between devices with their start and end apart: 30 -> 32, of which waited for: 13 -> 13; matrix products, arithmetic and copies ran while one was open for 2% -> 1% of each run, Pallas kernels for 24% -> 28%
where the time goes in v3:
time: 113 us
  waiting for transfers between devices  42.3 us (37%)
  starting transfers between devices  34.3 us (30%)
  Pallas kernels  32.7 us (29%)
  other arithmetic  2.3 us (2%)
    pallas_call x8, Pallas kernels, visit(): pl.pallas_call(functools.partial(visit_kernel, experts), out_shape=(jax.S...  26.6 us
    ppermute x7, waiting for transfers between devices, circulated(): block = lax.ppermute(block, 'tok', ring)  23.3 us
    ppermute x9, waiting for transfers between devices, circulated(): total = [lax.ppermute(x.astype(jnp.bfloat16), 'tok', ring) for x in sums]  19 us
    ppermute x9, starting transfers between devices, circulated(): total = [lax.ppermute(x.astype(jnp.bfloat16), 'tok', ring) for x in sums]  16.8 us
    ppermute x7, starting transfers between devices, circulated(): block = lax.ppermute(block, 'tok', ring)  15.3 us
    pallas_call x1, Pallas kernels, loaded(): pl.pallas_call(loaded_kernel, out_shape=(jax.ShapeDtypeStruct((1,), jnp.i...  4.82 us
  transfers between devices with their start and end apart: 32, of which 13 were waited for; matrix products, arithmetic and copies ran while one was open for 1% of the time, Pallas kernels for 28%

profile of v3, /device:TPU:0, one launch (start us, length us, event | category | flops | bytes accessed | tf_op | source)
XLA Modules:
  0.0 112.6 jit_solution(12790546601732371630)
XLA Ops:
  0.0 1.3 %packed.1.near_ref = bf16[128,2176]{1,0:T(8,128)(2,1)S(1)} custom-call(bf16[128,2048]{1,0:T(8,128)(2,1)} %tokens_hbm.1, f32[1,2048]{1,0:T(1,128)} %bitcast.3, s32[8,128]{1,0:T(8,128)} %bitcast.4, f32[8,128]{1,0:T(8,128)} %bitcast.5), custom_call_target="tpu_custom_call" | custom-call | tf_op jit(solution)/shard_map/packed/pallas_call | solution.py:109
  1.3 3.1 %collective-permute-start.2 = (bf16[128,2176]{1,0:T(8,128)(2,1)S(1)}, bf16[128,2176]{1,0:T(8,128)(2,1)S(1)}, u32[]{:S(2)}, u32[]{:S(2)}) collective-permute-start(bf16[128,2176]{1,0:T(8,128)(2,1)S(1)} %packed.1.near_ref), channel_id=1, source_target_pairs={{0,4},{5,1},{4,8},{9,5},{8,12},{13,9},{12,14},{15,13},{14,10},{11,... | collective-permute-start | bytes 1671176 | tf_op jit(solution)/shard_map/ppermute | solution.py:235
  4.4 7.5 %collective-permute-done.2.near_ref = bf16[128,2176]{1,0:T(8,128)(2,1)S(1)} collective-permute-done((bf16[128,2176]{1,0:T(8,128)(2,1)S(1)}, bf16[128,2176]{1,0:T(8,128)(2,1)S(1)}, u32[]{:S(2)}, u32[]{:S(2)}) %collective-permute-start.2) | collective-permute-done | bytes 557088 | tf_op jit(solution)/shard_map/ppermute | solution.py:235
  11.9 0.0 collective-permute-start.21
  11.9 0.7 copy-done
  12.6 4.8 %loaded.1 = (s32[1]{0:T(128)}, bf16[1,2,2048,768]{3,2,1,0:T(8,128)(2,1)S(1)}, bf16[1,2,768]{2,1,0:T(2,128)(2,1)S(1)}, bf16[1,768,2048]{2,1,0:T(8,128)(2,1)S(1)}, bf16[1,2048]{1,0:T(2,128)(2,1)S(1)}) custom-call(s32[16]{0:T(128)S(1)} %copy-done, bf16[1,2,2048,768]{3,2,1,0:T(8,128)(2,1)} %in_hbm.1, bf16[1,2,768]{2,1,0:T(2,128)(2,1)} %in_scale_hbm.1, ...), custom_call_target="tpu_custom_call" | custom-call | bytes 9437184 | tf_op jit(solution)/shard_map/loaded/pallas_call | solution.py:148
  17.4 2.1 %collective-permute-start.3 = (bf16[128,2176]{1,0:T(8,128)(2,1)S(1)}, bf16[128,2176]{1,0:T(8,128)(2,1)S(1)}, u32[]{:S(2)}, u32[]{:S(2)}) collective-permute-start(bf16[128,2176]{1,0:T(8,128)(2,1)S(1)} %collective-permute-done.2.near_ref), channel_id=1, source_target_pairs={{0,4},{5,1},{4,8},{9,5},{8,12},{13,9},{12,14},{15,13},{14,10},{11,... | collective-permute-start | bytes 1671176 | tf_op jit(solution)/shard_map/ppermute | solution.py:235
  19.5 0.0 collective-permute-done.21.far_ref
  19.5 3.3 %visit.15 = (f32[128,2048]{1,0:T(8,128)S(1)}, bf16[128,2048]{1,0:T(8,128)(2,1)S(1)}) custom-call(s32[1]{0:T(128)} %get-tuple-element.26.mine_ref, bf16[128,2176]{1,0:T(8,128)(2,1)S(1)} %collective-permute-done.2.near_ref, bf16[128,2176]{1,0:T(8,128)(2,1)S(1)} %collective-permute-done.21.far_ref, bf16[1,2,2048,768]{3,2,1,0:T(8,128)(2,1)S(1)} %get-tuple-element.27.in_ref, ...), custom_call_target="tpu_custom_call" | custom-call | flops 2415919104 | bytes 1572864 | tf_op jit(solution)/shard_map/visit/pallas_call | solution.py:198
  22.9 0.2 collective-permute-start.22
  23.1 3.9 %collective-permute-done.3.near_ref = bf16[128,2176]{1,0:T(8,128)(2,1)S(1)} collective-permute-done((bf16[128,2176]{1,0:T(8,128)(2,1)S(1)}, bf16[128,2176]{1,0:T(8,128)(2,1)S(1)}, u32[]{:S(2)}, u32[]{:S(2)}) %collective-permute-start.3) | collective-permute-done | bytes 557088 | tf_op jit(solution)/shard_map/ppermute | solution.py:235
  27.0 2.1 %collective-permute-start.4 = (bf16[128,2176]{1,0:T(8,128)(2,1)S(1)}, bf16[128,2176]{1,0:T(8,128)(2,1)S(1)}, u32[]{:S(2)}, u32[]{:S(2)}) collective-permute-start(bf16[128,2176]{1,0:T(8,128)(2,1)S(1)} %collective-permute-done.3.near_ref), channel_id=1, source_target_pairs={{0,4},{5,1},{4,8},{9,5},{8,12},{13,9},{12,14},{15,13},{14,10},{11,... | collective-permute-start | bytes 1671176 | tf_op jit(solution)/shard_map/ppermute | solution.py:235
  29.1 0.0 collective-permute-done.22
  29.1 0.1 add_convert_fusion.4
  29.2 1.6 %collective-permute-start.23 = (bf16[128,2048]{1,0:T(8,128)(2,1)S(1)}, bf16[128,2048]{1,0:T(8,128)(2,1)S(1)}, u32[]{:S(2)}, u32[]{:S(2)}) collective-permute-start(bf16[128,2048]{1,0:T(8,128)(2,1)S(1)} %add_convert_fusion.4), channel_id=1, source_target_pairs={{0,4},{5,1},{4,8},{9,5},{8,12},{13,9},{12,14},{15,13},{14,10},{11,... | collective-permute-start | bytes 1572872 | tf_op jit(solution)/shard_map/ppermute | solution.py:248
  30.8 3.3 %visit.14 = (f32[128,2048]{1,0:T(8,128)S(1)}, bf16[128,2048]{1,0:T(8,128)(2,1)S(1)}) custom-call(s32[1]{0:T(128)} %get-tuple-element.26.mine_ref, bf16[128,2176]{1,0:T(8,128)(2,1)S(1)} %collective-permute-done.3.near_ref, bf16[128,2176]{1,0:T(8,128)(2,1)S(1)} %collective-permute-done.19.far_ref, bf16[1,2,2048,768]{3,2,1,0:T(8,128)(2,1)S(1)} %get-tuple-element.27.in_ref, ...), custom_call_target="tpu_custom_call" | custom-call | flops 2415919104 | bytes 1572864 | tf_op jit(solution)/shard_map/visit/pallas_call | solution.py:198
  34.1 0.1 collective-permute-start.20
  34.2 2.3 %collective-permute-done.4.near_ref = bf16[128,2176]{1,0:T(8,128)(2,1)S(1)} collective-permute-done((bf16[128,2176]{1,0:T(8,128)(2,1)S(1)}, bf16[128,2176]{1,0:T(8,128)(2,1)S(1)}, u32[]{:S(2)}, u32[]{:S(2)}) %collective-permute-start.4) | collective-permute-done | bytes 557088 | tf_op jit(solution)/shard_map/ppermute | solution.py:235
  36.5 0.0 collective-permute-start.17
  36.5 2.1 %collective-permute-start.5 = (bf16[128,2176]{1,0:T(8,128)(2,1)S(1)}, bf16[128,2176]{1,0:T(8,128)(2,1)S(1)}, u32[]{:S(2)}, u32[]{:S(2)}) collective-permute-start(bf16[128,2176]{1,0:T(8,128)(2,1)S(1)} %collective-permute-done.4.near_ref), channel_id=1, source_target_pairs={{0,4},{5,1},{4,8},{9,5},{8,12},{13,9},{12,14},{15,13},{14,10},{11,... | collective-permute-start | bytes 1671176 | tf_op jit(solution)/shard_map/ppermute | solution.py:235
  38.6 3.5 %collective-permute-done.23 = bf16[128,2048]{1,0:T(8,128)(2,1)S(1)} collective-permute-done((bf16[128,2048]{1,0:T(8,128)(2,1)S(1)}, bf16[128,2048]{1,0:T(8,128)(2,1)S(1)}, u32[]{:S(2)}, u32[]{:S(2)}) %collective-permute-start.23) | collective-permute-done | bytes 524320 | tf_op jit(solution)/shard_map/ppermute | solution.py:248
  42.1 0.2 add_convert_fusion.3
  42.3 2.1 %collective-permute-start.24 = (bf16[128,2048]{1,0:T(8,128)(2,1)S(1)}, bf16[128,2048]{1,0:T(8,128)(2,1)S(1)}, u32[]{:S(2)}, u32[]{:S(2)}) collective-permute-start(bf16[128,2048]{1,0:T(8,128)(2,1)S(1)} %add_convert_fusion.3), channel_id=1, source_target_pairs={{0,4},{5,1},{4,8},{9,5},{8,12},{13,9},{12,14},{15,13},{14,10},{11,... | collective-permute-start | bytes 1572872 | tf_op jit(solution)/shard_map/ppermute | solution.py:248
  44.5 3.3 %visit.13 = (f32[128,2048]{1,0:T(8,128)S(1)}, bf16[128,2048]{1,0:T(8,128)(2,1)S(1)}) custom-call(s32[1]{0:T(128)} %get-tuple-element.26.mine_ref, bf16[128,2176]{1,0:T(8,128)(2,1)S(1)} %collective-permute-done.4.near_ref, bf16[128,2176]{1,0:T(8,128)(2,1)S(1)} %collective-permute-done.17.far_ref, bf16[1,2,2048,768]{3,2,1,0:T(8,128)(2,1)S(1)} %get-tuple-element.27.in_ref, ...), custom_call_target="tpu_custom_call" | custom-call | flops 2415919104 | bytes 1572864 | tf_op jit(solution)/shard_map/visit/pallas_call | solution.py:198
  47.8 0.1 collective-permute-start.18
  47.9 0.2 collective-permute-done.5.near_ref
  48.1 0.3 collective-permute-start.15
  48.4 1.8 %collective-permute-start.6 = (bf16[128,2176]{1,0:T(8,128)(2,1)S(1)}, bf16[128,2176]{1,0:T(8,128)(2,1)S(1)}, u32[]{:S(2)}, u32[]{:S(2)}) collective-permute-start(bf16[128,2176]{1,0:T(8,128)(2,1)S(1)} %collective-permute-done.5.near_ref), channel_id=1, source_target_pairs={{0,4},{5,1},{4,8},{9,5},{8,12},{13,9},{12,14},{15,13},{14,10},{11,... | collective-permute-start | bytes 1671176 | tf_op jit(solution)/shard_map/ppermute | solution.py:235
  50.2 3.5 %collective-permute-done.24 = bf16[128,2048]{1,0:T(8,128)(2,1)S(1)} collective-permute-done((bf16[128,2048]{1,0:T(8,128)(2,1)S(1)}, bf16[128,2048]{1,0:T(8,128)(2,1)S(1)}, u32[]{:S(2)}, u32[]{:S(2)}) %collective-permute-start.24) | collective-permute-done | bytes 524320 | tf_op jit(solution)/shard_map/ppermute | solution.py:248
  53.7 0.2 add_convert_fusion.2
  53.9 2.1 %collective-permute-start.25 = (bf16[128,2048]{1,0:T(8,128)(2,1)S(1)}, bf16[128,2048]{1,0:T(8,128)(2,1)S(1)}, u32[]{:S(2)}, u32[]{:S(2)}) collective-permute-start(bf16[128,2048]{1,0:T(8,128)(2,1)S(1)} %add_convert_fusion.2), channel_id=1, source_target_pairs={{0,4},{5,1},{4,8},{9,5},{8,12},{13,9},{12,14},{15,13},{14,10},{11,... | collective-permute-start | bytes 1572872 | tf_op jit(solution)/shard_map/ppermute | solution.py:248
  56.0 3.3 %visit.12 = (f32[128,2048]{1,0:T(8,128)S(1)}, bf16[128,2048]{1,0:T(8,128)(2,1)S(1)}) custom-call(s32[1]{0:T(128)} %get-tuple-element.26.mine_ref, bf16[128,2176]{1,0:T(8,128)(2,1)S(1)} %collective-permute-done.5.near_ref, bf16[128,2176]{1,0:T(8,128)(2,1)S(1)} %collective-permute-done.15.far_ref, bf16[1,2,2048,768]{3,2,1,0:T(8,128)(2,1)S(1)} %get-tuple-element.27.in_ref, ...), custom_call_target="tpu_custom_call" | custom-call | flops 2415919104 | bytes 1572864 | tf_op jit(solution)/shard_map/visit/pallas_call | solution.py:198
  59.4 0.1 collective-permute-start.16
  59.5 0.2 collective-permute-done.6.near_ref
  59.7 2.1 %collective-permute-start.7 = (bf16[128,2176]{1,0:T(8,128)(2,1)S(1)}, bf16[128,2176]{1,0:T(8,128)(2,1)S(1)}, u32[]{:S(2)}, u32[]{:S(2)}) collective-permute-start(bf16[128,2176]{1,0:T(8,128)(2,1)S(1)} %collective-permute-done.6.near_ref), channel_id=1, source_target_pairs={{0,4},{5,1},{4,8},{9,5},{8,12},{13,9},{12,14},{15,13},{14,10},{11,... | collective-permute-start | bytes 1671176 | tf_op jit(solution)/shard_map/ppermute | solution.py:235
  61.8 3.5 %collective-permute-done.25 = bf16[128,2048]{1,0:T(8,128)(2,1)S(1)} collective-permute-done((bf16[128,2048]{1,0:T(8,128)(2,1)S(1)}, bf16[128,2048]{1,0:T(8,128)(2,1)S(1)}, u32[]{:S(2)}, u32[]{:S(2)}) %collective-permute-start.25) | collective-permute-done | bytes 524320 | tf_op jit(solution)/shard_map/ppermute | solution.py:248
  65.3 0.2 add_convert_fusion.1
  65.5 2.1 %collective-permute-start.26 = (bf16[128,2048]{1,0:T(8,128)(2,1)S(1)}, bf16[128,2048]{1,0:T(8,128)(2,1)S(1)}, u32[]{:S(2)}, u32[]{:S(2)}) collective-permute-start(bf16[128,2048]{1,0:T(8,128)(2,1)S(1)} %add_convert_fusion.1), channel_id=1, source_target_pairs={{0,4},{5,1},{4,8},{9,5},{8,12},{13,9},{12,14},{15,13},{14,10},{11,... | collective-permute-start | bytes 1572872 | tf_op jit(solution)/shard_map/ppermute | solution.py:248
  67.6 3.6 %collective-permute-done.7.near_ref = bf16[128,2176]{1,0:T(8,128)(2,1)S(1)} collective-permute-done((bf16[128,2176]{1,0:T(8,128)(2,1)S(1)}, bf16[128,2176]{1,0:T(8,128)(2,1)S(1)}, u32[]{:S(2)}, u32[]{:S(2)}) %collective-permute-start.7) | collective-permute-done | bytes 557088 | tf_op jit(solution)/shard_map/ppermute | solution.py:235
  71.3 2.1 %collective-permute-start.8 = (bf16[128,2176]{1,0:T(8,128)(2,1)S(1)}, bf16[128,2176]{1,0:T(8,128)(2,1)S(1)}, u32[]{:S(2)}, u32[]{:S(2)}) collective-permute-start(bf16[128,2176]{1,0:T(8,128)(2,1)S(1)} %collective-permute-done.7.near_ref), channel_id=1, source_target_pairs={{0,4},{5,1},{4,8},{9,5},{8,12},{13,9},{12,14},{15,13},{14,10},{11,... | collective-permute-start | bytes 1671176 | tf_op jit(solution)/shard_map/ppermute | solution.py:235
  73.3 3.3 %visit.11 = (f32[128,2048]{1,0:T(8,128)S(1)}, bf16[128,2048]{1,0:T(8,128)(2,1)S(1)}) custom-call(s32[1]{0:T(128)} %get-tuple-element.26.mine_ref, bf16[128,2176]{1,0:T(8,128)(2,1)S(1)} %collective-permute-done.6.near_ref, bf16[128,2176]{1,0:T(8,128)(2,1)S(1)} %collective-permute-done.13.far_ref, bf16[1,2,2048,768]{3,2,1,0:T(8,128)(2,1)S(1)} %get-tuple-element.27.in_ref, ...), custom_call_target="tpu_custom_call" | custom-call | flops 2415919104 | bytes 1572864 | tf_op jit(solution)/shard_map/visit/pallas_call | solution.py:198
  76.7 0.1 collective-permute-start.14
  76.8 0.5 collective-permute-start.11
  77.3 5.6 %collective-permute-done.8.near_ref = bf16[128,2176]{1,0:T(8,128)(2,1)S(1)} collective-permute-done((bf16[128,2176]{1,0:T(8,128)(2,1)S(1)}, bf16[128,2176]{1,0:T(8,128)(2,1)S(1)}, u32[]{:S(2)}, u32[]{:S(2)}) %collective-permute-start.8) | collective-permute-done | bytes 557088 | tf_op jit(solution)/shard_map/ppermute | solution.py:235
  82.9 0.2 add_convert_fusion
  83.1 2.1 %collective-permute-start.27 = (bf16[128,2048]{1,0:T(8,128)(2,1)S(1)}, bf16[128,2048]{1,0:T(8,128)(2,1)S(1)}, u32[]{:S(2)}, u32[]{:S(2)}) collective-permute-start(bf16[128,2048]{1,0:T(8,128)(2,1)S(1)} %add_convert_fusion), channel_id=1, source_target_pairs={{0,4},{5,1},{4,8},{9,5},{8,12},{13,9},{12,14},{15,13},{14,10},{11,... | collective-permute-start | bytes 1572872 | tf_op jit(solution)/shard_map/ppermute | solution.py:248
  85.2 3.3 %visit.10 = (f32[128,2048]{1,0:T(8,128)S(1)}, bf16[128,2048]{1,0:T(8,128)(2,1)S(1)}) custom-call(s32[1]{0:T(128)} %get-tuple-element.26.mine_ref, bf16[128,2176]{1,0:T(8,128)(2,1)S(1)} %collective-permute-done.7.near_ref, bf16[128,2176]{1,0:T(8,128)(2,1)S(1)} %collective-permute-done.11.far_ref, bf16[1,2,2048,768]{3,2,1,0:T(8,128)(2,1)S(1)} %get-tuple-element.27.in_ref, ...), custom_call_target="tpu_custom_call" | custom-call | flops 2415919104 | bytes 1572864 | tf_op jit(solution)/shard_map/visit/pallas_call | solution.py:198
  88.5 0.2 collective-permute-start.12
  88.8 0.3 collective-permute-start
  89.1 3.3 %visit.9 = (f32[128,2048]{1,0:T(8,128)S(1)}, bf16[128,2048]{1,0:T(8,128)(2,1)S(1)}) custom-call(s32[1]{0:T(128)} %get-tuple-element.26.mine_ref, bf16[128,2176]{1,0:T(8,128)(2,1)S(1)} %collective-permute-done.8.near_ref, bf16[128,2176]{1,0:T(8,128)(2,1)S(1)} %collective-permute-done.9.far_ref, bf16[1,2,2048,768]{3,2,1,0:T(8,128)(2,1)S(1)} %get-tuple-element.27.in_ref, ...), custom_call_target="tpu_custom_call" | custom-call | flops 2415919104 | bytes 1572864 | tf_op jit(solution)/shard_map/visit/pallas_call | solution.py:198
  92.4 0.2 collective-permute-start.10
  92.7 0.2 add_convert_fusion.10
  92.9 1.8 %collective-permute-start.28 = (bf16[64,2048]{1,0:T(8,128)(2,1)S(1)}, bf16[64,2048]{1,0:T(8,128)(2,1)S(1)}, u32[]{:S(2)}, u32[]{:S(2)}) collective-permute-start(bf16[64,2048]{1,0:T(8,128)(2,1)S(1)} %get-tuple-element.47), channel_id=1, source_target_pairs={{0,4},{5,1},{4,8},{9,5},{8,12},{13,9},{12,14},{15,13},{14,10},{11,... | collective-permute-start | bytes 786440 | tf_op jit(solution)/shard_map/ppermute | solution.py:248
  94.6 1.6 %collective-permute-start.30 = (bf16[64,2048]{1,0:T(8,128)(2,1)S(1)}, bf16[64,2048]{1,0:T(8,128)(2,1)S(1)}, u32[]{:S(2)}, u32[]{:S(2)}) collective-permute-start(bf16[64,2048]{1,0:T(8,128)(2,1)S(1)} %get-tuple-element.48), channel_id=1, source_target_pairs={{0,4},{5,1},{4,8},{9,5},{8,12},{13,9},{12,14},{15,13},{14,10},{11,... | collective-permute-start | bytes 786440 | tf_op jit(solution)/shard_map/ppermute | solution.py:248
  96.2 3.3 %visit.8 = (f32[128,2048]{1,0:T(8,128)S(1)}, bf16[128,2048]{1,0:T(8,128)(2,1)S(1)}) custom-call(s32[1]{0:T(128)} %get-tuple-element.26.mine_ref, bf16[128,2176]{1,0:T(8,128)(2,1)S(1)} %packed.1.near_ref, bf16[128,2176]{1,0:T(8,128)(2,1)S(1)} %collective-permute-done.far_ref, bf16[1,2,2048,768]{3,2,1,0:T(8,128)(2,1)S(1)} %get-tuple-element.27.in_ref, ...), custom_call_target="tpu_custom_call" | custom-call | flops 2415919104 | bytes 1572864 | tf_op jit(solution)/shard_map/visit/pallas_call | solution.py:198
  99.5 0.1 collective-permute-start.1
  99.6 2.5 %collective-permute-done.30 = bf16[64,2048]{1,0:T(8,128)(2,1)S(1)} collective-permute-done((bf16[64,2048]{1,0:T(8,128)(2,1)S(1)}, bf16[64,2048]{1,0:T(8,128)(2,1)S(1)}, u32[]{:S(2)}, u32[]{:S(2)}) %collective-permute-start.30) | collective-permute-done | bytes 262176 | tf_op jit(solution)/shard_map/ppermute | solution.py:248
  102.1 0.2 add_convert_fusion.9
  102.3 1.8 %collective-permute-start.29 = (bf16[64,2048]{1,0:T(8,128)(2,1)S(1)}, bf16[64,2048]{1,0:T(8,128)(2,1)S(1)}, u32[]{:S(2)}, u32[]{:S(2)}) collective-permute-start(bf16[64,2048]{1,0:T(8,128)(2,1)S(1)} %get-tuple-element.51), channel_id=1, source_target_pairs={{0,4},{5,1},{4,8},{9,5},{8,12},{13,9},{12,14},{15,13},{14,10},{11,... | collective-permute-start | bytes 786440 | tf_op jit(solution)/shard_map/ppermute | solution.py:248
  104.1 1.6 %collective-permute-start.31 = (bf16[64,2048]{1,0:T(8,128)(2,1)S(1)}, bf16[64,2048]{1,0:T(8,128)(2,1)S(1)}, u32[]{:S(2)}, u32[]{:S(2)}) collective-permute-start(bf16[64,2048]{1,0:T(8,128)(2,1)S(1)} %get-tuple-element.52), channel_id=1, source_target_pairs={{0,4},{5,1},{4,8},{9,5},{8,12},{13,9},{12,14},{15,13},{14,10},{11,... | collective-permute-start | bytes 786440 | tf_op jit(solution)/shard_map/ppermute | solution.py:248
  105.7 3.1 %collective-permute-done.29 = bf16[64,2048]{1,0:T(8,128)(2,1)S(1)} collective-permute-done((bf16[64,2048]{1,0:T(8,128)(2,1)S(1)}, bf16[64,2048]{1,0:T(8,128)(2,1)S(1)}, u32[]{:S(2)}, u32[]{:S(2)}) %collective-permute-start.29) | collective-permute-done | bytes 262176 | tf_op jit(solution)/shard_map/ppermute | solution.py:248
  108.8 2.8 %collective-permute-done.31 = bf16[64,2048]{1,0:T(8,128)(2,1)S(1)} collective-permute-done((bf16[64,2048]{1,0:T(8,128)(2,1)S(1)}, bf16[64,2048]{1,0:T(8,128)(2,1)S(1)}, u32[]{:S(2)}, u32[]{:S(2)}) %collective-permute-start.31) | collective-permute-done | bytes 262176 | tf_op jit(solution)/shard_map/ppermute | solution.py:248
  111.6 0.2 add_convert_fusion.8
  111.8 0.8 pad_maximum_fusion
  (21 shorter events, 0.1 us)
Async XLA Ops:
  1.3 10.6 %collective-permute-start.2 = (bf16[128,2176]{1,0:T(8,128)(2,1)S(1)}, bf16[128,2176]{1,0:T(8,128)(2,1)S(1)}, u32[]{:S(2)}, u32[]{:S(2)}) collective-permute-start(bf16[128,2176]{1,0:T(8,128)(2,1)S(1)} %packed.1.near_ref), channel_id=1, source_target_pairs={{0,4},{5,1},{4,8},{9,5},{8,12},{13,9},{12,14},{15,13},{14,10},{11,... | collective-permute-start | bytes 1671176 | tf_op jit(solution)/shard_map/ppermute | solution.py:235
  11.9 7.6 %collective-permute-start.21 = (bf16[128,2176]{1,0:T(8,128)(2,1)S(1)}, bf16[128,2176]{1,0:T(8,128)(2,1)S(1)}, u32[]{:S(2)}, u32[]{:S(2)}) collective-permute-start(bf16[128,2176]{1,0:T(8,128)(2,1)S(1)} %collective-permute-done.2.near_ref), channel_id=1, source_target_pairs={{0,1},{1,0},{2,3},{3,2},{4,5},{5,4},{6,7},{7,6},{8,9},{9,8},{10,11... | collective-permute-start | bytes 1671176 | tf_op jit(solution)/shard_map/ppermute | solution.py:232
  11.9 0.7 copy-start
  17.4 9.6 %collective-permute-start.3 = (bf16[128,2176]{1,0:T(8,128)(2,1)S(1)}, bf16[128,2176]{1,0:T(8,128)(2,1)S(1)}, u32[]{:S(2)}, u32[]{:S(2)}) collective-permute-start(bf16[128,2176]{1,0:T(8,128)(2,1)S(1)} %collective-permute-done.2.near_ref), channel_id=1, source_target_pairs={{0,4},{5,1},{4,8},{9,5},{8,12},{13,9},{12,14},{15,13},{14,10},{11,... | collective-permute-start | bytes 1671176 | tf_op jit(solution)/shard_map/ppermute | solution.py:235
  22.9 6.2 %collective-permute-start.22 = (bf16[128,2048]{1,0:T(8,128)(2,1)S(1)}, bf16[128,2048]{1,0:T(8,128)(2,1)S(1)}, u32[]{:S(2)}, u32[]{:S(2)}) collective-permute-start(bf16[128,2048]{1,0:T(8,128)(2,1)S(1)} %get-tuple-element.46), channel_id=1, source_target_pairs={{0,1},{1,0},{2,3},{3,2},{4,5},{5,4},{6,7},{7,6},{8,9},{9,8},{10,11... | collective-permute-start | bytes 1572872 | tf_op jit(solution)/shard_map/ppermute | solution.py:237
  27.0 3.8 %collective-permute-start.19 = (bf16[128,2176]{1,0:T(8,128)(2,1)S(1)}, bf16[128,2176]{1,0:T(8,128)(2,1)S(1)}, u32[]{:S(2)}, u32[]{:S(2)}) collective-permute-start(bf16[128,2176]{1,0:T(8,128)(2,1)S(1)} %collective-permute-done.3.near_ref), channel_id=1, source_target_pairs={{0,1},{1,0},{2,3},{3,2},{4,5},{5,4},{6,7},{7,6},{8,9},{9,8},{10,11... | collective-permute-start | bytes 1671176 | tf_op jit(solution)/shard_map/ppermute | solution.py:232
  27.0 9.5 %collective-permute-start.4 = (bf16[128,2176]{1,0:T(8,128)(2,1)S(1)}, bf16[128,2176]{1,0:T(8,128)(2,1)S(1)}, u32[]{:S(2)}, u32[]{:S(2)}) collective-permute-start(bf16[128,2176]{1,0:T(8,128)(2,1)S(1)} %collective-permute-done.3.near_ref), channel_id=1, source_target_pairs={{0,4},{5,1},{4,8},{9,5},{8,12},{13,9},{12,14},{15,13},{14,10},{11,... | collective-permute-start | bytes 1671176 | tf_op jit(solution)/shard_map/ppermute | solution.py:235
  29.2 13.0 %collective-permute-start.23 = (bf16[128,2048]{1,0:T(8,128)(2,1)S(1)}, bf16[128,2048]{1,0:T(8,128)(2,1)S(1)}, u32[]{:S(2)}, u32[]{:S(2)}) collective-permute-start(bf16[128,2048]{1,0:T(8,128)(2,1)S(1)} %add_convert_fusion.4), channel_id=1, source_target_pairs={{0,4},{5,1},{4,8},{9,5},{8,12},{13,9},{12,14},{15,13},{14,10},{11,... | collective-permute-start | bytes 1572872 | tf_op jit(solution)/shard_map/ppermute | solution.py:248
  34.1 8.0 %collective-permute-start.20 = (bf16[128,2048]{1,0:T(8,128)(2,1)S(1)}, bf16[128,2048]{1,0:T(8,128)(2,1)S(1)}, u32[]{:S(2)}, u32[]{:S(2)}) collective-permute-start(bf16[128,2048]{1,0:T(8,128)(2,1)S(1)} %get-tuple-element.44), channel_id=1, source_target_pairs={{0,1},{1,0},{2,3},{3,2},{4,5},{5,4},{6,7},{7,6},{8,9},{9,8},{10,11... | collective-permute-start | bytes 1572872 | tf_op jit(solution)/shard_map/ppermute | solution.py:237
  36.5 8.0 %collective-permute-start.17 = (bf16[128,2176]{1,0:T(8,128)(2,1)S(1)}, bf16[128,2176]{1,0:T(8,128)(2,1)S(1)}, u32[]{:S(2)}, u32[]{:S(2)}) collective-permute-start(bf16[128,2176]{1,0:T(8,128)(2,1)S(1)} %collective-permute-done.4.near_ref), channel_id=1, source_target_pairs={{0,1},{1,0},{2,3},{3,2},{4,5},{5,4},{6,7},{7,6},{8,9},{9,8},{10,11... | collective-permute-start | bytes 1671176 | tf_op jit(solution)/shard_map/ppermute | solution.py:232
  36.5 11.6 %collective-permute-start.5 = (bf16[128,2176]{1,0:T(8,128)(2,1)S(1)}, bf16[128,2176]{1,0:T(8,128)(2,1)S(1)}, u32[]{:S(2)}, u32[]{:S(2)}) collective-permute-start(bf16[128,2176]{1,0:T(8,128)(2,1)S(1)} %collective-permute-done.4.near_ref), channel_id=1, source_target_pairs={{0,4},{5,1},{4,8},{9,5},{8,12},{13,9},{12,14},{15,13},{14,10},{11,... | collective-permute-start | bytes 1671176 | tf_op jit(solution)/shard_map/ppermute | solution.py:235
  42.3 11.4 %collective-permute-start.24 = (bf16[128,2048]{1,0:T(8,128)(2,1)S(1)}, bf16[128,2048]{1,0:T(8,128)(2,1)S(1)}, u32[]{:S(2)}, u32[]{:S(2)}) collective-permute-start(bf16[128,2048]{1,0:T(8,128)(2,1)S(1)} %add_convert_fusion.3), channel_id=1, source_target_pairs={{0,4},{5,1},{4,8},{9,5},{8,12},{13,9},{12,14},{15,13},{14,10},{11,... | collective-permute-start | bytes 1572872 | tf_op jit(solution)/shard_map/ppermute | solution.py:248
  47.8 5.9 %collective-permute-start.18 = (bf16[128,2048]{1,0:T(8,128)(2,1)S(1)}, bf16[128,2048]{1,0:T(8,128)(2,1)S(1)}, u32[]{:S(2)}, u32[]{:S(2)}) collective-permute-start(bf16[128,2048]{1,0:T(8,128)(2,1)S(1)} %get-tuple-element.42), channel_id=1, source_target_pairs={{0,1},{1,0},{2,3},{3,2},{4,5},{5,4},{6,7},{7,6},{8,9},{9,8},{10,11... | collective-permute-start | bytes 1572872 | tf_op jit(solution)/shard_map/ppermute | solution.py:237
  48.1 8.0 %collective-permute-start.15 = (bf16[128,2176]{1,0:T(8,128)(2,1)S(1)}, bf16[128,2176]{1,0:T(8,128)(2,1)S(1)}, u32[]{:S(2)}, u32[]{:S(2)}) collective-permute-start(bf16[128,2176]{1,0:T(8,128)(2,1)S(1)} %collective-permute-done.5.near_ref), channel_id=1, source_target_pairs={{0,1},{1,0},{2,3},{3,2},{4,5},{5,4},{6,7},{7,6},{8,9},{9,8},{10,11... | collective-permute-start | bytes 1671176 | tf_op jit(solution)/shard_map/ppermute | solution.py:232
  48.4 11.3 %collective-permute-start.6 = (bf16[128,2176]{1,0:T(8,128)(2,1)S(1)}, bf16[128,2176]{1,0:T(8,128)(2,1)S(1)}, u32[]{:S(2)}, u32[]{:S(2)}) collective-permute-start(bf16[128,2176]{1,0:T(8,128)(2,1)S(1)} %collective-permute-done.5.near_ref), channel_id=1, source_target_pairs={{0,4},{5,1},{4,8},{9,5},{8,12},{13,9},{12,14},{15,13},{14,10},{11,... | collective-permute-start | bytes 1671176 | tf_op jit(solution)/shard_map/ppermute | solution.py:235
  53.9 11.4 %collective-permute-start.25 = (bf16[128,2048]{1,0:T(8,128)(2,1)S(1)}, bf16[128,2048]{1,0:T(8,128)(2,1)S(1)}, u32[]{:S(2)}, u32[]{:S(2)}) collective-permute-start(bf16[128,2048]{1,0:T(8,128)(2,1)S(1)} %add_convert_fusion.2), channel_id=1, source_target_pairs={{0,4},{5,1},{4,8},{9,5},{8,12},{13,9},{12,14},{15,13},{14,10},{11,... | collective-permute-start | bytes 1572872 | tf_op jit(solution)/shard_map/ppermute | solution.py:248
  59.4 5.9 %collective-permute-start.16 = (bf16[128,2048]{1,0:T(8,128)(2,1)S(1)}, bf16[128,2048]{1,0:T(8,128)(2,1)S(1)}, u32[]{:S(2)}, u32[]{:S(2)}) collective-permute-start(bf16[128,2048]{1,0:T(8,128)(2,1)S(1)} %get-tuple-element.40), channel_id=1, source_target_pairs={{0,1},{1,0},{2,3},{3,2},{4,5},{5,4},{6,7},{7,6},{8,9},{9,8},{10,11... | collective-permute-start | bytes 1572872 | tf_op jit(solution)/shard_map/ppermute | solution.py:237
  59.7 11.6 %collective-permute-start.7 = (bf16[128,2176]{1,0:T(8,128)(2,1)S(1)}, bf16[128,2176]{1,0:T(8,128)(2,1)S(1)}, u32[]{:S(2)}, u32[]{:S(2)}) collective-permute-start(bf16[128,2176]{1,0:T(8,128)(2,1)S(1)} %collective-permute-done.6.near_ref), channel_id=1, source_target_pairs={{0,4},{5,1},{4,8},{9,5},{8,12},{13,9},{12,14},{15,13},{14,10},{11,... | collective-permute-start | bytes 1671176 | tf_op jit(solution)/shard_map/ppermute | solution.py:235
  61.8 11.6 %collective-permute-start.13 = (bf16[128,2176]{1,0:T(8,128)(2,1)S(1)}, bf16[128,2176]{1,0:T(8,128)(2,1)S(1)}, u32[]{:S(2)}, u32[]{:S(2)}) collective-permute-start(bf16[128,2176]{1,0:T(8,128)(2,1)S(1)} %collective-permute-done.6.near_ref), channel_id=1, source_target_pairs={{0,1},{1,0},{2,3},{3,2},{4,5},{5,4},{6,7},{7,6},{8,9},{9,8},{10,11... | collective-permute-start | bytes 1671176 | tf_op jit(solution)/shard_map/ppermute | solution.py:232
  65.5 17.4 %collective-permute-start.26 = (bf16[128,2048]{1,0:T(8,128)(2,1)S(1)}, bf16[128,2048]{1,0:T(8,128)(2,1)S(1)}, u32[]{:S(2)}, u32[]{:S(2)}) collective-permute-start(bf16[128,2048]{1,0:T(8,128)(2,1)S(1)} %add_convert_fusion.1), channel_id=1, source_target_pairs={{0,4},{5,1},{4,8},{9,5},{8,12},{13,9},{12,14},{15,13},{14,10},{11,... | collective-permute-start | bytes 1572872 | tf_op jit(solution)/shard_map/ppermute | solution.py:248
  71.3 11.6 %collective-permute-start.8 = (bf16[128,2176]{1,0:T(8,128)(2,1)S(1)}, bf16[128,2176]{1,0:T(8,128)(2,1)S(1)}, u32[]{:S(2)}, u32[]{:S(2)}) collective-permute-start(bf16[128,2176]{1,0:T(8,128)(2,1)S(1)} %collective-permute-done.7.near_ref), channel_id=1, source_target_pairs={{0,4},{5,1},{4,8},{9,5},{8,12},{13,9},{12,14},{15,13},{14,10},{11,... | collective-permute-start | bytes 1671176 | tf_op jit(solution)/shard_map/ppermute | solution.py:235
  76.7 6.2 %collective-permute-start.14 = (bf16[128,2048]{1,0:T(8,128)(2,1)S(1)}, bf16[128,2048]{1,0:T(8,128)(2,1)S(1)}, u32[]{:S(2)}, u32[]{:S(2)}) collective-permute-start(bf16[128,2048]{1,0:T(8,128)(2,1)S(1)} %get-tuple-element.38), channel_id=1, source_target_pairs={{0,1},{1,0},{2,3},{3,2},{4,5},{5,4},{6,7},{7,6},{8,9},{9,8},{10,11... | collective-permute-start | bytes 1572872 | tf_op jit(solution)/shard_map/ppermute | solution.py:237
  76.8 8.4 %collective-permute-start.11 = (bf16[128,2176]{1,0:T(8,128)(2,1)S(1)}, bf16[128,2176]{1,0:T(8,128)(2,1)S(1)}, u32[]{:S(2)}, u32[]{:S(2)}) collective-permute-start(bf16[128,2176]{1,0:T(8,128)(2,1)S(1)} %collective-permute-done.7.near_ref), channel_id=1, source_target_pairs={{0,1},{1,0},{2,3},{3,2},{4,5},{5,4},{6,7},{7,6},{8,9},{9,8},{10,11... | collective-permute-start | bytes 1671176 | tf_op jit(solution)/shard_map/ppermute | solution.py:232
  82.9 6.2 %collective-permute-start.9 = (bf16[128,2176]{1,0:T(8,128)(2,1)S(1)}, bf16[128,2176]{1,0:T(8,128)(2,1)S(1)}, u32[]{:S(2)}, u32[]{:S(2)}) collective-permute-start(bf16[128,2176]{1,0:T(8,128)(2,1)S(1)} %collective-permute-done.8.near_ref), channel_id=1, source_target_pairs={{0,1},{1,0},{2,3},{3,2},{4,5},{5,4},{6,7},{7,6},{8,9},{9,8},{10,11... | collective-permute-start | bytes 1671176 | tf_op jit(solution)/shard_map/ppermute | solution.py:232
  83.1 9.6 %collective-permute-start.27 = (bf16[128,2048]{1,0:T(8,128)(2,1)S(1)}, bf16[128,2048]{1,0:T(8,128)(2,1)S(1)}, u32[]{:S(2)}, u32[]{:S(2)}) collective-permute-start(bf16[128,2048]{1,0:T(8,128)(2,1)S(1)} %add_convert_fusion), channel_id=1, source_target_pairs={{0,4},{5,1},{4,8},{9,5},{8,12},{13,9},{12,14},{15,13},{14,10},{11,... | collective-permute-start | bytes 1572872 | tf_op jit(solution)/shard_map/ppermute | solution.py:248
  88.5 4.2 %collective-permute-start.12 = (bf16[128,2048]{1,0:T(8,128)(2,1)S(1)}, bf16[128,2048]{1,0:T(8,128)(2,1)S(1)}, u32[]{:S(2)}, u32[]{:S(2)}) collective-permute-start(bf16[128,2048]{1,0:T(8,128)(2,1)S(1)} %get-tuple-element.36), channel_id=1, source_target_pairs={{0,1},{1,0},{2,3},{3,2},{4,5},{5,4},{6,7},{7,6},{8,9},{9,8},{10,11... | collective-permute-start | bytes 1572872 | tf_op jit(solution)/shard_map/ppermute | solution.py:237
  88.8 7.4 %collective-permute-start = (bf16[128,2176]{1,0:T(8,128)(2,1)S(1)}, bf16[128,2176]{1,0:T(8,128)(2,1)S(1)}, u32[]{:S(2)}, u32[]{:S(2)}) collective-permute-start(bf16[128,2176]{1,0:T(8,128)(2,1)S(1)} %packed.1.near_ref), channel_id=1, source_target_pairs={{0,1},{1,0},{2,3},{3,2},{4,5},{5,4},{6,7},{7,6},{8,9},{9,8},{10,11... | collective-permute-start | bytes 1671176 | tf_op jit(solution)/shard_map/ppermute | solution.py:232
  92.4 9.7 %collective-permute-start.10 = (bf16[128,2048]{1,0:T(8,128)(2,1)S(1)}, bf16[128,2048]{1,0:T(8,128)(2,1)S(1)}, u32[]{:S(2)}, u32[]{:S(2)}) collective-permute-start(bf16[128,2048]{1,0:T(8,128)(2,1)S(1)} %get-tuple-element.34), channel_id=1, source_target_pairs={{0,1},{1,0},{2,3},{3,2},{4,5},{5,4},{6,7},{7,6},{8,9},{9,8},{10,11... | collective-permute-start | bytes 1572872 | tf_op jit(solution)/shard_map/ppermute | solution.py:237
  92.9 6.7 %collective-permute-start.28 = (bf16[64,2048]{1,0:T(8,128)(2,1)S(1)}, bf16[64,2048]{1,0:T(8,128)(2,1)S(1)}, u32[]{:S(2)}, u32[]{:S(2)}) collective-permute-start(bf16[64,2048]{1,0:T(8,128)(2,1)S(1)} %get-tuple-element.47), channel_id=1, source_target_pairs={{0,4},{5,1},{4,8},{9,5},{8,12},{13,9},{12,14},{15,13},{14,10},{11,... | collective-permute-start | bytes 786440 | tf_op jit(solution)/shard_map/ppermute | solution.py:248
  94.6 7.5 %collective-permute-start.30 = (bf16[64,2048]{1,0:T(8,128)(2,1)S(1)}, bf16[64,2048]{1,0:T(8,128)(2,1)S(1)}, u32[]{:S(2)}, u32[]{:S(2)}) collective-permute-start(bf16[64,2048]{1,0:T(8,128)(2,1)S(1)} %get-tuple-element.48), channel_id=1, source_target_pairs={{0,4},{5,1},{4,8},{9,5},{8,12},{13,9},{12,14},{15,13},{14,10},{11,... | collective-permute-start | bytes 786440 | tf_op jit(solution)/shard_map/ppermute | solution.py:248
  99.5 6.1 %collective-permute-start.1 = (bf16[128,2048]{1,0:T(8,128)(2,1)S(1)}, bf16[128,2048]{1,0:T(8,128)(2,1)S(1)}, u32[]{:S(2)}, u32[]{:S(2)}) collective-permute-start(bf16[128,2048]{1,0:T(8,128)(2,1)S(1)} %get-tuple-element.32), channel_id=1, source_target_pairs={{0,1},{1,0},{2,3},{3,2},{4,5},{5,4},{6,7},{7,6},{8,9},{9,8},{10,11... | collective-permute-start | bytes 1572872 | tf_op jit(solution)/shard_map/ppermute | solution.py:237
  102.3 6.4 %collective-permute-start.29 = (bf16[64,2048]{1,0:T(8,128)(2,1)S(1)}, bf16[64,2048]{1,0:T(8,128)(2,1)S(1)}, u32[]{:S(2)}, u32[]{:S(2)}) collective-permute-start(bf16[64,2048]{1,0:T(8,128)(2,1)S(1)} %get-tuple-element.51), channel_id=1, source_target_pairs={{0,4},{5,1},{4,8},{9,5},{8,12},{13,9},{12,14},{15,13},{14,10},{11,... | collective-permute-start | bytes 786440 | tf_op jit(solution)/shard_map/ppermute | solution.py:248
  104.1 7.5 %collective-permute-start.31 = (bf16[64,2048]{1,0:T(8,128)(2,1)S(1)}, bf16[64,2048]{1,0:T(8,128)(2,1)S(1)}, u32[]{:S(2)}, u32[]{:S(2)}) collective-permute-start(bf16[64,2048]{1,0:T(8,128)(2,1)S(1)} %get-tuple-element.52), channel_id=1, source_target_pairs={{0,4},{5,1},{4,8},{9,5},{8,12},{13,9},{12,14},{15,13},{14,10},{11,... | collective-permute-start | bytes 786440 | tf_op jit(solution)/shard_map/ppermute | solution.py:248

commit v4 on v3

--- a/solution.py
+++ b/solution.py
@@ -229,30 +229,26 @@
 
     parts = []
     for step in range(chips):
-        other = lax.ppermute(block, "tok", swap)
         here = block
+        other = lax.ppermute(here, "tok", swap)
         if step < chips - 1:
-            block = lax.ppermute(block, "tok", ring)
+            block = lax.ppermute(here, "tok", ring)
         part, lent = visit(mine, here, other, experts, *blocks)
         parts.append((part, lax.ppermute(lent, "tok", swap)))
 
-    total = None
-    for step in range(1, chips):
-        part, lent = parts[step]
-        cuts = (slice(None),) if step < chips - 2 else (slice(0, half), slice(half, None))
-        if total is not None and len(total) < len(cuts):
-            total = [total[0][cut] for cut in cuts]
-        sums = [part[cut] + lent[cut].astype(jnp.float32) for cut in cuts]
-        if total is not None:
-            sums = [x + y.astype(jnp.float32) for x, y in zip(sums, total)]
-        total = [lax.ppermute(x.astype(jnp.bfloat16), "tok", ring) for x in sums]
-    part, lent = parts[0]
-    return jnp.concatenate(
-        [
-            (part[cut] + lent[cut].astype(jnp.float32) + x.astype(jnp.float32)).astype(jnp.bfloat16)
-            for cut, x in zip((slice(0, half), slice(half, None)), total)
-        ]
-    )
+    def summed(step, cut, arrived):
+        part, lent = (x[cut].astype(jnp.float32) for x in parts[step])
+        return (part + lent + arrived.astype(jnp.float32)).astype(jnp.bfloat16)
+
+    total = jnp.zeros((), jnp.bfloat16)
+    for step in range(1, chips - 2):
+        total = lax.ppermute(summed(step, slice(None), total), "tok", ring)
+    halves = {"a": slice(0, half), "b": slice(half, None)}
+    totals = {name: total[cut] for name, cut in halves.items()}
+    for step in range(chips - 2, chips):
+        for name, cut in halves.items():
+            totals[name] = lax.ppermute(summed(step, cut, totals[name]), "tok", ring)
+    return jnp.concatenate([summed(0, cut, totals[name]) for name, cut in halves.items()])
 
 
 def solution(mesh):
@@ -268,7 +264,6 @@
             out_specs=row,
             check_vma=False,
         )
-
 
     def step(tokens, norm_gain, expert_ids, gate_weights, owner_map, *blocks):
         tok_rows = tokens.shape[0] // mesh.size

time: 113 us -> 113 us (level)
  no operation moved by 1% of the time
where the time goes in v4:
time: 113 us
  waiting for transfers between devices  42.3 us (37%)
  starting transfers between devices  34.3 us (30%)
  Pallas kernels  32.7 us (29%)
  other arithmetic  2.3 us (2%)
    pallas_call x8, Pallas kernels, visit(): pl.pallas_call(functools.partial(visit_kernel, experts), out_shape=(jax.S...  26.6 us
    ppermute x7, waiting for transfers between devices, circulated(): block = lax.ppermute(here, 'tok', ring)  23.3 us
    ppermute x7, starting transfers between devices, circulated(): block = lax.ppermute(here, 'tok', ring)  15.3 us
    ppermute x5, waiting for transfers between devices, circulated(): total = lax.ppermute(summed(step, slice(None), total), 'tok', ring)  10.6 us
    ppermute x5, starting transfers between devices, circulated(): total = lax.ppermute(summed(step, slice(None), total), 'tok', ring)  10.1 us
    ppermute x4, waiting for transfers between devices, circulated(): totals[name] = lax.ppermute(summed(step, cut, totals[name]), 'tok', ring)  8.38 us
    ppermute x4, starting transfers between devices, circulated(): totals[name] = lax.ppermute(summed(step, cut, totals[name]), 'tok', ring)  6.66 us
    pallas_call x1, Pallas kernels, loaded(): pl.pallas_call(loaded_kernel, out_shape=(jax.ShapeDtypeStruct((1,), jnp.i...  4.82 us
  transfers between devices with their start and end apart: 32, of which 13 were waited for; matrix products, arithmetic and copies ran while one was open for 1% of the time, Pallas kernels for 28%

profile of v4, /device:TPU:0, one launch (start us, length us, event | category | flops | bytes accessed | tf_op | source)
XLA Modules:
  0.0 112.6 jit_solution(12790546601732371630)
XLA Ops:
  0.0 1.3 %packed.1.near_ref = bf16[128,2176]{1,0:T(8,128)(2,1)S(1)} custom-call(bf16[128,2048]{1,0:T(8,128)(2,1)} %tokens_hbm.1, f32[1,2048]{1,0:T(1,128)} %bitcast.3, s32[8,128]{1,0:T(8,128)} %bitcast.4, f32[8,128]{1,0:T(8,128)} %bitcast.5), custom_call_target="tpu_custom_call" | custom-call | tf_op jit(solution)/shard_map/packed/pallas_call | solution.py:109
  1.3 3.1 %collective-permute-start.2 = (bf16[128,2176]{1,0:T(8,128)(2,1)S(1)}, bf16[128,2176]{1,0:T(8,128)(2,1)S(1)}, u32[]{:S(2)}, u32[]{:S(2)}) collective-permute-start(bf16[128,2176]{1,0:T(8,128)(2,1)S(1)} %packed.1.near_ref), channel_id=1, source_target_pairs={{0,4},{5,1},{4,8},{9,5},{8,12},{13,9},{12,14},{15,13},{14,10},{11,... | collective-permute-start | bytes 1671176 | tf_op jit(solution)/shard_map/ppermute | solution.py:235
  4.4 7.5 %collective-permute-done.2.near_ref = bf16[128,2176]{1,0:T(8,128)(2,1)S(1)} collective-permute-done((bf16[128,2176]{1,0:T(8,128)(2,1)S(1)}, bf16[128,2176]{1,0:T(8,128)(2,1)S(1)}, u32[]{:S(2)}, u32[]{:S(2)}) %collective-permute-start.2) | collective-permute-done | bytes 557088 | tf_op jit(solution)/shard_map/ppermute | solution.py:235
  11.9 0.0 collective-permute-start.21
  11.9 0.7 copy-done
  12.6 4.8 %loaded.1 = (s32[1]{0:T(128)}, bf16[1,2,2048,768]{3,2,1,0:T(8,128)(2,1)S(1)}, bf16[1,2,768]{2,1,0:T(2,128)(2,1)S(1)}, bf16[1,768,2048]{2,1,0:T(8,128)(2,1)S(1)}, bf16[1,2048]{1,0:T(2,128)(2,1)S(1)}) custom-call(s32[16]{0:T(128)S(1)} %copy-done, bf16[1,2,2048,768]{3,2,1,0:T(8,128)(2,1)} %in_hbm.1, bf16[1,2,768]{2,1,0:T(2,128)(2,1)} %in_scale_hbm.1, ...), custom_call_target="tpu_custom_call" | custom-call | bytes 9437184 | tf_op jit(solution)/shard_map/loaded/pallas_call | solution.py:148
  17.4 2.1 %collective-permute-start.3 = (bf16[128,2176]{1,0:T(8,128)(2,1)S(1)}, bf16[128,2176]{1,0:T(8,128)(2,1)S(1)}, u32[]{:S(2)}, u32[]{:S(2)}) collective-permute-start(bf16[128,2176]{1,0:T(8,128)(2,1)S(1)} %collective-permute-done.2.near_ref), channel_id=1, source_target_pairs={{0,4},{5,1},{4,8},{9,5},{8,12},{13,9},{12,14},{15,13},{14,10},{11,... | collective-permute-start | bytes 1671176 | tf_op jit(solution)/shard_map/ppermute | solution.py:235
  19.5 0.0 collective-permute-done.21.far_ref
  19.5 3.3 %visit.15 = (f32[128,2048]{1,0:T(8,128)S(1)}, bf16[128,2048]{1,0:T(8,128)(2,1)S(1)}) custom-call(s32[1]{0:T(128)} %get-tuple-element.26.mine_ref, bf16[128,2176]{1,0:T(8,128)(2,1)S(1)} %collective-permute-done.2.near_ref, bf16[128,2176]{1,0:T(8,128)(2,1)S(1)} %collective-permute-done.21.far_ref, bf16[1,2,2048,768]{3,2,1,0:T(8,128)(2,1)S(1)} %get-tuple-element.27.in_ref, ...), custom_call_target="tpu_custom_call" | custom-call | flops 2415919104 | bytes 1572864 | tf_op jit(solution)/shard_map/visit/pallas_call | solution.py:198
  22.9 0.2 collective-permute-start.22
  23.1 3.9 %collective-permute-done.3.near_ref = bf16[128,2176]{1,0:T(8,128)(2,1)S(1)} collective-permute-done((bf16[128,2176]{1,0:T(8,128)(2,1)S(1)}, bf16[128,2176]{1,0:T(8,128)(2,1)S(1)}, u32[]{:S(2)}, u32[]{:S(2)}) %collective-permute-start.3) | collective-permute-done | bytes 557088 | tf_op jit(solution)/shard_map/ppermute | solution.py:235
  27.0 2.1 %collective-permute-start.4 = (bf16[128,2176]{1,0:T(8,128)(2,1)S(1)}, bf16[128,2176]{1,0:T(8,128)(2,1)S(1)}, u32[]{:S(2)}, u32[]{:S(2)}) collective-permute-start(bf16[128,2176]{1,0:T(8,128)(2,1)S(1)} %collective-permute-done.3.near_ref), channel_id=1, source_target_pairs={{0,4},{5,1},{4,8},{9,5},{8,12},{13,9},{12,14},{15,13},{14,10},{11,... | collective-permute-start | bytes 1671176 | tf_op jit(solution)/shard_map/ppermute | solution.py:235
  29.1 0.0 collective-permute-done.22
  29.1 0.1 add_convert_fusion.4
  29.2 1.6 %collective-permute-start.23 = (bf16[128,2048]{1,0:T(8,128)(2,1)S(1)}, bf16[128,2048]{1,0:T(8,128)(2,1)S(1)}, u32[]{:S(2)}, u32[]{:S(2)}) collective-permute-start(bf16[128,2048]{1,0:T(8,128)(2,1)S(1)} %add_convert_fusion.4), channel_id=1, source_target_pairs={{0,4},{5,1},{4,8},{9,5},{8,12},{13,9},{12,14},{15,13},{14,10},{11,... | collective-permute-start | bytes 1572872 | tf_op jit(solution)/shard_map/ppermute | solution.py:245
  30.8 3.3 %visit.14 = (f32[128,2048]{1,0:T(8,128)S(1)}, bf16[128,2048]{1,0:T(8,128)(2,1)S(1)}) custom-call(s32[1]{0:T(128)} %get-tuple-element.26.mine_ref, bf16[128,2176]{1,0:T(8,128)(2,1)S(1)} %collective-permute-done.3.near_ref, bf16[128,2176]{1,0:T(8,128)(2,1)S(1)} %collective-permute-done.19.far_ref, bf16[1,2,2048,768]{3,2,1,0:T(8,128)(2,1)S(1)} %get-tuple-element.27.in_ref, ...), custom_call_target="tpu_custom_call" | custom-call | flops 2415919104 | bytes 1572864 | tf_op jit(solution)/shard_map/visit/pallas_call | solution.py:198
  34.1 0.1 collective-permute-start.20
  34.2 2.3 %collective-permute-done.4.near_ref = bf16[128,2176]{1,0:T(8,128)(2,1)S(1)} collective-permute-done((bf16[128,2176]{1,0:T(8,128)(2,1)S(1)}, bf16[128,2176]{1,0:T(8,128)(2,1)S(1)}, u32[]{:S(2)}, u32[]{:S(2)}) %collective-permute-start.4) | collective-permute-done | bytes 557088 | tf_op jit(solution)/shard_map/ppermute | solution.py:235
  36.5 0.0 collective-permute-start.17
  36.5 2.1 %collective-permute-start.5 = (bf16[128,2176]{1,0:T(8,128)(2,1)S(1)}, bf16[128,2176]{1,0:T(8,128)(2,1)S(1)}, u32[]{:S(2)}, u32[]{:S(2)}) collective-permute-start(bf16[128,2176]{1,0:T(8,128)(2,1)S(1)} %collective-permute-done.4.near_ref), channel_id=1, source_target_pairs={{0,4},{5,1},{4,8},{9,5},{8,12},{13,9},{12,14},{15,13},{14,10},{11,... | collective-permute-start | bytes 1671176 | tf_op jit(solution)/shard_map/ppermute | solution.py:235
  38.6 3.5 %collective-permute-done.23 = bf16[128,2048]{1,0:T(8,128)(2,1)S(1)} collective-permute-done((bf16[128,2048]{1,0:T(8,128)(2,1)S(1)}, bf16[128,2048]{1,0:T(8,128)(2,1)S(1)}, u32[]{:S(2)}, u32[]{:S(2)}) %collective-permute-start.23) | collective-permute-done | bytes 524320 | tf_op jit(solution)/shard_map/ppermute | solution.py:245
  42.1 0.2 add_convert_fusion.3
  42.3 2.1 %collective-permute-start.24 = (bf16[128,2048]{1,0:T(8,128)(2,1)S(1)}, bf16[128,2048]{1,0:T(8,128)(2,1)S(1)}, u32[]{:S(2)}, u32[]{:S(2)}) collective-permute-start(bf16[128,2048]{1,0:T(8,128)(2,1)S(1)} %add_convert_fusion.3), channel_id=1, source_target_pairs={{0,4},{5,1},{4,8},{9,5},{8,12},{13,9},{12,14},{15,13},{14,10},{11,... | collective-permute-start | bytes 1572872 | tf_op jit(solution)/shard_map/ppermute | solution.py:245
  44.5 3.3 %visit.13 = (f32[128,2048]{1,0:T(8,128)S(1)}, bf16[128,2048]{1,0:T(8,128)(2,1)S(1)}) custom-call(s32[1]{0:T(128)} %get-tuple-element.26.mine_ref, bf16[128,2176]{1,0:T(8,128)(2,1)S(1)} %collective-permute-done.4.near_ref, bf16[128,2176]{1,0:T(8,128)(2,1)S(1)} %collective-permute-done.17.far_ref, bf16[1,2,2048,768]{3,2,1,0:T(8,128)(2,1)S(1)} %get-tuple-element.27.in_ref, ...), custom_call_target="tpu_custom_call" | custom-call | flops 2415919104 | bytes 1572864 | tf_op jit(solution)/shard_map/visit/pallas_call | solution.py:198
  47.8 0.1 collective-permute-start.18
  47.9 0.2 collective-permute-done.5.near_ref
  48.1 0.3 collective-permute-start.15
  48.4 1.8 %collective-permute-start.6 = (bf16[128,2176]{1,0:T(8,128)(2,1)S(1)}, bf16[128,2176]{1,0:T(8,128)(2,1)S(1)}, u32[]{:S(2)}, u32[]{:S(2)}) collective-permute-start(bf16[128,2176]{1,0:T(8,128)(2,1)S(1)} %collective-permute-done.5.near_ref), channel_id=1, source_target_pairs={{0,4},{5,1},{4,8},{9,5},{8,12},{13,9},{12,14},{15,13},{14,10},{11,... | collective-permute-start | bytes 1671176 | tf_op jit(solution)/shard_map/ppermute | solution.py:235
  50.2 3.5 %collective-permute-done.24 = bf16[128,2048]{1,0:T(8,128)(2,1)S(1)} collective-permute-done((bf16[128,2048]{1,0:T(8,128)(2,1)S(1)}, bf16[128,2048]{1,0:T(8,128)(2,1)S(1)}, u32[]{:S(2)}, u32[]{:S(2)}) %collective-permute-start.24) | collective-permute-done | bytes 524320 | tf_op jit(solution)/shard_map/ppermute | solution.py:245
  53.7 0.2 add_convert_fusion.2
  53.9 2.1 %collective-permute-start.25 = (bf16[128,2048]{1,0:T(8,128)(2,1)S(1)}, bf16[128,2048]{1,0:T(8,128)(2,1)S(1)}, u32[]{:S(2)}, u32[]{:S(2)}) collective-permute-start(bf16[128,2048]{1,0:T(8,128)(2,1)S(1)} %add_convert_fusion.2), channel_id=1, source_target_pairs={{0,4},{5,1},{4,8},{9,5},{8,12},{13,9},{12,14},{15,13},{14,10},{11,... | collective-permute-start | bytes 1572872 | tf_op jit(solution)/shard_map/ppermute | solution.py:245
  56.0 3.3 %visit.12 = (f32[128,2048]{1,0:T(8,128)S(1)}, bf16[128,2048]{1,0:T(8,128)(2,1)S(1)}) custom-call(s32[1]{0:T(128)} %get-tuple-element.26.mine_ref, bf16[128,2176]{1,0:T(8,128)(2,1)S(1)} %collective-permute-done.5.near_ref, bf16[128,2176]{1,0:T(8,128)(2,1)S(1)} %collective-permute-done.15.far_ref, bf16[1,2,2048,768]{3,2,1,0:T(8,128)(2,1)S(1)} %get-tuple-element.27.in_ref, ...), custom_call_target="tpu_custom_call" | custom-call | flops 2415919104 | bytes 1572864 | tf_op jit(solution)/shard_map/visit/pallas_call | solution.py:198
  59.4 0.1 collective-permute-start.16
  59.5 0.2 collective-permute-done.6.near_ref
  59.7 2.1 %collective-permute-start.7 = (bf16[128,2176]{1,0:T(8,128)(2,1)S(1)}, bf16[128,2176]{1,0:T(8,128)(2,1)S(1)}, u32[]{:S(2)}, u32[]{:S(2)}) collective-permute-start(bf16[128,2176]{1,0:T(8,128)(2,1)S(1)} %collective-permute-done.6.near_ref), channel_id=1, source_target_pairs={{0,4},{5,1},{4,8},{9,5},{8,12},{13,9},{12,14},{15,13},{14,10},{11,... | collective-permute-start | bytes 1671176 | tf_op jit(solution)/shard_map/ppermute | solution.py:235
  61.8 3.5 %collective-permute-done.25 = bf16[128,2048]{1,0:T(8,128)(2,1)S(1)} collective-permute-done((bf16[128,2048]{1,0:T(8,128)(2,1)S(1)}, bf16[128,2048]{1,0:T(8,128)(2,1)S(1)}, u32[]{:S(2)}, u32[]{:S(2)}) %collective-permute-start.25) | collective-permute-done | bytes 524320 | tf_op jit(solution)/shard_map/ppermute | solution.py:245
  65.3 0.2 add_convert_fusion.1
  65.5 2.1 %collective-permute-start.26 = (bf16[128,2048]{1,0:T(8,128)(2,1)S(1)}, bf16[128,2048]{1,0:T(8,128)(2,1)S(1)}, u32[]{:S(2)}, u32[]{:S(2)}) collective-permute-start(bf16[128,2048]{1,0:T(8,128)(2,1)S(1)} %add_convert_fusion.1), channel_id=1, source_target_pairs={{0,4},{5,1},{4,8},{9,5},{8,12},{13,9},{12,14},{15,13},{14,10},{11,... | collective-permute-start | bytes 1572872 | tf_op jit(solution)/shard_map/ppermute | solution.py:245
  67.6 3.6 %collective-permute-done.7.near_ref = bf16[128,2176]{1,0:T(8,128)(2,1)S(1)} collective-permute-done((bf16[128,2176]{1,0:T(8,128)(2,1)S(1)}, bf16[128,2176]{1,0:T(8,128)(2,1)S(1)}, u32[]{:S(2)}, u32[]{:S(2)}) %collective-permute-start.7) | collective-permute-done | bytes 557088 | tf_op jit(solution)/shard_map/ppermute | solution.py:235
  71.3 2.1 %collective-permute-start.8 = (bf16[128,2176]{1,0:T(8,128)(2,1)S(1)}, bf16[128,2176]{1,0:T(8,128)(2,1)S(1)}, u32[]{:S(2)}, u32[]{:S(2)}) collective-permute-start(bf16[128,2176]{1,0:T(8,128)(2,1)S(1)} %collective-permute-done.7.near_ref), channel_id=1, source_target_pairs={{0,4},{5,1},{4,8},{9,5},{8,12},{13,9},{12,14},{15,13},{14,10},{11,... | collective-permute-start | bytes 1671176 | tf_op jit(solution)/shard_map/ppermute | solution.py:235
  73.3 3.3 %visit.11 = (f32[128,2048]{1,0:T(8,128)S(1)}, bf16[128,2048]{1,0:T(8,128)(2,1)S(1)}) custom-call(s32[1]{0:T(128)} %get-tuple-element.26.mine_ref, bf16[128,2176]{1,0:T(8,128)(2,1)S(1)} %collective-permute-done.6.near_ref, bf16[128,2176]{1,0:T(8,128)(2,1)S(1)} %collective-permute-done.13.far_ref, bf16[1,2,2048,768]{3,2,1,0:T(8,128)(2,1)S(1)} %get-tuple-element.27.in_ref, ...), custom_call_target="tpu_custom_call" | custom-call | flops 2415919104 | bytes 1572864 | tf_op jit(solution)/shard_map/visit/pallas_call | solution.py:198
  76.7 0.1 collective-permute-start.14
  76.8 0.5 collective-permute-start.11
  77.3 5.6 %collective-permute-done.8.near_ref = bf16[128,2176]{1,0:T(8,128)(2,1)S(1)} collective-permute-done((bf16[128,2176]{1,0:T(8,128)(2,1)S(1)}, bf16[128,2176]{1,0:T(8,128)(2,1)S(1)}, u32[]{:S(2)}, u32[]{:S(2)}) %collective-permute-start.8) | collective-permute-done | bytes 557088 | tf_op jit(solution)/shard_map/ppermute | solution.py:235
  82.9 0.2 add_convert_fusion
  83.1 2.1 %collective-permute-start.27 = (bf16[128,2048]{1,0:T(8,128)(2,1)S(1)}, bf16[128,2048]{1,0:T(8,128)(2,1)S(1)}, u32[]{:S(2)}, u32[]{:S(2)}) collective-permute-start(bf16[128,2048]{1,0:T(8,128)(2,1)S(1)} %add_convert_fusion), channel_id=1, source_target_pairs={{0,4},{5,1},{4,8},{9,5},{8,12},{13,9},{12,14},{15,13},{14,10},{11,... | collective-permute-start | bytes 1572872 | tf_op jit(solution)/shard_map/ppermute | solution.py:245
  85.2 3.3 %visit.10 = (f32[128,2048]{1,0:T(8,128)S(1)}, bf16[128,2048]{1,0:T(8,128)(2,1)S(1)}) custom-call(s32[1]{0:T(128)} %get-tuple-element.26.mine_ref, bf16[128,2176]{1,0:T(8,128)(2,1)S(1)} %collective-permute-done.7.near_ref, bf16[128,2176]{1,0:T(8,128)(2,1)S(1)} %collective-permute-done.11.far_ref, bf16[1,2,2048,768]{3,2,1,0:T(8,128)(2,1)S(1)} %get-tuple-element.27.in_ref, ...), custom_call_target="tpu_custom_call" | custom-call | flops 2415919104 | bytes 1572864 | tf_op jit(solution)/shard_map/visit/pallas_call | solution.py:198
  88.5 0.2 collective-permute-start.12
  88.8 0.3 collective-permute-start
  89.1 3.3 %visit.9 = (f32[128,2048]{1,0:T(8,128)S(1)}, bf16[128,2048]{1,0:T(8,128)(2,1)S(1)}) custom-call(s32[1]{0:T(128)} %get-tuple-element.26.mine_ref, bf16[128,2176]{1,0:T(8,128)(2,1)S(1)} %collective-permute-done.8.near_ref, bf16[128,2176]{1,0:T(8,128)(2,1)S(1)} %collective-permute-done.9.far_ref, bf16[1,2,2048,768]{3,2,1,0:T(8,128)(2,1)S(1)} %get-tuple-element.27.in_ref, ...), custom_call_target="tpu_custom_call" | custom-call | flops 2415919104 | bytes 1572864 | tf_op jit(solution)/shard_map/visit/pallas_call | solution.py:198
  92.4 0.2 collective-permute-start.10
  92.7 0.2 add_convert_fusion.10
  92.9 1.8 %collective-permute-start.28 = (bf16[64,2048]{1,0:T(8,128)(2,1)S(1)}, bf16[64,2048]{1,0:T(8,128)(2,1)S(1)}, u32[]{:S(2)}, u32[]{:S(2)}) collective-permute-start(bf16[64,2048]{1,0:T(8,128)(2,1)S(1)} %get-tuple-element.47), channel_id=1, source_target_pairs={{0,4},{5,1},{4,8},{9,5},{8,12},{13,9},{12,14},{15,13},{14,10},{11,... | collective-permute-start | bytes 786440 | tf_op jit(solution)/shard_map/ppermute | solution.py:250
  94.6 1.6 %collective-permute-start.30 = (bf16[64,2048]{1,0:T(8,128)(2,1)S(1)}, bf16[64,2048]{1,0:T(8,128)(2,1)S(1)}, u32[]{:S(2)}, u32[]{:S(2)}) collective-permute-start(bf16[64,2048]{1,0:T(8,128)(2,1)S(1)} %get-tuple-element.48), channel_id=1, source_target_pairs={{0,4},{5,1},{4,8},{9,5},{8,12},{13,9},{12,14},{15,13},{14,10},{11,... | collective-permute-start | bytes 786440 | tf_op jit(solution)/shard_map/ppermute | solution.py:250
  96.2 3.3 %visit.8 = (f32[128,2048]{1,0:T(8,128)S(1)}, bf16[128,2048]{1,0:T(8,128)(2,1)S(1)}) custom-call(s32[1]{0:T(128)} %get-tuple-element.26.mine_ref, bf16[128,2176]{1,0:T(8,128)(2,1)S(1)} %packed.1.near_ref, bf16[128,2176]{1,0:T(8,128)(2,1)S(1)} %collective-permute-done.far_ref, bf16[1,2,2048,768]{3,2,1,0:T(8,128)(2,1)S(1)} %get-tuple-element.27.in_ref, ...), custom_call_target="tpu_custom_call" | custom-call | flops 2415919104 | bytes 1572864 | tf_op jit(solution)/shard_map/visit/pallas_call | solution.py:198
  99.5 0.1 collective-permute-start.1
  99.6 2.5 %collective-permute-done.30 = bf16[64,2048]{1,0:T(8,128)(2,1)S(1)} collective-permute-done((bf16[64,2048]{1,0:T(8,128)(2,1)S(1)}, bf16[64,2048]{1,0:T(8,128)(2,1)S(1)}, u32[]{:S(2)}, u32[]{:S(2)}) %collective-permute-start.30) | collective-permute-done | bytes 262176 | tf_op jit(solution)/shard_map/ppermute | solution.py:250
  102.1 0.2 add_convert_fusion.9
  102.3 1.8 %collective-permute-start.29 = (bf16[64,2048]{1,0:T(8,128)(2,1)S(1)}, bf16[64,2048]{1,0:T(8,128)(2,1)S(1)}, u32[]{:S(2)}, u32[]{:S(2)}) collective-permute-start(bf16[64,2048]{1,0:T(8,128)(2,1)S(1)} %get-tuple-element.51), channel_id=1, source_target_pairs={{0,4},{5,1},{4,8},{9,5},{8,12},{13,9},{12,14},{15,13},{14,10},{11,... | collective-permute-start | bytes 786440 | tf_op jit(solution)/shard_map/ppermute | solution.py:250
  104.1 1.6 %collective-permute-start.31 = (bf16[64,2048]{1,0:T(8,128)(2,1)S(1)}, bf16[64,2048]{1,0:T(8,128)(2,1)S(1)}, u32[]{:S(2)}, u32[]{:S(2)}) collective-permute-start(bf16[64,2048]{1,0:T(8,128)(2,1)S(1)} %get-tuple-element.52), channel_id=1, source_target_pairs={{0,4},{5,1},{4,8},{9,5},{8,12},{13,9},{12,14},{15,13},{14,10},{11,... | collective-permute-start | bytes 786440 | tf_op jit(solution)/shard_map/ppermute | solution.py:250
  105.7 3.1 %collective-permute-done.29 = bf16[64,2048]{1,0:T(8,128)(2,1)S(1)} collective-permute-done((bf16[64,2048]{1,0:T(8,128)(2,1)S(1)}, bf16[64,2048]{1,0:T(8,128)(2,1)S(1)}, u32[]{:S(2)}, u32[]{:S(2)}) %collective-permute-start.29) | collective-permute-done | bytes 262176 | tf_op jit(solution)/shard_map/ppermute | solution.py:250
  108.8 2.8 %collective-permute-done.31 = bf16[64,2048]{1,0:T(8,128)(2,1)S(1)} collective-permute-done((bf16[64,2048]{1,0:T(8,128)(2,1)S(1)}, bf16[64,2048]{1,0:T(8,128)(2,1)S(1)}, u32[]{:S(2)}, u32[]{:S(2)}) %collective-permute-start.31) | collective-permute-done | bytes 262176 | tf_op jit(solution)/shard_map/ppermute | solution.py:250
  111.6 0.2 add_convert_fusion.8
  111.8 0.8 pad_maximum_fusion
  (21 shorter events, 0.1 us)
Async XLA Ops:
  1.3 10.6 %collective-permute-start.2 = (bf16[128,2176]{1,0:T(8,128)(2,1)S(1)}, bf16[128,2176]{1,0:T(8,128)(2,1)S(1)}, u32[]{:S(2)}, u32[]{:S(2)}) collective-permute-start(bf16[128,2176]{1,0:T(8,128)(2,1)S(1)} %packed.1.near_ref), channel_id=1, source_target_pairs={{0,4},{5,1},{4,8},{9,5},{8,12},{13,9},{12,14},{15,13},{14,10},{11,... | collective-permute-start | bytes 1671176 | tf_op jit(solution)/shard_map/ppermute | solution.py:235
  11.9 7.6 %collective-permute-start.21 = (bf16[128,2176]{1,0:T(8,128)(2,1)S(1)}, bf16[128,2176]{1,0:T(8,128)(2,1)S(1)}, u32[]{:S(2)}, u32[]{:S(2)}) collective-permute-start(bf16[128,2176]{1,0:T(8,128)(2,1)S(1)} %collective-permute-done.2.near_ref), channel_id=1, source_target_pairs={{0,1},{1,0},{2,3},{3,2},{4,5},{5,4},{6,7},{7,6},{8,9},{9,8},{10,11... | collective-permute-start | bytes 1671176 | tf_op jit(solution)/shard_map/ppermute | solution.py:233
  11.9 0.7 copy-start
  17.4 9.6 %collective-permute-start.3 = (bf16[128,2176]{1,0:T(8,128)(2,1)S(1)}, bf16[128,2176]{1,0:T(8,128)(2,1)S(1)}, u32[]{:S(2)}, u32[]{:S(2)}) collective-permute-start(bf16[128,2176]{1,0:T(8,128)(2,1)S(1)} %collective-permute-done.2.near_ref), channel_id=1, source_target_pairs={{0,4},{5,1},{4,8},{9,5},{8,12},{13,9},{12,14},{15,13},{14,10},{11,... | collective-permute-start | bytes 1671176 | tf_op jit(solution)/shard_map/ppermute | solution.py:235
  22.9 6.2 %collective-permute-start.22 = (bf16[128,2048]{1,0:T(8,128)(2,1)S(1)}, bf16[128,2048]{1,0:T(8,128)(2,1)S(1)}, u32[]{:S(2)}, u32[]{:S(2)}) collective-permute-start(bf16[128,2048]{1,0:T(8,128)(2,1)S(1)} %get-tuple-element.46), channel_id=1, source_target_pairs={{0,1},{1,0},{2,3},{3,2},{4,5},{5,4},{6,7},{7,6},{8,9},{9,8},{10,11... | collective-permute-start | bytes 1572872 | tf_op jit(solution)/shard_map/ppermute | solution.py:237
  27.0 3.8 %collective-permute-start.19 = (bf16[128,2176]{1,0:T(8,128)(2,1)S(1)}, bf16[128,2176]{1,0:T(8,128)(2,1)S(1)}, u32[]{:S(2)}, u32[]{:S(2)}) collective-permute-start(bf16[128,2176]{1,0:T(8,128)(2,1)S(1)} %collective-permute-done.3.near_ref), channel_id=1, source_target_pairs={{0,1},{1,0},{2,3},{3,2},{4,5},{5,4},{6,7},{7,6},{8,9},{9,8},{10,11... | collective-permute-start | bytes 1671176 | tf_op jit(solution)/shard_map/ppermute | solution.py:233
  27.0 9.5 %collective-permute-start.4 = (bf16[128,2176]{1,0:T(8,128)(2,1)S(1)}, bf16[128,2176]{1,0:T(8,128)(2,1)S(1)}, u32[]{:S(2)}, u32[]{:S(2)}) collective-permute-start(bf16[128,2176]{1,0:T(8,128)(2,1)S(1)} %collective-permute-done.3.near_ref), channel_id=1, source_target_pairs={{0,4},{5,1},{4,8},{9,5},{8,12},{13,9},{12,14},{15,13},{14,10},{11,... | collective-permute-start | bytes 1671176 | tf_op jit(solution)/shard_map/ppermute | solution.py:235
  29.2 13.0 %collective-permute-start.23 = (bf16[128,2048]{1,0:T(8,128)(2,1)S(1)}, bf16[128,2048]{1,0:T(8,128)(2,1)S(1)}, u32[]{:S(2)}, u32[]{:S(2)}) collective-permute-start(bf16[128,2048]{1,0:T(8,128)(2,1)S(1)} %add_convert_fusion.4), channel_id=1, source_target_pairs={{0,4},{5,1},{4,8},{9,5},{8,12},{13,9},{12,14},{15,13},{14,10},{11,... | collective-permute-start | bytes 1572872 | tf_op jit(solution)/shard_map/ppermute | solution.py:245
  34.1 8.0 %collective-permute-start.20 = (bf16[128,2048]{1,0:T(8,128)(2,1)S(1)}, bf16[128,2048]{1,0:T(8,128)(2,1)S(1)}, u32[]{:S(2)}, u32[]{:S(2)}) collective-permute-start(bf16[128,2048]{1,0:T(8,128)(2,1)S(1)} %get-tuple-element.44), channel_id=1, source_target_pairs={{0,1},{1,0},{2,3},{3,2},{4,5},{5,4},{6,7},{7,6},{8,9},{9,8},{10,11... | collective-permute-start | bytes 1572872 | tf_op jit(solution)/shard_map/ppermute | solution.py:237
  36.5 8.0 %collective-permute-start.17 = (bf16[128,2176]{1,0:T(8,128)(2,1)S(1)}, bf16[128,2176]{1,0:T(8,128)(2,1)S(1)}, u32[]{:S(2)}, u32[]{:S(2)}) collective-permute-start(bf16[128,2176]{1,0:T(8,128)(2,1)S(1)} %collective-permute-done.4.near_ref), channel_id=1, source_target_pairs={{0,1},{1,0},{2,3},{3,2},{4,5},{5,4},{6,7},{7,6},{8,9},{9,8},{10,11... | collective-permute-start | bytes 1671176 | tf_op jit(solution)/shard_map/ppermute | solution.py:233
  36.5 11.6 %collective-permute-start.5 = (bf16[128,2176]{1,0:T(8,128)(2,1)S(1)}, bf16[128,2176]{1,0:T(8,128)(2,1)S(1)}, u32[]{:S(2)}, u32[]{:S(2)}) collective-permute-start(bf16[128,2176]{1,0:T(8,128)(2,1)S(1)} %collective-permute-done.4.near_ref), channel_id=1, source_target_pairs={{0,4},{5,1},{4,8},{9,5},{8,12},{13,9},{12,14},{15,13},{14,10},{11,... | collective-permute-start | bytes 1671176 | tf_op jit(solution)/shard_map/ppermute | solution.py:235
  42.3 11.4 %collective-permute-start.24 = (bf16[128,2048]{1,0:T(8,128)(2,1)S(1)}, bf16[128,2048]{1,0:T(8,128)(2,1)S(1)}, u32[]{:S(2)}, u32[]{:S(2)}) collective-permute-start(bf16[128,2048]{1,0:T(8,128)(2,1)S(1)} %add_convert_fusion.3), channel_id=1, source_target_pairs={{0,4},{5,1},{4,8},{9,5},{8,12},{13,9},{12,14},{15,13},{14,10},{11,... | collective-permute-start | bytes 1572872 | tf_op jit(solution)/shard_map/ppermute | solution.py:245
  47.8 5.9 %collective-permute-start.18 = (bf16[128,2048]{1,0:T(8,128)(2,1)S(1)}, bf16[128,2048]{1,0:T(8,128)(2,1)S(1)}, u32[]{:S(2)}, u32[]{:S(2)}) collective-permute-start(bf16[128,2048]{1,0:T(8,128)(2,1)S(1)} %get-tuple-element.42), channel_id=1, source_target_pairs={{0,1},{1,0},{2,3},{3,2},{4,5},{5,4},{6,7},{7,6},{8,9},{9,8},{10,11... | collective-permute-start | bytes 1572872 | tf_op jit(solution)/shard_map/ppermute | solution.py:237
  48.1 8.0 %collective-permute-start.15 = (bf16[128,2176]{1,0:T(8,128)(2,1)S(1)}, bf16[128,2176]{1,0:T(8,128)(2,1)S(1)}, u32[]{:S(2)}, u32[]{:S(2)}) collective-permute-start(bf16[128,2176]{1,0:T(8,128)(2,1)S(1)} %collective-permute-done.5.near_ref), channel_id=1, source_target_pairs={{0,1},{1,0},{2,3},{3,2},{4,5},{5,4},{6,7},{7,6},{8,9},{9,8},{10,11... | collective-permute-start | bytes 1671176 | tf_op jit(solution)/shard_map/ppermute | solution.py:233
  48.4 11.3 %collective-permute-start.6 = (bf16[128,2176]{1,0:T(8,128)(2,1)S(1)}, bf16[128,2176]{1,0:T(8,128)(2,1)S(1)}, u32[]{:S(2)}, u32[]{:S(2)}) collective-permute-start(bf16[128,2176]{1,0:T(8,128)(2,1)S(1)} %collective-permute-done.5.near_ref), channel_id=1, source_target_pairs={{0,4},{5,1},{4,8},{9,5},{8,12},{13,9},{12,14},{15,13},{14,10},{11,... | collective-permute-start | bytes 1671176 | tf_op jit(solution)/shard_map/ppermute | solution.py:235
  53.9 11.4 %collective-permute-start.25 = (bf16[128,2048]{1,0:T(8,128)(2,1)S(1)}, bf16[128,2048]{1,0:T(8,128)(2,1)S(1)}, u32[]{:S(2)}, u32[]{:S(2)}) collective-permute-start(bf16[128,2048]{1,0:T(8,128)(2,1)S(1)} %add_convert_fusion.2), channel_id=1, source_target_pairs={{0,4},{5,1},{4,8},{9,5},{8,12},{13,9},{12,14},{15,13},{14,10},{11,... | collective-permute-start | bytes 1572872 | tf_op jit(solution)/shard_map/ppermute | solution.py:245
  59.4 5.9 %collective-permute-start.16 = (bf16[128,2048]{1,0:T(8,128)(2,1)S(1)}, bf16[128,2048]{1,0:T(8,128)(2,1)S(1)}, u32[]{:S(2)}, u32[]{:S(2)}) collective-permute-start(bf16[128,2048]{1,0:T(8,128)(2,1)S(1)} %get-tuple-element.40), channel_id=1, source_target_pairs={{0,1},{1,0},{2,3},{3,2},{4,5},{5,4},{6,7},{7,6},{8,9},{9,8},{10,11... | collective-permute-start | bytes 1572872 | tf_op jit(solution)/shard_map/ppermute | solution.py:237
  59.7 11.6 %collective-permute-start.7 = (bf16[128,2176]{1,0:T(8,128)(2,1)S(1)}, bf16[128,2176]{1,0:T(8,128)(2,1)S(1)}, u32[]{:S(2)}, u32[]{:S(2)}) collective-permute-start(bf16[128,2176]{1,0:T(8,128)(2,1)S(1)} %collective-permute-done.6.near_ref), channel_id=1, source_target_pairs={{0,4},{5,1},{4,8},{9,5},{8,12},{13,9},{12,14},{15,13},{14,10},{11,... | collective-permute-start | bytes 1671176 | tf_op jit(solution)/shard_map/ppermute | solution.py:235
  61.8 11.6 %collective-permute-start.13 = (bf16[128,2176]{1,0:T(8,128)(2,1)S(1)}, bf16[128,2176]{1,0:T(8,128)(2,1)S(1)}, u32[]{:S(2)}, u32[]{:S(2)}) collective-permute-start(bf16[128,2176]{1,0:T(8,128)(2,1)S(1)} %collective-permute-done.6.near_ref), channel_id=1, source_target_pairs={{0,1},{1,0},{2,3},{3,2},{4,5},{5,4},{6,7},{7,6},{8,9},{9,8},{10,11... | collective-permute-start | bytes 1671176 | tf_op jit(solution)/shard_map/ppermute | solution.py:233
  65.5 17.4 %collective-permute-start.26 = (bf16[128,2048]{1,0:T(8,128)(2,1)S(1)}, bf16[128,2048]{1,0:T(8,128)(2,1)S(1)}, u32[]{:S(2)}, u32[]{:S(2)}) collective-permute-start(bf16[128,2048]{1,0:T(8,128)(2,1)S(1)} %add_convert_fusion.1), channel_id=1, source_target_pairs={{0,4},{5,1},{4,8},{9,5},{8,12},{13,9},{12,14},{15,13},{14,10},{11,... | collective-permute-start | bytes 1572872 | tf_op jit(solution)/shard_map/ppermute | solution.py:245
  71.3 11.6 %collective-permute-start.8 = (bf16[128,2176]{1,0:T(8,128)(2,1)S(1)}, bf16[128,2176]{1,0:T(8,128)(2,1)S(1)}, u32[]{:S(2)}, u32[]{:S(2)}) collective-permute-start(bf16[128,2176]{1,0:T(8,128)(2,1)S(1)} %collective-permute-done.7.near_ref), channel_id=1, source_target_pairs={{0,4},{5,1},{4,8},{9,5},{8,12},{13,9},{12,14},{15,13},{14,10},{11,... | collective-permute-start | bytes 1671176 | tf_op jit(solution)/shard_map/ppermute | solution.py:235
  76.7 6.2 %collective-permute-start.14 = (bf16[128,2048]{1,0:T(8,128)(2,1)S(1)}, bf16[128,2048]{1,0:T(8,128)(2,1)S(1)}, u32[]{:S(2)}, u32[]{:S(2)}) collective-permute-start(bf16[128,2048]{1,0:T(8,128)(2,1)S(1)} %get-tuple-element.38), channel_id=1, source_target_pairs={{0,1},{1,0},{2,3},{3,2},{4,5},{5,4},{6,7},{7,6},{8,9},{9,8},{10,11... | collective-permute-start | bytes 1572872 | tf_op jit(solution)/shard_map/ppermute | solution.py:237
  76.8 8.4 %collective-permute-start.11 = (bf16[128,2176]{1,0:T(8,128)(2,1)S(1)}, bf16[128,2176]{1,0:T(8,128)(2,1)S(1)}, u32[]{:S(2)}, u32[]{:S(2)}) collective-permute-start(bf16[128,2176]{1,0:T(8,128)(2,1)S(1)} %collective-permute-done.7.near_ref), channel_id=1, source_target_pairs={{0,1},{1,0},{2,3},{3,2},{4,5},{5,4},{6,7},{7,6},{8,9},{9,8},{10,11... | collective-permute-start | bytes 1671176 | tf_op jit(solution)/shard_map/ppermute | solution.py:233
  82.9 6.2 %collective-permute-start.9 = (bf16[128,2176]{1,0:T(8,128)(2,1)S(1)}, bf16[128,2176]{1,0:T(8,128)(2,1)S(1)}, u32[]{:S(2)}, u32[]{:S(2)}) collective-permute-start(bf16[128,2176]{1,0:T(8,128)(2,1)S(1)} %collective-permute-done.8.near_ref), channel_id=1, source_target_pairs={{0,1},{1,0},{2,3},{3,2},{4,5},{5,4},{6,7},{7,6},{8,9},{9,8},{10,11... | collective-permute-start | bytes 1671176 | tf_op jit(solution)/shard_map/ppermute | solution.py:233
  83.1 9.6 %collective-permute-start.27 = (bf16[128,2048]{1,0:T(8,128)(2,1)S(1)}, bf16[128,2048]{1,0:T(8,128)(2,1)S(1)}, u32[]{:S(2)}, u32[]{:S(2)}) collective-permute-start(bf16[128,2048]{1,0:T(8,128)(2,1)S(1)} %add_convert_fusion), channel_id=1, source_target_pairs={{0,4},{5,1},{4,8},{9,5},{8,12},{13,9},{12,14},{15,13},{14,10},{11,... | collective-permute-start | bytes 1572872 | tf_op jit(solution)/shard_map/ppermute | solution.py:245
  88.5 4.2 %collective-permute-start.12 = (bf16[128,2048]{1,0:T(8,128)(2,1)S(1)}, bf16[128,2048]{1,0:T(8,128)(2,1)S(1)}, u32[]{:S(2)}, u32[]{:S(2)}) collective-permute-start(bf16[128,2048]{1,0:T(8,128)(2,1)S(1)} %get-tuple-element.36), channel_id=1, source_target_pairs={{0,1},{1,0},{2,3},{3,2},{4,5},{5,4},{6,7},{7,6},{8,9},{9,8},{10,11... | collective-permute-start | bytes 1572872 | tf_op jit(solution)/shard_map/ppermute | solution.py:237
  88.8 7.4 %collective-permute-start = (bf16[128,2176]{1,0:T(8,128)(2,1)S(1)}, bf16[128,2176]{1,0:T(8,128)(2,1)S(1)}, u32[]{:S(2)}, u32[]{:S(2)}) collective-permute-start(bf16[128,2176]{1,0:T(8,128)(2,1)S(1)} %packed.1.near_ref), channel_id=1, source_target_pairs={{0,1},{1,0},{2,3},{3,2},{4,5},{5,4},{6,7},{7,6},{8,9},{9,8},{10,11... | collective-permute-start | bytes 1671176 | tf_op jit(solution)/shard_map/ppermute | solution.py:233
  92.4 9.7 %collective-permute-start.10 = (bf16[128,2048]{1,0:T(8,128)(2,1)S(1)}, bf16[128,2048]{1,0:T(8,128)(2,1)S(1)}, u32[]{:S(2)}, u32[]{:S(2)}) collective-permute-start(bf16[128,2048]{1,0:T(8,128)(2,1)S(1)} %get-tuple-element.34), channel_id=1, source_target_pairs={{0,1},{1,0},{2,3},{3,2},{4,5},{5,4},{6,7},{7,6},{8,9},{9,8},{10,11... | collective-permute-start | bytes 1572872 | tf_op jit(solution)/shard_map/ppermute | solution.py:237
  92.9 6.7 %collective-permute-start.28 = (bf16[64,2048]{1,0:T(8,128)(2,1)S(1)}, bf16[64,2048]{1,0:T(8,128)(2,1)S(1)}, u32[]{:S(2)}, u32[]{:S(2)}) collective-permute-start(bf16[64,2048]{1,0:T(8,128)(2,1)S(1)} %get-tuple-element.47), channel_id=1, source_target_pairs={{0,4},{5,1},{4,8},{9,5},{8,12},{13,9},{12,14},{15,13},{14,10},{11,... | collective-permute-start | bytes 786440 | tf_op jit(solution)/shard_map/ppermute | solution.py:250
  94.6 7.5 %collective-permute-start.30 = (bf16[64,2048]{1,0:T(8,128)(2,1)S(1)}, bf16[64,2048]{1,0:T(8,128)(2,1)S(1)}, u32[]{:S(2)}, u32[]{:S(2)}) collective-permute-start(bf16[64,2048]{1,0:T(8,128)(2,1)S(1)} %get-tuple-element.48), channel_id=1, source_target_pairs={{0,4},{5,1},{4,8},{9,5},{8,12},{13,9},{12,14},{15,13},{14,10},{11,... | collective-permute-start | bytes 786440 | tf_op jit(solution)/shard_map/ppermute | solution.py:250
  99.5 6.1 %collective-permute-start.1 = (bf16[128,2048]{1,0:T(8,128)(2,1)S(1)}, bf16[128,2048]{1,0:T(8,128)(2,1)S(1)}, u32[]{:S(2)}, u32[]{:S(2)}) collective-permute-start(bf16[128,2048]{1,0:T(8,128)(2,1)S(1)} %get-tuple-element.32), channel_id=1, source_target_pairs={{0,1},{1,0},{2,3},{3,2},{4,5},{5,4},{6,7},{7,6},{8,9},{9,8},{10,11... | collective-permute-start | bytes 1572872 | tf_op jit(solution)/shard_map/ppermute | solution.py:237
  102.3 6.4 %collective-permute-start.29 = (bf16[64,2048]{1,0:T(8,128)(2,1)S(1)}, bf16[64,2048]{1,0:T(8,128)(2,1)S(1)}, u32[]{:S(2)}, u32[]{:S(2)}) collective-permute-start(bf16[64,2048]{1,0:T(8,128)(2,1)S(1)} %get-tuple-element.51), channel_id=1, source_target_pairs={{0,4},{5,1},{4,8},{9,5},{8,12},{13,9},{12,14},{15,13},{14,10},{11,... | collective-permute-start | bytes 786440 | tf_op jit(solution)/shard_map/ppermute | solution.py:250
  104.1 7.5 %collective-permute-start.31 = (bf16[64,2048]{1,0:T(8,128)(2,1)S(1)}, bf16[64,2048]{1,0:T(8,128)(2,1)S(1)}, u32[]{:S(2)}, u32[]{:S(2)}) collective-permute-start(bf16[64,2048]{1,0:T(8,128)(2,1)S(1)} %get-tuple-element.52), channel_id=1, source_target_pairs={{0,4},{5,1},{4,8},{9,5},{8,12},{13,9},{12,14},{15,13},{14,10},{11,... | collective-permute-start | bytes 786440 | tf_op jit(solution)/shard_map/ppermute | solution.py:250

commit v5 on v4

--- a/solution.py
+++ b/solution.py
@@ -123,41 +123,39 @@
     )(*map(in_hbm, (tokens, norm_gain[None, :], expert_ids.T, gate_weights.T)))
 
 
-def loaded_kernel(
-    owner_ref, in_hbm, in_scale_hbm, down_hbm, down_scale_hbm,
-    mine_ref, in_ref, in_scale_ref, down_ref, down_scale_ref, sems,
-):
-    pairs = (
-        (in_hbm, in_ref), (in_scale_hbm, in_scale_ref), (down_hbm, down_ref), (down_scale_hbm, down_scale_ref),
-    )
-    moves = [
-        pltpu.make_async_copy(source, target, sems.at[i]) for i, (source, target) in enumerate(pairs)
-    ]
-    for move in moves:
-        move.start()
+def found_kernel(owner_ref, mine_ref):
     me = lax.axis_index("tok")
     mine_ref[0] = lax.fori_loop(
         0, owner_ref.shape[0], lambda i, found: jnp.where(owner_ref[i] == me, i, found), 0
     )
+
+
+def loaded_kernel(count, *refs):
+    sources, targets, sems = refs[:count], refs[count : 2 * count], refs[-1]
+    moves = [
+        pltpu.make_async_copy(source, target, sems.at[i])
+        for i, (source, target) in enumerate(zip(sources, targets))
+    ]
+    for move in moves:
+        move.start()
     for move in moves:
         move.wait()
 
 
-def loaded(owner_map, in_q, in_scale, down_q, down_scale):
-    blocks = (in_q, in_scale, down_q, down_scale)
+def loaded(*arrays):
+    count = len(arrays)
     return pl.pallas_call(
-        loaded_kernel,
-        out_shape=(jax.ShapeDtypeStruct((1,), jnp.int32),)
-        + tuple(jax.ShapeDtypeStruct(x.shape, x.dtype) for x in blocks),
-        in_specs=[pl.BlockSpec(memory_space=pltpu.SMEM)] + [pl.BlockSpec(memory_space=pltpu.HBM)] * 4,
-        out_specs=(pl.BlockSpec(memory_space=pltpu.SMEM),) + (pl.BlockSpec(memory_space=pltpu.VMEM),) * 4,
-        scratch_shapes=[pltpu.SemaphoreType.DMA((4,))],
+        functools.partial(loaded_kernel, count),
+        out_shape=tuple(jax.ShapeDtypeStruct(x.shape, x.dtype) for x in arrays),
+        in_specs=[pl.BlockSpec(memory_space=pltpu.HBM)] * count,
+        out_specs=(pl.BlockSpec(memory_space=pltpu.VMEM),) * count,
+        scratch_shapes=[pltpu.SemaphoreType.DMA((count,))],
         compiler_params=pltpu.CompilerParams(vmem_limit_bytes=SMALL),
         cost_estimate=pl.CostEstimate(
-            flops=0, bytes_accessed=2 * (in_q.size + down_q.size), transcendentals=0
+            flops=0, bytes_accessed=2 * sum(x.size for x in arrays), transcendentals=0
         ),
         name="loaded",
-    )(owner_map, *map(in_hbm, blocks))
+    )(*map(in_hbm, arrays))
 
 
 def visit_kernel(
@@ -225,13 +223,22 @@
     swap = [(i, i ^ 1) for i in range(devices)]
     half = tokens.shape[0] // 2
     block = packed(tokens, norm_gain, expert_ids, gate_weights, experts)
-    mine, *blocks = loaded(owner_map, in_q, in_scale, down_q, down_scale)
-
+    blocks = loaded(in_q, in_scale, down_q, down_scale)
+    mine = pl.pallas_call(
+        found_kernel,
+        out_shape=jax.ShapeDtypeStruct((1,), jnp.int32),
+        in_specs=[pl.BlockSpec(memory_space=pltpu.SMEM)],
+        out_specs=pl.BlockSpec(memory_space=pltpu.SMEM),
+        compiler_params=pltpu.CompilerParams(vmem_limit_bytes=SMALL),
+        name="found",
+    )(owner_map)
+
+    back = lax.ppermute(block, "tok", [(target, source) for source, target in ring])
     parts = []
     for step in range(chips):
-        here = block
+        here = block if step < chips - 1 else back
         other = lax.ppermute(here, "tok", swap)
-        if step < chips - 1:
+        if step < chips - 2:
             block = lax.ppermute(here, "tok", ring)
         part, lent = visit(mine, here, other, experts, *blocks)
         parts.append((part, lax.ppermute(lent, "tok", swap)))

time: 113 us -> 113 us (level)
  starting transfers between devices: 34.3 us -> 33 us
  waiting for transfers between devices: 42.3 us -> 43.5 us
    ppermute x5, waiting for transfers between devices: 10.6 us -> 17.7 us  [circulated(): total = lax.ppermute(summed(step, slice(None), total), 'tok', ring)]
    ppermute x7 -> x6, waiting for transfers between devices: 23.3 us -> 17.6 us  [circulated(): block = lax.ppermute(here, 'tok', ring)]
    ppermute x7 -> x6, starting transfers between devices: 15.3 us -> 11.5 us  [circulated(): block = lax.ppermute(here, 'tok', ring)]
    ppermute x0 -> x1, starting transfers between devices: none -> 1.74 us  [circulated(): lax.ppermute(block, 'tok', [(target, source) for source, target in ring])]
    pallas_call x1 -> x2, Pallas kernels: 4.82 us -> 5 us  [the longest x1 3.77 us: loaded(): pl.pallas_call(functools.partial(loaded_kernel, count), out_shape=tuple((...]
where the time goes in v5:
time: 113 us
  waiting for transfers between devices  43.5 us (38%)
  starting transfers between devices  33 us (29%)
  Pallas kernels  32.9 us (29%)
  other arithmetic  2.31 us (2%)
    pallas_call x8, Pallas kernels, visit(): pl.pallas_call(functools.partial(visit_kernel, experts), out_shape=(jax.S...  26.6 us
    ppermute x5, waiting for transfers between devices, circulated(): total = lax.ppermute(summed(step, slice(None), total), 'tok', ring)  17.7 us
    ppermute x6, waiting for transfers between devices, circulated(): block = lax.ppermute(here, 'tok', ring)  17.6 us
    ppermute x6, starting transfers between devices, circulated(): block = lax.ppermute(here, 'tok', ring)  11.5 us
    ppermute x5, starting transfers between devices, circulated(): total = lax.ppermute(summed(step, slice(None), total), 'tok', ring)  10.6 us
    ppermute x4, waiting for transfers between devices, circulated(): totals[name] = lax.ppermute(summed(step, cut, totals[name]), 'tok', ring)  8.19 us
    ppermute x4, starting transfers between devices, circulated(): totals[name] = lax.ppermute(summed(step, cut, totals[name]), 'tok', ring)  6.84 us
    pallas_call x1, Pallas kernels, loaded(): pl.pallas_call(functools.partial(loaded_kernel, count), out_shape=tuple((...  3.77 us
  transfers between devices with their start and end apart: 32, of which 13 were waited for; matrix products, arithmetic and copies ran while one was open for 1% of the time, Pallas kernels for 28%

profile of v5, /device:TPU:0, one launch (start us, length us, event | category | flops | bytes accessed | tf_op | source)
XLA Modules:
  0.0 112.7 jit_solution(5663065057335962377)
XLA Ops:
  0.0 1.3 %packed.1.near_ref = bf16[128,2176]{1,0:T(8,128)(2,1)S(1)} custom-call(bf16[128,2048]{1,0:T(8,128)(2,1)} %tokens_hbm.1, f32[1,2048]{1,0:T(1,128)} %bitcast.3, s32[8,128]{1,0:T(8,128)} %bitcast.4, f32[8,128]{1,0:T(8,128)} %bitcast.5), custom_call_target="tpu_custom_call" | custom-call | tf_op jit(solution)/shard_map/packed/pallas_call | solution.py:109
  1.3 3.1 %collective-permute-start.5 = (bf16[128,2176]{1,0:T(8,128)(2,1)S(1)}, bf16[128,2176]{1,0:T(8,128)(2,1)S(1)}, u32[]{:S(2)}, u32[]{:S(2)}) collective-permute-start(bf16[128,2176]{1,0:T(8,128)(2,1)S(1)} %packed.1.near_ref), channel_id=1, source_target_pairs={{0,4},{5,1},{4,8},{9,5},{8,12},{13,9},{12,14},{15,13},{14,10},{11,... | collective-permute-start | bytes 1671176 | tf_op jit(solution)/shard_map/ppermute | solution.py:242
  4.4 7.5 %collective-permute-done.5.near_ref = bf16[128,2176]{1,0:T(8,128)(2,1)S(1)} collective-permute-done((bf16[128,2176]{1,0:T(8,128)(2,1)S(1)}, bf16[128,2176]{1,0:T(8,128)(2,1)S(1)}, u32[]{:S(2)}, u32[]{:S(2)}) %collective-permute-start.5) | collective-permute-done | bytes 557088 | tf_op jit(solution)/shard_map/ppermute | solution.py:242
  11.9 0.0 collective-permute-start.21
  11.9 0.7 copy-done
  12.6 1.2 %found.1.mine_ref = s32[1]{0:T(128)} custom-call(s32[16]{0:T(128)S(1)} %copy-done), custom_call_target="tpu_custom_call" | custom-call | tf_op jit(solution)/shard_map/found/pallas_call | solution.py:227
  13.8 3.8 %loaded.1 = (bf16[1,2,2048,768]{3,2,1,0:T(8,128)(2,1)S(1)}, bf16[1,2,768]{2,1,0:T(2,128)(2,1)S(1)}, bf16[1,768,2048]{2,1,0:T(8,128)(2,1)S(1)}, bf16[1,2048]{1,0:T(2,128)(2,1)S(1)}) custom-call(bf16[1,2,2048,768]{3,2,1,0:T(8,128)(2,1)} %refs_0_.1, bf16[1,2,768]{2,1,0:T(2,128)(2,1)} %refs_1_.1, bf16[1,768,2048]{2,1,0:T(8,128)(2,1)} %refs_2_.1, ...), custom_call_target="tpu_custom_call" | custom-call | bytes 9444352 | tf_op jit(solution)/shard_map/loaded/pallas_call | solution.py:147
  17.6 2.1 %collective-permute-start.6 = (bf16[128,2176]{1,0:T(8,128)(2,1)S(1)}, bf16[128,2176]{1,0:T(8,128)(2,1)S(1)}, u32[]{:S(2)}, u32[]{:S(2)}) collective-permute-start(bf16[128,2176]{1,0:T(8,128)(2,1)S(1)} %collective-permute-done.5.near_ref), channel_id=1, source_target_pairs={{0,4},{5,1},{4,8},{9,5},{8,12},{13,9},{12,14},{15,13},{14,10},{11,... | collective-permute-start | bytes 1671176 | tf_op jit(solution)/shard_map/ppermute | solution.py:242
  19.7 0.0 collective-permute-done.21.far_ref
  19.7 3.3 %visit.15 = (f32[128,2048]{1,0:T(8,128)S(1)}, bf16[128,2048]{1,0:T(8,128)(2,1)S(1)}) custom-call(s32[1]{0:T(128)} %found.1.mine_ref, bf16[128,2176]{1,0:T(8,128)(2,1)S(1)} %collective-permute-done.5.near_ref, bf16[128,2176]{1,0:T(8,128)(2,1)S(1)} %collective-permute-done.21.far_ref, bf16[1,2,2048,768]{3,2,1,0:T(8,128)(2,1)S(1)} %get-tuple-element.25.in_ref, ...), custom_call_target="tpu_custom_call" | custom-call | flops 2415919104 | bytes 1572864 | tf_op jit(solution)/shard_map/visit/pallas_call | solution.py:196
  23.0 0.2 collective-permute-start.22
  23.3 3.9 %collective-permute-done.6.near_ref = bf16[128,2176]{1,0:T(8,128)(2,1)S(1)} collective-permute-done((bf16[128,2176]{1,0:T(8,128)(2,1)S(1)}, bf16[128,2176]{1,0:T(8,128)(2,1)S(1)}, u32[]{:S(2)}, u32[]{:S(2)}) %collective-permute-start.6) | collective-permute-done | bytes 557088 | tf_op jit(solution)/shard_map/ppermute | solution.py:242
  27.2 2.1 %collective-permute-start.7 = (bf16[128,2176]{1,0:T(8,128)(2,1)S(1)}, bf16[128,2176]{1,0:T(8,128)(2,1)S(1)}, u32[]{:S(2)}, u32[]{:S(2)}) collective-permute-start(bf16[128,2176]{1,0:T(8,128)(2,1)S(1)} %collective-permute-done.6.near_ref), channel_id=1, source_target_pairs={{0,4},{5,1},{4,8},{9,5},{8,12},{13,9},{12,14},{15,13},{14,10},{11,... | collective-permute-start | bytes 1671176 | tf_op jit(solution)/shard_map/ppermute | solution.py:242
  29.2 0.1 add_convert_fusion.4
  29.4 1.6 %collective-permute-start.23 = (bf16[128,2048]{1,0:T(8,128)(2,1)S(1)}, bf16[128,2048]{1,0:T(8,128)(2,1)S(1)}, u32[]{:S(2)}, u32[]{:S(2)}) collective-permute-start(bf16[128,2048]{1,0:T(8,128)(2,1)S(1)} %add_convert_fusion.4), channel_id=1, source_target_pairs={{0,4},{5,1},{4,8},{9,5},{8,12},{13,9},{12,14},{15,13},{14,10},{11,... | collective-permute-start | bytes 1572872 | tf_op jit(solution)/shard_map/ppermute | solution.py:252
  31.0 3.3 %visit.14 = (f32[128,2048]{1,0:T(8,128)S(1)}, bf16[128,2048]{1,0:T(8,128)(2,1)S(1)}) custom-call(s32[1]{0:T(128)} %found.1.mine_ref, bf16[128,2176]{1,0:T(8,128)(2,1)S(1)} %collective-permute-done.6.near_ref, bf16[128,2176]{1,0:T(8,128)(2,1)S(1)} %collective-permute-done.19.far_ref, bf16[1,2,2048,768]{3,2,1,0:T(8,128)(2,1)S(1)} %get-tuple-element.25.in_ref, ...), custom_call_target="tpu_custom_call" | custom-call | flops 2415919104 | bytes 1572864 | tf_op jit(solution)/shard_map/visit/pallas_call | solution.py:196
  34.3 0.1 collective-permute-start.20
  34.4 2.3 %collective-permute-done.7.near_ref = bf16[128,2176]{1,0:T(8,128)(2,1)S(1)} collective-permute-done((bf16[128,2176]{1,0:T(8,128)(2,1)S(1)}, bf16[128,2176]{1,0:T(8,128)(2,1)S(1)}, u32[]{:S(2)}, u32[]{:S(2)}) %collective-permute-start.7) | collective-permute-done | bytes 557088 | tf_op jit(solution)/shard_map/ppermute | solution.py:242
  36.7 2.1 %collective-permute-start.8 = (bf16[128,2176]{1,0:T(8,128)(2,1)S(1)}, bf16[128,2176]{1,0:T(8,128)(2,1)S(1)}, u32[]{:S(2)}, u32[]{:S(2)}) collective-permute-start(bf16[128,2176]{1,0:T(8,128)(2,1)S(1)} %collective-permute-done.7.near_ref), channel_id=1, source_target_pairs={{0,4},{5,1},{4,8},{9,5},{8,12},{13,9},{12,14},{15,13},{14,10},{11,... | collective-permute-start | bytes 1671176 | tf_op jit(solution)/shard_map/ppermute | solution.py:242
  38.8 3.5 %collective-permute-done.23 = bf16[128,2048]{1,0:T(8,128)(2,1)S(1)} collective-permute-done((bf16[128,2048]{1,0:T(8,128)(2,1)S(1)}, bf16[128,2048]{1,0:T(8,128)(2,1)S(1)}, u32[]{:S(2)}, u32[]{:S(2)}) %collective-permute-start.23) | collective-permute-done | bytes 524320 | tf_op jit(solution)/shard_map/ppermute | solution.py:252
  42.3 0.2 add_convert_fusion.3
  42.5 2.1 %collective-permute-start.24 = (bf16[128,2048]{1,0:T(8,128)(2,1)S(1)}, bf16[128,2048]{1,0:T(8,128)(2,1)S(1)}, u32[]{:S(2)}, u32[]{:S(2)}) collective-permute-start(bf16[128,2048]{1,0:T(8,128)(2,1)S(1)} %add_convert_fusion.3), channel_id=1, source_target_pairs={{0,4},{5,1},{4,8},{9,5},{8,12},{13,9},{12,14},{15,13},{14,10},{11,... | collective-permute-start | bytes 1572872 | tf_op jit(solution)/shard_map/ppermute | solution.py:252
  44.6 3.3 %visit.13 = (f32[128,2048]{1,0:T(8,128)S(1)}, bf16[128,2048]{1,0:T(8,128)(2,1)S(1)}) custom-call(s32[1]{0:T(128)} %found.1.mine_ref, bf16[128,2176]{1,0:T(8,128)(2,1)S(1)} %collective-permute-done.7.near_ref, bf16[128,2176]{1,0:T(8,128)(2,1)S(1)} %collective-permute-done.17.far_ref, bf16[1,2,2048,768]{3,2,1,0:T(8,128)(2,1)S(1)} %get-tuple-element.25.in_ref, ...), custom_call_target="tpu_custom_call" | custom-call | flops 2415919104 | bytes 1572864 | tf_op jit(solution)/shard_map/visit/pallas_call | solution.py:196
  48.0 0.1 collective-permute-start.18
  48.1 0.2 collective-permute-done.8.near_ref
  48.3 0.3 collective-permute-start.15
  48.6 1.8 %collective-permute-start.9 = (bf16[128,2176]{1,0:T(8,128)(2,1)S(1)}, bf16[128,2176]{1,0:T(8,128)(2,1)S(1)}, u32[]{:S(2)}, u32[]{:S(2)}) collective-permute-start(bf16[128,2176]{1,0:T(8,128)(2,1)S(1)} %collective-permute-done.8.near_ref), channel_id=1, source_target_pairs={{0,4},{5,1},{4,8},{9,5},{8,12},{13,9},{12,14},{15,13},{14,10},{11,... | collective-permute-start | bytes 1671176 | tf_op jit(solution)/shard_map/ppermute | solution.py:242
  50.4 3.5 %collective-permute-done.24 = bf16[128,2048]{1,0:T(8,128)(2,1)S(1)} collective-permute-done((bf16[128,2048]{1,0:T(8,128)(2,1)S(1)}, bf16[128,2048]{1,0:T(8,128)(2,1)S(1)}, u32[]{:S(2)}, u32[]{:S(2)}) %collective-permute-start.24) | collective-permute-done | bytes 524320 | tf_op jit(solution)/shard_map/ppermute | solution.py:252
  53.9 0.2 add_convert_fusion.2
  54.1 2.1 %collective-permute-start.25 = (bf16[128,2048]{1,0:T(8,128)(2,1)S(1)}, bf16[128,2048]{1,0:T(8,128)(2,1)S(1)}, u32[]{:S(2)}, u32[]{:S(2)}) collective-permute-start(bf16[128,2048]{1,0:T(8,128)(2,1)S(1)} %add_convert_fusion.2), channel_id=1, source_target_pairs={{0,4},{5,1},{4,8},{9,5},{8,12},{13,9},{12,14},{15,13},{14,10},{11,... | collective-permute-start | bytes 1572872 | tf_op jit(solution)/shard_map/ppermute | solution.py:252
  56.2 3.3 %visit.12 = (f32[128,2048]{1,0:T(8,128)S(1)}, bf16[128,2048]{1,0:T(8,128)(2,1)S(1)}) custom-call(s32[1]{0:T(128)} %found.1.mine_ref, bf16[128,2176]{1,0:T(8,128)(2,1)S(1)} %collective-permute-done.8.near_ref, bf16[128,2176]{1,0:T(8,128)(2,1)S(1)} %collective-permute-done.15.far_ref, bf16[1,2,2048,768]{3,2,1,0:T(8,128)(2,1)S(1)} %get-tuple-element.25.in_ref, ...), custom_call_target="tpu_custom_call" | custom-call | flops 2415919104 | bytes 1572864 | tf_op jit(solution)/shard_map/visit/pallas_call | solution.py:196
  59.6 0.1 collective-permute-start.16
  59.7 0.2 collective-permute-done.9.near_ref
  59.9 0.3 collective-permute-start.13
  60.2 1.7 %collective-permute-start.2 = (bf16[128,2176]{1,0:T(8,128)(2,1)S(1)}, bf16[128,2176]{1,0:T(8,128)(2,1)S(1)}, u32[]{:S(2)}, u32[]{:S(2)}) collective-permute-start(bf16[128,2176]{1,0:T(8,128)(2,1)S(1)} %packed.1.near_ref), channel_id=1, source_target_pairs={{4,0},{1,5},{8,4},{5,9},{12,8},{9,13},{14,12},{13,15},{10,14},{15,... | collective-permute-start | bytes 1671176 | tf_op jit(solution)/shard_map/ppermute | solution.py:236
  61.9 0.3 collective-permute-start.10
  62.2 5.5 %collective-permute-done.25 = bf16[128,2048]{1,0:T(8,128)(2,1)S(1)} collective-permute-done((bf16[128,2048]{1,0:T(8,128)(2,1)S(1)}, bf16[128,2048]{1,0:T(8,128)(2,1)S(1)}, u32[]{:S(2)}, u32[]{:S(2)}) %collective-permute-start.25) | collective-permute-done | bytes 524320 | tf_op jit(solution)/shard_map/ppermute | solution.py:252
  67.7 0.2 add_convert_fusion.1
  67.9 2.6 %collective-permute-start.26 = (bf16[128,2048]{1,0:T(8,128)(2,1)S(1)}, bf16[128,2048]{1,0:T(8,128)(2,1)S(1)}, u32[]{:S(2)}, u32[]{:S(2)}) collective-permute-start(bf16[128,2048]{1,0:T(8,128)(2,1)S(1)} %add_convert_fusion.1), channel_id=1, source_target_pairs={{0,4},{5,1},{4,8},{9,5},{8,12},{13,9},{12,14},{15,13},{14,10},{11,... | collective-permute-start | bytes 1572872 | tf_op jit(solution)/shard_map/ppermute | solution.py:252
  70.5 3.3 %visit.11 = (f32[128,2048]{1,0:T(8,128)S(1)}, bf16[128,2048]{1,0:T(8,128)(2,1)S(1)}) custom-call(s32[1]{0:T(128)} %found.1.mine_ref, bf16[128,2176]{1,0:T(8,128)(2,1)S(1)} %collective-permute-done.9.near_ref, bf16[128,2176]{1,0:T(8,128)(2,1)S(1)} %collective-permute-done.13.far_ref, bf16[1,2,2048,768]{3,2,1,0:T(8,128)(2,1)S(1)} %get-tuple-element.25.in_ref, ...), custom_call_target="tpu_custom_call" | custom-call | flops 2415919104 | bytes 1572864 | tf_op jit(solution)/shard_map/visit/pallas_call | solution.py:196
  73.8 0.1 collective-permute-start.14
  73.9 3.5 %collective-permute-done.10.near_ref = bf16[128,2176]{1,0:T(8,128)(2,1)S(1)} collective-permute-done((bf16[128,2176]{1,0:T(8,128)(2,1)S(1)}, bf16[128,2176]{1,0:T(8,128)(2,1)S(1)}, u32[]{:S(2)}, u32[]{:S(2)}) %collective-permute-start.10) | collective-permute-done | bytes 557088 | tf_op jit(solution)/shard_map/ppermute | solution.py:242
  77.4 0.5 collective-permute-start.3
  77.9 5.1 %collective-permute-done.26 = bf16[128,2048]{1,0:T(8,128)(2,1)S(1)} collective-permute-done((bf16[128,2048]{1,0:T(8,128)(2,1)S(1)}, bf16[128,2048]{1,0:T(8,128)(2,1)S(1)}, u32[]{:S(2)}, u32[]{:S(2)}) %collective-permute-start.26) | collective-permute-done | bytes 524320 | tf_op jit(solution)/shard_map/ppermute | solution.py:252
  83.0 0.2 add_convert_fusion
  83.2 2.1 %collective-permute-start.27 = (bf16[128,2048]{1,0:T(8,128)(2,1)S(1)}, bf16[128,2048]{1,0:T(8,128)(2,1)S(1)}, u32[]{:S(2)}, u32[]{:S(2)}) collective-permute-start(bf16[128,2048]{1,0:T(8,128)(2,1)S(1)} %add_convert_fusion), channel_id=1, source_target_pairs={{0,4},{5,1},{4,8},{9,5},{8,12},{13,9},{12,14},{15,13},{14,10},{11,... | collective-permute-start | bytes 1572872 | tf_op jit(solution)/shard_map/ppermute | solution.py:252
  85.4 3.3 %visit.10 = (f32[128,2048]{1,0:T(8,128)S(1)}, bf16[128,2048]{1,0:T(8,128)(2,1)S(1)}) custom-call(s32[1]{0:T(128)} %found.1.mine_ref, bf16[128,2176]{1,0:T(8,128)(2,1)S(1)} %collective-permute-done.10.near_ref, bf16[128,2176]{1,0:T(8,128)(2,1)S(1)} %collective-permute-done.11.far_ref, bf16[1,2,2048,768]{3,2,1,0:T(8,128)(2,1)S(1)} %get-tuple-element.25.in_ref, ...), custom_call_target="tpu_custom_call" | custom-call | flops 2415919104 | bytes 1572864 | tf_op jit(solution)/shard_map/visit/pallas_call | solution.py:196
  88.7 0.1 collective-permute-start.12
  88.8 0.5 collective-permute-start
  89.3 3.3 %visit.9 = (f32[128,2048]{1,0:T(8,128)S(1)}, bf16[128,2048]{1,0:T(8,128)(2,1)S(1)}) custom-call(s32[1]{0:T(128)} %found.1.mine_ref, bf16[128,2176]{1,0:T(8,128)(2,1)S(1)} %collective-permute-done.2.near_ref, bf16[128,2176]{1,0:T(8,128)(2,1)S(1)} %collective-permute-done.3.far_ref, bf16[1,2,2048,768]{3,2,1,0:T(8,128)(2,1)S(1)} %get-tuple-element.25.in_ref, ...), custom_call_target="tpu_custom_call" | custom-call | flops 2415919104 | bytes 1572864 | tf_op jit(solution)/shard_map/visit/pallas_call | solution.py:196
  92.6 0.1 collective-permute-start.4
  92.8 0.2 add_convert_fusion.10
  93.0 1.8 %collective-permute-start.28 = (bf16[64,2048]{1,0:T(8,128)(2,1)S(1)}, bf16[64,2048]{1,0:T(8,128)(2,1)S(1)}, u32[]{:S(2)}, u32[]{:S(2)}) collective-permute-start(bf16[64,2048]{1,0:T(8,128)(2,1)S(1)} %get-tuple-element.45), channel_id=1, source_target_pairs={{0,4},{5,1},{4,8},{9,5},{8,12},{13,9},{12,14},{15,13},{14,10},{11,... | collective-permute-start | bytes 786440 | tf_op jit(solution)/shard_map/ppermute | solution.py:257
  94.8 1.6 %collective-permute-start.30 = (bf16[64,2048]{1,0:T(8,128)(2,1)S(1)}, bf16[64,2048]{1,0:T(8,128)(2,1)S(1)}, u32[]{:S(2)}, u32[]{:S(2)}) collective-permute-start(bf16[64,2048]{1,0:T(8,128)(2,1)S(1)} %get-tuple-element.46), channel_id=1, source_target_pairs={{0,4},{5,1},{4,8},{9,5},{8,12},{13,9},{12,14},{15,13},{14,10},{11,... | collective-permute-start | bytes 786440 | tf_op jit(solution)/shard_map/ppermute | solution.py:257
  96.4 3.3 %visit.8 = (f32[128,2048]{1,0:T(8,128)S(1)}, bf16[128,2048]{1,0:T(8,128)(2,1)S(1)}) custom-call(s32[1]{0:T(128)} %found.1.mine_ref, bf16[128,2176]{1,0:T(8,128)(2,1)S(1)} %packed.1.near_ref, bf16[128,2176]{1,0:T(8,128)(2,1)S(1)} %collective-permute-done.far_ref, bf16[1,2,2048,768]{3,2,1,0:T(8,128)(2,1)S(1)} %get-tuple-element.25.in_ref, ...), custom_call_target="tpu_custom_call" | custom-call | flops 2415919104 | bytes 1572864 | tf_op jit(solution)/shard_map/visit/pallas_call | solution.py:196
  99.7 0.1 collective-permute-start.1
  99.8 2.4 %collective-permute-done.30 = bf16[64,2048]{1,0:T(8,128)(2,1)S(1)} collective-permute-done((bf16[64,2048]{1,0:T(8,128)(2,1)S(1)}, bf16[64,2048]{1,0:T(8,128)(2,1)S(1)}, u32[]{:S(2)}, u32[]{:S(2)}) %collective-permute-start.30) | collective-permute-done | bytes 262176 | tf_op jit(solution)/shard_map/ppermute | solution.py:257
  102.2 0.2 add_convert_fusion.9
  102.4 1.8 %collective-permute-start.29 = (bf16[64,2048]{1,0:T(8,128)(2,1)S(1)}, bf16[64,2048]{1,0:T(8,128)(2,1)S(1)}, u32[]{:S(2)}, u32[]{:S(2)}) collective-permute-start(bf16[64,2048]{1,0:T(8,128)(2,1)S(1)} %get-tuple-element.49), channel_id=1, source_target_pairs={{0,4},{5,1},{4,8},{9,5},{8,12},{13,9},{12,14},{15,13},{14,10},{11,... | collective-permute-start | bytes 786440 | tf_op jit(solution)/shard_map/ppermute | solution.py:257
  104.2 1.6 %collective-permute-start.31 = (bf16[64,2048]{1,0:T(8,128)(2,1)S(1)}, bf16[64,2048]{1,0:T(8,128)(2,1)S(1)}, u32[]{:S(2)}, u32[]{:S(2)}) collective-permute-start(bf16[64,2048]{1,0:T(8,128)(2,1)S(1)} %get-tuple-element.50), channel_id=1, source_target_pairs={{0,4},{5,1},{4,8},{9,5},{8,12},{13,9},{12,14},{15,13},{14,10},{11,... | collective-permute-start | bytes 786440 | tf_op jit(solution)/shard_map/ppermute | solution.py:257
  105.8 3.0 %collective-permute-done.29 = bf16[64,2048]{1,0:T(8,128)(2,1)S(1)} collective-permute-done((bf16[64,2048]{1,0:T(8,128)(2,1)S(1)}, bf16[64,2048]{1,0:T(8,128)(2,1)S(1)}, u32[]{:S(2)}, u32[]{:S(2)}) %collective-permute-start.29) | collective-permute-done | bytes 262176 | tf_op jit(solution)/shard_map/ppermute | solution.py:257
  108.8 2.8 %collective-permute-done.31 = bf16[64,2048]{1,0:T(8,128)(2,1)S(1)} collective-permute-done((bf16[64,2048]{1,0:T(8,128)(2,1)S(1)}, bf16[64,2048]{1,0:T(8,128)(2,1)S(1)}, u32[]{:S(2)}, u32[]{:S(2)}) %collective-permute-start.31) | collective-permute-done | bytes 262176 | tf_op jit(solution)/shard_map/ppermute | solution.py:257
  111.6 0.2 add_convert_fusion.8
  111.8 0.8 pad_maximum_fusion
  (22 shorter events, 0.1 us)
Async XLA Ops:
  1.3 10.6 %collective-permute-start.5 = (bf16[128,2176]{1,0:T(8,128)(2,1)S(1)}, bf16[128,2176]{1,0:T(8,128)(2,1)S(1)}, u32[]{:S(2)}, u32[]{:S(2)}) collective-permute-start(bf16[128,2176]{1,0:T(8,128)(2,1)S(1)} %packed.1.near_ref), channel_id=1, source_target_pairs={{0,4},{5,1},{4,8},{9,5},{8,12},{13,9},{12,14},{15,13},{14,10},{11,... | collective-permute-start | bytes 1671176 | tf_op jit(solution)/shard_map/ppermute | solution.py:242
  11.9 7.8 %collective-permute-start.21 = (bf16[128,2176]{1,0:T(8,128)(2,1)S(1)}, bf16[128,2176]{1,0:T(8,128)(2,1)S(1)}, u32[]{:S(2)}, u32[]{:S(2)}) collective-permute-start(bf16[128,2176]{1,0:T(8,128)(2,1)S(1)} %collective-permute-done.5.near_ref), channel_id=1, source_target_pairs={{0,1},{1,0},{2,3},{3,2},{4,5},{5,4},{6,7},{7,6},{8,9},{9,8},{10,11... | collective-permute-start | bytes 1671176 | tf_op jit(solution)/shard_map/ppermute | solution.py:240
  11.9 0.7 copy-start
  17.6 9.6 %collective-permute-start.6 = (bf16[128,2176]{1,0:T(8,128)(2,1)S(1)}, bf16[128,2176]{1,0:T(8,128)(2,1)S(1)}, u32[]{:S(2)}, u32[]{:S(2)}) collective-permute-start(bf16[128,2176]{1,0:T(8,128)(2,1)S(1)} %collective-permute-done.5.near_ref), channel_id=1, source_target_pairs={{0,4},{5,1},{4,8},{9,5},{8,12},{13,9},{12,14},{15,13},{14,10},{11,... | collective-permute-start | bytes 1671176 | tf_op jit(solution)/shard_map/ppermute | solution.py:242
  23.0 6.2 %collective-permute-start.22 = (bf16[128,2048]{1,0:T(8,128)(2,1)S(1)}, bf16[128,2048]{1,0:T(8,128)(2,1)S(1)}, u32[]{:S(2)}, u32[]{:S(2)}) collective-permute-start(bf16[128,2048]{1,0:T(8,128)(2,1)S(1)} %get-tuple-element.44), channel_id=1, source_target_pairs={{0,1},{1,0},{2,3},{3,2},{4,5},{5,4},{6,7},{7,6},{8,9},{9,8},{10,11... | collective-permute-start | bytes 1572872 | tf_op jit(solution)/shard_map/ppermute | solution.py:244
  27.2 3.8 %collective-permute-start.19 = (bf16[128,2176]{1,0:T(8,128)(2,1)S(1)}, bf16[128,2176]{1,0:T(8,128)(2,1)S(1)}, u32[]{:S(2)}, u32[]{:S(2)}) collective-permute-start(bf16[128,2176]{1,0:T(8,128)(2,1)S(1)} %collective-permute-done.6.near_ref), channel_id=1, source_target_pairs={{0,1},{1,0},{2,3},{3,2},{4,5},{5,4},{6,7},{7,6},{8,9},{9,8},{10,11... | collective-permute-start | bytes 1671176 | tf_op jit(solution)/shard_map/ppermute | solution.py:240
  27.2 9.5 %collective-permute-start.7 = (bf16[128,2176]{1,0:T(8,128)(2,1)S(1)}, bf16[128,2176]{1,0:T(8,128)(2,1)S(1)}, u32[]{:S(2)}, u32[]{:S(2)}) collective-permute-start(bf16[128,2176]{1,0:T(8,128)(2,1)S(1)} %collective-permute-done.6.near_ref), channel_id=1, source_target_pairs={{0,4},{5,1},{4,8},{9,5},{8,12},{13,9},{12,14},{15,13},{14,10},{11,... | collective-permute-start | bytes 1671176 | tf_op jit(solution)/shard_map/ppermute | solution.py:242
  29.4 12.9 %collective-permute-start.23 = (bf16[128,2048]{1,0:T(8,128)(2,1)S(1)}, bf16[128,2048]{1,0:T(8,128)(2,1)S(1)}, u32[]{:S(2)}, u32[]{:S(2)}) collective-permute-start(bf16[128,2048]{1,0:T(8,128)(2,1)S(1)} %add_convert_fusion.4), channel_id=1, source_target_pairs={{0,4},{5,1},{4,8},{9,5},{8,12},{13,9},{12,14},{15,13},{14,10},{11,... | collective-permute-start | bytes 1572872 | tf_op jit(solution)/shard_map/ppermute | solution.py:252
  34.3 8.0 %collective-permute-start.20 = (bf16[128,2048]{1,0:T(8,128)(2,1)S(1)}, bf16[128,2048]{1,0:T(8,128)(2,1)S(1)}, u32[]{:S(2)}, u32[]{:S(2)}) collective-permute-start(bf16[128,2048]{1,0:T(8,128)(2,1)S(1)} %get-tuple-element.42), channel_id=1, source_target_pairs={{0,1},{1,0},{2,3},{3,2},{4,5},{5,4},{6,7},{7,6},{8,9},{9,8},{10,11... | collective-permute-start | bytes 1572872 | tf_op jit(solution)/shard_map/ppermute | solution.py:244
  36.7 8.0 %collective-permute-start.17 = (bf16[128,2176]{1,0:T(8,128)(2,1)S(1)}, bf16[128,2176]{1,0:T(8,128)(2,1)S(1)}, u32[]{:S(2)}, u32[]{:S(2)}) collective-permute-start(bf16[128,2176]{1,0:T(8,128)(2,1)S(1)} %collective-permute-done.7.near_ref), channel_id=1, source_target_pairs={{0,1},{1,0},{2,3},{3,2},{4,5},{5,4},{6,7},{7,6},{8,9},{9,8},{10,11... | collective-permute-start | bytes 1671176 | tf_op jit(solution)/shard_map/ppermute | solution.py:240
  36.7 11.6 %collective-permute-start.8 = (bf16[128,2176]{1,0:T(8,128)(2,1)S(1)}, bf16[128,2176]{1,0:T(8,128)(2,1)S(1)}, u32[]{:S(2)}, u32[]{:S(2)}) collective-permute-start(bf16[128,2176]{1,0:T(8,128)(2,1)S(1)} %collective-permute-done.7.near_ref), channel_id=1, source_target_pairs={{0,4},{5,1},{4,8},{9,5},{8,12},{13,9},{12,14},{15,13},{14,10},{11,... | collective-permute-start | bytes 1671176 | tf_op jit(solution)/shard_map/ppermute | solution.py:242
  42.5 11.4 %collective-permute-start.24 = (bf16[128,2048]{1,0:T(8,128)(2,1)S(1)}, bf16[128,2048]{1,0:T(8,128)(2,1)S(1)}, u32[]{:S(2)}, u32[]{:S(2)}) collective-permute-start(bf16[128,2048]{1,0:T(8,128)(2,1)S(1)} %add_convert_fusion.3), channel_id=1, source_target_pairs={{0,4},{5,1},{4,8},{9,5},{8,12},{13,9},{12,14},{15,13},{14,10},{11,... | collective-permute-start | bytes 1572872 | tf_op jit(solution)/shard_map/ppermute | solution.py:252
  48.0 5.9 %collective-permute-start.18 = (bf16[128,2048]{1,0:T(8,128)(2,1)S(1)}, bf16[128,2048]{1,0:T(8,128)(2,1)S(1)}, u32[]{:S(2)}, u32[]{:S(2)}) collective-permute-start(bf16[128,2048]{1,0:T(8,128)(2,1)S(1)} %get-tuple-element.40), channel_id=1, source_target_pairs={{0,1},{1,0},{2,3},{3,2},{4,5},{5,4},{6,7},{7,6},{8,9},{9,8},{10,11... | collective-permute-start | bytes 1572872 | tf_op jit(solution)/shard_map/ppermute | solution.py:244
  48.3 8.0 %collective-permute-start.15 = (bf16[128,2176]{1,0:T(8,128)(2,1)S(1)}, bf16[128,2176]{1,0:T(8,128)(2,1)S(1)}, u32[]{:S(2)}, u32[]{:S(2)}) collective-permute-start(bf16[128,2176]{1,0:T(8,128)(2,1)S(1)} %collective-permute-done.8.near_ref), channel_id=1, source_target_pairs={{0,1},{1,0},{2,3},{3,2},{4,5},{5,4},{6,7},{7,6},{8,9},{9,8},{10,11... | collective-permute-start | bytes 1671176 | tf_op jit(solution)/shard_map/ppermute | solution.py:240
  48.6 11.3 %collective-permute-start.9 = (bf16[128,2176]{1,0:T(8,128)(2,1)S(1)}, bf16[128,2176]{1,0:T(8,128)(2,1)S(1)}, u32[]{:S(2)}, u32[]{:S(2)}) collective-permute-start(bf16[128,2176]{1,0:T(8,128)(2,1)S(1)} %collective-permute-done.8.near_ref), channel_id=1, source_target_pairs={{0,4},{5,1},{4,8},{9,5},{8,12},{13,9},{12,14},{15,13},{14,10},{11,... | collective-permute-start | bytes 1671176 | tf_op jit(solution)/shard_map/ppermute | solution.py:242
  54.1 13.6 %collective-permute-start.25 = (bf16[128,2048]{1,0:T(8,128)(2,1)S(1)}, bf16[128,2048]{1,0:T(8,128)(2,1)S(1)}, u32[]{:S(2)}, u32[]{:S(2)}) collective-permute-start(bf16[128,2048]{1,0:T(8,128)(2,1)S(1)} %add_convert_fusion.2), channel_id=1, source_target_pairs={{0,4},{5,1},{4,8},{9,5},{8,12},{13,9},{12,14},{15,13},{14,10},{11,... | collective-permute-start | bytes 1572872 | tf_op jit(solution)/shard_map/ppermute | solution.py:252
  59.6 8.1 %collective-permute-start.16 = (bf16[128,2048]{1,0:T(8,128)(2,1)S(1)}, bf16[128,2048]{1,0:T(8,128)(2,1)S(1)}, u32[]{:S(2)}, u32[]{:S(2)}) collective-permute-start(bf16[128,2048]{1,0:T(8,128)(2,1)S(1)} %get-tuple-element.38), channel_id=1, source_target_pairs={{0,1},{1,0},{2,3},{3,2},{4,5},{5,4},{6,7},{7,6},{8,9},{9,8},{10,11... | collective-permute-start | bytes 1572872 | tf_op jit(solution)/shard_map/ppermute | solution.py:244
  59.9 10.6 %collective-permute-start.13 = (bf16[128,2176]{1,0:T(8,128)(2,1)S(1)}, bf16[128,2176]{1,0:T(8,128)(2,1)S(1)}, u32[]{:S(2)}, u32[]{:S(2)}) collective-permute-start(bf16[128,2176]{1,0:T(8,128)(2,1)S(1)} %collective-permute-done.9.near_ref), channel_id=1, source_target_pairs={{0,1},{1,0},{2,3},{3,2},{4,5},{5,4},{6,7},{7,6},{8,9},{9,8},{10,11... | collective-permute-start | bytes 1671176 | tf_op jit(solution)/shard_map/ppermute | solution.py:240
  60.2 17.3 %collective-permute-start.2 = (bf16[128,2176]{1,0:T(8,128)(2,1)S(1)}, bf16[128,2176]{1,0:T(8,128)(2,1)S(1)}, u32[]{:S(2)}, u32[]{:S(2)}) collective-permute-start(bf16[128,2176]{1,0:T(8,128)(2,1)S(1)} %packed.1.near_ref), channel_id=1, source_target_pairs={{4,0},{1,5},{8,4},{5,9},{12,8},{9,13},{14,12},{13,15},{10,14},{15,... | collective-permute-start | bytes 1671176 | tf_op jit(solution)/shard_map/ppermute | solution.py:236
  61.9 15.5 %collective-permute-start.10 = (bf16[128,2176]{1,0:T(8,128)(2,1)S(1)}, bf16[128,2176]{1,0:T(8,128)(2,1)S(1)}, u32[]{:S(2)}, u32[]{:S(2)}) collective-permute-start(bf16[128,2176]{1,0:T(8,128)(2,1)S(1)} %collective-permute-done.9.near_ref), channel_id=1, source_target_pairs={{0,4},{5,1},{4,8},{9,5},{8,12},{13,9},{12,14},{15,13},{14,10},{11,... | collective-permute-start | bytes 1671176 | tf_op jit(solution)/shard_map/ppermute | solution.py:242
  67.9 15.1 %collective-permute-start.26 = (bf16[128,2048]{1,0:T(8,128)(2,1)S(1)}, bf16[128,2048]{1,0:T(8,128)(2,1)S(1)}, u32[]{:S(2)}, u32[]{:S(2)}) collective-permute-start(bf16[128,2048]{1,0:T(8,128)(2,1)S(1)} %add_convert_fusion.1), channel_id=1, source_target_pairs={{0,4},{5,1},{4,8},{9,5},{8,12},{13,9},{12,14},{15,13},{14,10},{11,... | collective-permute-start | bytes 1572872 | tf_op jit(solution)/shard_map/ppermute | solution.py:252
  73.8 9.2 %collective-permute-start.14 = (bf16[128,2048]{1,0:T(8,128)(2,1)S(1)}, bf16[128,2048]{1,0:T(8,128)(2,1)S(1)}, u32[]{:S(2)}, u32[]{:S(2)}) collective-permute-start(bf16[128,2048]{1,0:T(8,128)(2,1)S(1)} %get-tuple-element.36), channel_id=1, source_target_pairs={{0,1},{1,0},{2,3},{3,2},{4,5},{5,4},{6,7},{7,6},{8,9},{9,8},{10,11... | collective-permute-start | bytes 1572872 | tf_op jit(solution)/shard_map/ppermute | solution.py:244
  77.4 7.9 %collective-permute-start.11 = (bf16[128,2176]{1,0:T(8,128)(2,1)S(1)}, bf16[128,2176]{1,0:T(8,128)(2,1)S(1)}, u32[]{:S(2)}, u32[]{:S(2)}) collective-permute-start(bf16[128,2176]{1,0:T(8,128)(2,1)S(1)} %collective-permute-done.10.near_ref), channel_id=1, source_target_pairs={{0,1},{1,0},{2,3},{3,2},{4,5},{5,4},{6,7},{7,6},{8,9},{9,8},{10,11... | collective-permute-start | bytes 1671176 | tf_op jit(solution)/shard_map/ppermute | solution.py:240
  77.4 11.9 %collective-permute-start.3 = (bf16[128,2176]{1,0:T(8,128)(2,1)S(1)}, bf16[128,2176]{1,0:T(8,128)(2,1)S(1)}, u32[]{:S(2)}, u32[]{:S(2)}) collective-permute-start(bf16[128,2176]{1,0:T(8,128)(2,1)S(1)} %collective-permute-done.2.near_ref), channel_id=1, source_target_pairs={{0,1},{1,0},{2,3},{3,2},{4,5},{5,4},{6,7},{7,6},{8,9},{9,8},{10,11... | collective-permute-start | bytes 1671176 | tf_op jit(solution)/shard_map/ppermute | solution.py:240
  83.2 9.5 %collective-permute-start.27 = (bf16[128,2048]{1,0:T(8,128)(2,1)S(1)}, bf16[128,2048]{1,0:T(8,128)(2,1)S(1)}, u32[]{:S(2)}, u32[]{:S(2)}) collective-permute-start(bf16[128,2048]{1,0:T(8,128)(2,1)S(1)} %add_convert_fusion), channel_id=1, source_target_pairs={{0,4},{5,1},{4,8},{9,5},{8,12},{13,9},{12,14},{15,13},{14,10},{11,... | collective-permute-start | bytes 1572872 | tf_op jit(solution)/shard_map/ppermute | solution.py:252
  88.7 4.1 %collective-permute-start.12 = (bf16[128,2048]{1,0:T(8,128)(2,1)S(1)}, bf16[128,2048]{1,0:T(8,128)(2,1)S(1)}, u32[]{:S(2)}, u32[]{:S(2)}) collective-permute-start(bf16[128,2048]{1,0:T(8,128)(2,1)S(1)} %get-tuple-element.34), channel_id=1, source_target_pairs={{0,1},{1,0},{2,3},{3,2},{4,5},{5,4},{6,7},{7,6},{8,9},{9,8},{10,11... | collective-permute-start | bytes 1572872 | tf_op jit(solution)/shard_map/ppermute | solution.py:244
  88.8 7.6 %collective-permute-start = (bf16[128,2176]{1,0:T(8,128)(2,1)S(1)}, bf16[128,2176]{1,0:T(8,128)(2,1)S(1)}, u32[]{:S(2)}, u32[]{:S(2)}) collective-permute-start(bf16[128,2176]{1,0:T(8,128)(2,1)S(1)} %packed.1.near_ref), channel_id=1, source_target_pairs={{0,1},{1,0},{2,3},{3,2},{4,5},{5,4},{6,7},{7,6},{8,9},{9,8},{10,11... | collective-permute-start | bytes 1671176 | tf_op jit(solution)/shard_map/ppermute | solution.py:240
  92.6 7.2 %collective-permute-start.4 = (bf16[128,2048]{1,0:T(8,128)(2,1)S(1)}, bf16[128,2048]{1,0:T(8,128)(2,1)S(1)}, u32[]{:S(2)}, u32[]{:S(2)}) collective-permute-start(bf16[128,2048]{1,0:T(8,128)(2,1)S(1)} %get-tuple-element.32), channel_id=1, source_target_pairs={{0,1},{1,0},{2,3},{3,2},{4,5},{5,4},{6,7},{7,6},{8,9},{9,8},{10,11... | collective-permute-start | bytes 1572872 | tf_op jit(solution)/shard_map/ppermute | solution.py:244
  93.0 6.8 %collective-permute-start.28 = (bf16[64,2048]{1,0:T(8,128)(2,1)S(1)}, bf16[64,2048]{1,0:T(8,128)(2,1)S(1)}, u32[]{:S(2)}, u32[]{:S(2)}) collective-permute-start(bf16[64,2048]{1,0:T(8,128)(2,1)S(1)} %get-tuple-element.45), channel_id=1, source_target_pairs={{0,4},{5,1},{4,8},{9,5},{8,12},{13,9},{12,14},{15,13},{14,10},{11,... | collective-permute-start | bytes 786440 | tf_op jit(solution)/shard_map/ppermute | solution.py:257
  94.8 7.4 %collective-permute-start.30 = (bf16[64,2048]{1,0:T(8,128)(2,1)S(1)}, bf16[64,2048]{1,0:T(8,128)(2,1)S(1)}, u32[]{:S(2)}, u32[]{:S(2)}) collective-permute-start(bf16[64,2048]{1,0:T(8,128)(2,1)S(1)} %get-tuple-element.46), channel_id=1, source_target_pairs={{0,4},{5,1},{4,8},{9,5},{8,12},{13,9},{12,14},{15,13},{14,10},{11,... | collective-permute-start | bytes 786440 | tf_op jit(solution)/shard_map/ppermute | solution.py:257
  99.7 6.1 %collective-permute-start.1 = (bf16[128,2048]{1,0:T(8,128)(2,1)S(1)}, bf16[128,2048]{1,0:T(8,128)(2,1)S(1)}, u32[]{:S(2)}, u32[]{:S(2)}) collective-permute-start(bf16[128,2048]{1,0:T(8,128)(2,1)S(1)} %get-tuple-element.30), channel_id=1, source_target_pairs={{0,1},{1,0},{2,3},{3,2},{4,5},{5,4},{6,7},{7,6},{8,9},{9,8},{10,11... | collective-permute-start | bytes 1572872 | tf_op jit(solution)/shard_map/ppermute | solution.py:244
  102.4 6.4 %collective-permute-start.29 = (bf16[64,2048]{1,0:T(8,128)(2,1)S(1)}, bf16[64,2048]{1,0:T(8,128)(2,1)S(1)}, u32[]{:S(2)}, u32[]{:S(2)}) collective-permute-start(bf16[64,2048]{1,0:T(8,128)(2,1)S(1)} %get-tuple-element.49), channel_id=1, source_target_pairs={{0,4},{5,1},{4,8},{9,5},{8,12},{13,9},{12,14},{15,13},{14,10},{11,... | collective-permute-start | bytes 786440 | tf_op jit(solution)/shard_map/ppermute | solution.py:257
  104.2 7.4 %collective-permute-start.31 = (bf16[64,2048]{1,0:T(8,128)(2,1)S(1)}, bf16[64,2048]{1,0:T(8,128)(2,1)S(1)}, u32[]{:S(2)}, u32[]{:S(2)}) collective-permute-start(bf16[64,2048]{1,0:T(8,128)(2,1)S(1)} %get-tuple-element.50), channel_id=1, source_target_pairs={{0,4},{5,1},{4,8},{9,5},{8,12},{13,9},{12,14},{15,13},{14,10},{11,... | collective-permute-start | bytes 786440 | tf_op jit(solution)/shard_map/ppermute | solution.py:257

commit v6 on v5

--- a/solution.py
+++ b/solution.py
@@ -221,7 +221,7 @@
     devices = lax.axis_size("tok")
     ring, chips = ring_pairs(devices)
     swap = [(i, i ^ 1) for i in range(devices)]
-    half = tokens.shape[0] // 2
+    cut = tokens.shape[0] // 16 * 7
     block = packed(tokens, norm_gain, expert_ids, gate_weights, experts)
     blocks = loaded(in_q, in_scale, down_q, down_scale)
     mine = pl.pallas_call(
@@ -243,19 +243,19 @@
         part, lent = visit(mine, here, other, experts, *blocks)
         parts.append((part, lax.ppermute(lent, "tok", swap)))
 
-    def summed(step, cut, arrived):
-        part, lent = (x[cut].astype(jnp.float32) for x in parts[step])
+    def summed(step, rows, arrived):
+        part, lent = (x[rows].astype(jnp.float32) for x in parts[step])
         return (part + lent + arrived.astype(jnp.float32)).astype(jnp.bfloat16)
 
     total = jnp.zeros((), jnp.bfloat16)
     for step in range(1, chips - 2):
         total = lax.ppermute(summed(step, slice(None), total), "tok", ring)
-    halves = {"a": slice(0, half), "b": slice(half, None)}
-    totals = {name: total[cut] for name, cut in halves.items()}
+    shares = {"a": slice(0, cut), "b": slice(cut, None)}
+    totals = {name: total[rows] for name, rows in shares.items()}
     for step in range(chips - 2, chips):
-        for name, cut in halves.items():
-            totals[name] = lax.ppermute(summed(step, cut, totals[name]), "tok", ring)
-    return jnp.concatenate([summed(0, cut, totals[name]) for name, cut in halves.items()])
+        for name, rows in shares.items():
+            totals[name] = lax.ppermute(summed(step, rows, totals[name]), "tok", ring)
+    return jnp.concatenate([summed(0, rows, totals[name]) for name, rows in shares.items()])
 
 
 def solution(mesh):

time: 113 us -> 114 us (level)
  transfers between devices with their start and end apart: 32 -> 32, of which waited for: 13 -> 14; matrix products, arithmetic and copies ran while one was open for 1% -> 1% of each run, Pallas kernels for 28% -> 28%
where the time goes in v6:
time: 114 us; the launch traced here: 113 us
  waiting for transfers between devices  44.5 us (39%)
  Pallas kernels  33 us (29%)
  starting transfers between devices  32.7 us (29%)
  other arithmetic  2.3 us (2%)
    pallas_call x8, Pallas kernels, visit(): pl.pallas_call(functools.partial(visit_kernel, experts), out_shape=(jax.S...  26.6 us
    ppermute x5, waiting for transfers between devices, circulated(): total = lax.ppermute(summed(step, slice(None), total), 'tok', ring)  17.7 us
    ppermute x6, waiting for transfers between devices, circulated(): block = lax.ppermute(here, 'tok', ring)  17.5 us
    ppermute x6, starting transfers between devices, circulated(): block = lax.ppermute(here, 'tok', ring)  11.5 us
    ppermute x5, starting transfers between devices, circulated(): total = lax.ppermute(summed(step, slice(None), total), 'tok', ring)  10.6 us
    ppermute x4, waiting for transfers between devices, circulated(): totals[name] = lax.ppermute(summed(step, rows, totals[name]), 'tok', ring)  9.2 us
    ppermute x4, starting transfers between devices, circulated(): totals[name] = lax.ppermute(summed(step, rows, totals[name]), 'tok', ring)  6.53 us
    pallas_call x1, Pallas kernels, loaded(): pl.pallas_call(functools.partial(loaded_kernel, count), out_shape=tuple((...  3.77 us
  transfers between devices with their start and end apart: 32, of which 14 were waited for; matrix products, arithmetic and copies ran while one was open for 1% of the time, Pallas kernels for 28%

profile of v6, /device:TPU:0, one launch (start us, length us, event | category | flops | bytes accessed | tf_op | source)
XLA Modules:
  0.0 113.3 jit_solution(10264881861342374979)
XLA Ops:
  0.0 1.3 %packed.1.near_ref = bf16[128,2176]{1,0:T(8,128)(2,1)S(1)} custom-call(bf16[128,2048]{1,0:T(8,128)(2,1)} %tokens_hbm.1, f32[1,2048]{1,0:T(1,128)} %bitcast.3, s32[8,128]{1,0:T(8,128)} %bitcast.4, f32[8,128]{1,0:T(8,128)} %bitcast.5), custom_call_target="tpu_custom_call" | custom-call | tf_op jit(solution)/shard_map/packed/pallas_call | solution.py:109
  1.3 3.1 %collective-permute-start.5 = (bf16[128,2176]{1,0:T(8,128)(2,1)S(1)}, bf16[128,2176]{1,0:T(8,128)(2,1)S(1)}, u32[]{:S(2)}, u32[]{:S(2)}) collective-permute-start(bf16[128,2176]{1,0:T(8,128)(2,1)S(1)} %packed.1.near_ref), channel_id=1, source_target_pairs={{0,4},{5,1},{4,8},{9,5},{8,12},{13,9},{12,14},{15,13},{14,10},{11,... | collective-permute-start | bytes 1671176 | tf_op jit(solution)/shard_map/ppermute | solution.py:242
  4.4 7.5 %collective-permute-done.5.near_ref = bf16[128,2176]{1,0:T(8,128)(2,1)S(1)} collective-permute-done((bf16[128,2176]{1,0:T(8,128)(2,1)S(1)}, bf16[128,2176]{1,0:T(8,128)(2,1)S(1)}, u32[]{:S(2)}, u32[]{:S(2)}) %collective-permute-start.5) | collective-permute-done | bytes 557088 | tf_op jit(solution)/shard_map/ppermute | solution.py:242
  11.9 0.7 copy-done
  12.6 1.2 %found.1.mine_ref = s32[1]{0:T(128)} custom-call(s32[16]{0:T(128)S(1)} %copy-done), custom_call_target="tpu_custom_call" | custom-call | tf_op jit(solution)/shard_map/found/pallas_call | solution.py:227
  13.8 3.8 %loaded.1 = (bf16[1,2,2048,768]{3,2,1,0:T(8,128)(2,1)S(1)}, bf16[1,2,768]{2,1,0:T(2,128)(2,1)S(1)}, bf16[1,768,2048]{2,1,0:T(8,128)(2,1)S(1)}, bf16[1,2048]{1,0:T(2,128)(2,1)S(1)}) custom-call(bf16[1,2,2048,768]{3,2,1,0:T(8,128)(2,1)} %refs_0_.1, bf16[1,2,768]{2,1,0:T(2,128)(2,1)} %refs_1_.1, bf16[1,768,2048]{2,1,0:T(8,128)(2,1)} %refs_2_.1, ...), custom_call_target="tpu_custom_call" | custom-call | bytes 9444352 | tf_op jit(solution)/shard_map/loaded/pallas_call | solution.py:147
  17.6 2.1 %collective-permute-start.6 = (bf16[128,2176]{1,0:T(8,128)(2,1)S(1)}, bf16[128,2176]{1,0:T(8,128)(2,1)S(1)}, u32[]{:S(2)}, u32[]{:S(2)}) collective-permute-start(bf16[128,2176]{1,0:T(8,128)(2,1)S(1)} %collective-permute-done.5.near_ref), channel_id=1, source_target_pairs={{0,4},{5,1},{4,8},{9,5},{8,12},{13,9},{12,14},{15,13},{14,10},{11,... | collective-permute-start | bytes 1671176 | tf_op jit(solution)/shard_map/ppermute | solution.py:242
  19.7 3.3 %visit.15 = (f32[128,2048]{1,0:T(8,128)S(1)}, bf16[128,2048]{1,0:T(8,128)(2,1)S(1)}) custom-call(s32[1]{0:T(128)} %found.1.mine_ref, bf16[128,2176]{1,0:T(8,128)(2,1)S(1)} %collective-permute-done.5.near_ref, bf16[128,2176]{1,0:T(8,128)(2,1)S(1)} %collective-permute-done.21.far_ref, bf16[1,2,2048,768]{3,2,1,0:T(8,128)(2,1)S(1)} %get-tuple-element.25.in_ref, ...), custom_call_target="tpu_custom_call" | custom-call | flops 2415919104 | bytes 1572864 | tf_op jit(solution)/shard_map/visit/pallas_call | solution.py:196
  23.0 0.2 collective-permute-start.22
  23.3 3.9 %collective-permute-done.6.near_ref = bf16[128,2176]{1,0:T(8,128)(2,1)S(1)} collective-permute-done((bf16[128,2176]{1,0:T(8,128)(2,1)S(1)}, bf16[128,2176]{1,0:T(8,128)(2,1)S(1)}, u32[]{:S(2)}, u32[]{:S(2)}) %collective-permute-start.6) | collective-permute-done | bytes 557088 | tf_op jit(solution)/shard_map/ppermute | solution.py:242
  27.2 2.1 %collective-permute-start.7 = (bf16[128,2176]{1,0:T(8,128)(2,1)S(1)}, bf16[128,2176]{1,0:T(8,128)(2,1)S(1)}, u32[]{:S(2)}, u32[]{:S(2)}) collective-permute-start(bf16[128,2176]{1,0:T(8,128)(2,1)S(1)} %collective-permute-done.6.near_ref), channel_id=1, source_target_pairs={{0,4},{5,1},{4,8},{9,5},{8,12},{13,9},{12,14},{15,13},{14,10},{11,... | collective-permute-start | bytes 1671176 | tf_op jit(solution)/shard_map/ppermute | solution.py:242
  29.2 0.1 add_convert_fusion.4
  29.4 1.6 %collective-permute-start.23 = (bf16[128,2048]{1,0:T(8,128)(2,1)S(1)}, bf16[128,2048]{1,0:T(8,128)(2,1)S(1)}, u32[]{:S(2)}, u32[]{:S(2)}) collective-permute-start(bf16[128,2048]{1,0:T(8,128)(2,1)S(1)} %add_convert_fusion.4), channel_id=1, source_target_pairs={{0,4},{5,1},{4,8},{9,5},{8,12},{13,9},{12,14},{15,13},{14,10},{11,... | collective-permute-start | bytes 1572872 | tf_op jit(solution)/shard_map/ppermute | solution.py:252
  31.0 3.3 %visit.14 = (f32[128,2048]{1,0:T(8,128)S(1)}, bf16[128,2048]{1,0:T(8,128)(2,1)S(1)}) custom-call(s32[1]{0:T(128)} %found.1.mine_ref, bf16[128,2176]{1,0:T(8,128)(2,1)S(1)} %collective-permute-done.6.near_ref, bf16[128,2176]{1,0:T(8,128)(2,1)S(1)} %collective-permute-done.19.far_ref, bf16[1,2,2048,768]{3,2,1,0:T(8,128)(2,1)S(1)} %get-tuple-element.25.in_ref, ...), custom_call_target="tpu_custom_call" | custom-call | flops 2415919104 | bytes 1572864 | tf_op jit(solution)/shard_map/visit/pallas_call | solution.py:196
  34.3 0.1 collective-permute-start.20
  34.4 2.3 %collective-permute-done.7.near_ref = bf16[128,2176]{1,0:T(8,128)(2,1)S(1)} collective-permute-done((bf16[128,2176]{1,0:T(8,128)(2,1)S(1)}, bf16[128,2176]{1,0:T(8,128)(2,1)S(1)}, u32[]{:S(2)}, u32[]{:S(2)}) %collective-permute-start.7) | collective-permute-done | bytes 557088 | tf_op jit(solution)/shard_map/ppermute | solution.py:242
  36.7 2.1 %collective-permute-start.8 = (bf16[128,2176]{1,0:T(8,128)(2,1)S(1)}, bf16[128,2176]{1,0:T(8,128)(2,1)S(1)}, u32[]{:S(2)}, u32[]{:S(2)}) collective-permute-start(bf16[128,2176]{1,0:T(8,128)(2,1)S(1)} %collective-permute-done.7.near_ref), channel_id=1, source_target_pairs={{0,4},{5,1},{4,8},{9,5},{8,12},{13,9},{12,14},{15,13},{14,10},{11,... | collective-permute-start | bytes 1671176 | tf_op jit(solution)/shard_map/ppermute | solution.py:242
  38.8 3.5 %collective-permute-done.23 = bf16[128,2048]{1,0:T(8,128)(2,1)S(1)} collective-permute-done((bf16[128,2048]{1,0:T(8,128)(2,1)S(1)}, bf16[128,2048]{1,0:T(8,128)(2,1)S(1)}, u32[]{:S(2)}, u32[]{:S(2)}) %collective-permute-start.23) | collective-permute-done | bytes 524320 | tf_op jit(solution)/shard_map/ppermute | solution.py:252
  42.3 0.2 add_convert_fusion.3
  42.5 2.1 %collective-permute-start.24 = (bf16[128,2048]{1,0:T(8,128)(2,1)S(1)}, bf16[128,2048]{1,0:T(8,128)(2,1)S(1)}, u32[]{:S(2)}, u32[]{:S(2)}) collective-permute-start(bf16[128,2048]{1,0:T(8,128)(2,1)S(1)} %add_convert_fusion.3), channel_id=1, source_target_pairs={{0,4},{5,1},{4,8},{9,5},{8,12},{13,9},{12,14},{15,13},{14,10},{11,... | collective-permute-start | bytes 1572872 | tf_op jit(solution)/shard_map/ppermute | solution.py:252
  44.6 3.3 %visit.13 = (f32[128,2048]{1,0:T(8,128)S(1)}, bf16[128,2048]{1,0:T(8,128)(2,1)S(1)}) custom-call(s32[1]{0:T(128)} %found.1.mine_ref, bf16[128,2176]{1,0:T(8,128)(2,1)S(1)} %collective-permute-done.7.near_ref, bf16[128,2176]{1,0:T(8,128)(2,1)S(1)} %collective-permute-done.17.far_ref, bf16[1,2,2048,768]{3,2,1,0:T(8,128)(2,1)S(1)} %get-tuple-element.25.in_ref, ...), custom_call_target="tpu_custom_call" | custom-call | flops 2415919104 | bytes 1572864 | tf_op jit(solution)/shard_map/visit/pallas_call | solution.py:196
  48.1 0.2 collective-permute-done.8.near_ref
  48.3 0.3 collective-permute-start.15
  48.6 1.8 %collective-permute-start.9 = (bf16[128,2176]{1,0:T(8,128)(2,1)S(1)}, bf16[128,2176]{1,0:T(8,128)(2,1)S(1)}, u32[]{:S(2)}, u32[]{:S(2)}) collective-permute-start(bf16[128,2176]{1,0:T(8,128)(2,1)S(1)} %collective-permute-done.8.near_ref), channel_id=1, source_target_pairs={{0,4},{5,1},{4,8},{9,5},{8,12},{13,9},{12,14},{15,13},{14,10},{11,... | collective-permute-start | bytes 1671176 | tf_op jit(solution)/shard_map/ppermute | solution.py:242
  50.4 3.5 %collective-permute-done.24 = bf16[128,2048]{1,0:T(8,128)(2,1)S(1)} collective-permute-done((bf16[128,2048]{1,0:T(8,128)(2,1)S(1)}, bf16[128,2048]{1,0:T(8,128)(2,1)S(1)}, u32[]{:S(2)}, u32[]{:S(2)}) %collective-permute-start.24) | collective-permute-done | bytes 524320 | tf_op jit(solution)/shard_map/ppermute | solution.py:252
  53.9 0.2 add_convert_fusion.2
  54.1 2.1 %collective-permute-start.25 = (bf16[128,2048]{1,0:T(8,128)(2,1)S(1)}, bf16[128,2048]{1,0:T(8,128)(2,1)S(1)}, u32[]{:S(2)}, u32[]{:S(2)}) collective-permute-start(bf16[128,2048]{1,0:T(8,128)(2,1)S(1)} %add_convert_fusion.2), channel_id=1, source_target_pairs={{0,4},{5,1},{4,8},{9,5},{8,12},{13,9},{12,14},{15,13},{14,10},{11,... | collective-permute-start | bytes 1572872 | tf_op jit(solution)/shard_map/ppermute | solution.py:252
  56.2 3.3 %visit.12 = (f32[128,2048]{1,0:T(8,128)S(1)}, bf16[128,2048]{1,0:T(8,128)(2,1)S(1)}) custom-call(s32[1]{0:T(128)} %found.1.mine_ref, bf16[128,2176]{1,0:T(8,128)(2,1)S(1)} %collective-permute-done.8.near_ref, bf16[128,2176]{1,0:T(8,128)(2,1)S(1)} %collective-permute-done.15.far_ref, bf16[1,2,2048,768]{3,2,1,0:T(8,128)(2,1)S(1)} %get-tuple-element.25.in_ref, ...), custom_call_target="tpu_custom_call" | custom-call | flops 2415919104 | bytes 1572864 | tf_op jit(solution)/shard_map/visit/pallas_call | solution.py:196
  59.6 0.1 collective-permute-start.16
  59.7 0.2 collective-permute-done.9.near_ref
  59.9 0.3 collective-permute-start.13
  60.2 1.7 %collective-permute-start.2 = (bf16[128,2176]{1,0:T(8,128)(2,1)S(1)}, bf16[128,2176]{1,0:T(8,128)(2,1)S(1)}, u32[]{:S(2)}, u32[]{:S(2)}) collective-permute-start(bf16[128,2176]{1,0:T(8,128)(2,1)S(1)} %packed.1.near_ref), channel_id=1, source_target_pairs={{4,0},{1,5},{8,4},{5,9},{12,8},{9,13},{14,12},{13,15},{10,14},{15,... | collective-permute-start | bytes 1671176 | tf_op jit(solution)/shard_map/ppermute | solution.py:236
  61.9 0.3 collective-permute-start.10
  62.2 5.5 %collective-permute-done.25 = bf16[128,2048]{1,0:T(8,128)(2,1)S(1)} collective-permute-done((bf16[128,2048]{1,0:T(8,128)(2,1)S(1)}, bf16[128,2048]{1,0:T(8,128)(2,1)S(1)}, u32[]{:S(2)}, u32[]{:S(2)}) %collective-permute-start.25) | collective-permute-done | bytes 524320 | tf_op jit(solution)/shard_map/ppermute | solution.py:252
  67.7 0.2 add_convert_fusion.1
  67.9 2.6 %collective-permute-start.26 = (bf16[128,2048]{1,0:T(8,128)(2,1)S(1)}, bf16[128,2048]{1,0:T(8,128)(2,1)S(1)}, u32[]{:S(2)}, u32[]{:S(2)}) collective-permute-start(bf16[128,2048]{1,0:T(8,128)(2,1)S(1)} %add_convert_fusion.1), channel_id=1, source_target_pairs={{0,4},{5,1},{4,8},{9,5},{8,12},{13,9},{12,14},{15,13},{14,10},{11,... | collective-permute-start | bytes 1572872 | tf_op jit(solution)/shard_map/ppermute | solution.py:252
  70.5 3.3 %visit.11 = (f32[128,2048]{1,0:T(8,128)S(1)}, bf16[128,2048]{1,0:T(8,128)(2,1)S(1)}) custom-call(s32[1]{0:T(128)} %found.1.mine_ref, bf16[128,2176]{1,0:T(8,128)(2,1)S(1)} %collective-permute-done.9.near_ref, bf16[128,2176]{1,0:T(8,128)(2,1)S(1)} %collective-permute-done.13.far_ref, bf16[1,2,2048,768]{3,2,1,0:T(8,128)(2,1)S(1)} %get-tuple-element.25.in_ref, ...), custom_call_target="tpu_custom_call" | custom-call | flops 2415919104 | bytes 1572864 | tf_op jit(solution)/shard_map/visit/pallas_call | solution.py:196
  73.9 0.1 collective-permute-start.14
  73.9 3.5 %collective-permute-done.10.near_ref = bf16[128,2176]{1,0:T(8,128)(2,1)S(1)} collective-permute-done((bf16[128,2176]{1,0:T(8,128)(2,1)S(1)}, bf16[128,2176]{1,0:T(8,128)(2,1)S(1)}, u32[]{:S(2)}, u32[]{:S(2)}) %collective-permute-start.10) | collective-permute-done | bytes 557088 | tf_op jit(solution)/shard_map/ppermute | solution.py:242
  77.4 0.5 collective-permute-start
  77.9 5.1 %collective-permute-done.26 = bf16[128,2048]{1,0:T(8,128)(2,1)S(1)} collective-permute-done((bf16[128,2048]{1,0:T(8,128)(2,1)S(1)}, bf16[128,2048]{1,0:T(8,128)(2,1)S(1)}, u32[]{:S(2)}, u32[]{:S(2)}) %collective-permute-start.26) | collective-permute-done | bytes 524320 | tf_op jit(solution)/shard_map/ppermute | solution.py:252
  83.0 0.2 add_convert_fusion
  83.2 2.1 %collective-permute-start.27 = (bf16[128,2048]{1,0:T(8,128)(2,1)S(1)}, bf16[128,2048]{1,0:T(8,128)(2,1)S(1)}, u32[]{:S(2)}, u32[]{:S(2)}) collective-permute-start(bf16[128,2048]{1,0:T(8,128)(2,1)S(1)} %add_convert_fusion), channel_id=1, source_target_pairs={{0,4},{5,1},{4,8},{9,5},{8,12},{13,9},{12,14},{15,13},{14,10},{11,... | collective-permute-start | bytes 1572872 | tf_op jit(solution)/shard_map/ppermute | solution.py:252
  85.4 3.4 %visit.10 = (f32[128,2048]{1,0:T(8,128)S(1)}, bf16[128,2048]{1,0:T(8,128)(2,1)S(1)}) custom-call(s32[1]{0:T(128)} %found.1.mine_ref, bf16[128,2176]{1,0:T(8,128)(2,1)S(1)} %collective-permute-done.10.near_ref, bf16[128,2176]{1,0:T(8,128)(2,1)S(1)} %collective-permute-done.11.far_ref, bf16[1,2,2048,768]{3,2,1,0:T(8,128)(2,1)S(1)} %get-tuple-element.25.in_ref, ...), custom_call_target="tpu_custom_call" | custom-call | flops 2415919104 | bytes 1572864 | tf_op jit(solution)/shard_map/visit/pallas_call | solution.py:196
  88.7 0.1 collective-permute-start.12
  88.8 3.3 %visit.8 = (f32[128,2048]{1,0:T(8,128)S(1)}, bf16[128,2048]{1,0:T(8,128)(2,1)S(1)}) custom-call(s32[1]{0:T(128)} %found.1.mine_ref, bf16[128,2176]{1,0:T(8,128)(2,1)S(1)} %packed.1.near_ref, bf16[128,2176]{1,0:T(8,128)(2,1)S(1)} %collective-permute-done.far_ref, bf16[1,2,2048,768]{3,2,1,0:T(8,128)(2,1)S(1)} %get-tuple-element.25.in_ref, ...), custom_call_target="tpu_custom_call" | custom-call | flops 2415919104 | bytes 1572864 | tf_op jit(solution)/shard_map/visit/pallas_call | solution.py:196
  92.2 0.6 collective-permute-start.1
  92.7 3.3 %visit.9 = (f32[128,2048]{1,0:T(8,128)S(1)}, bf16[128,2048]{1,0:T(8,128)(2,1)S(1)}) custom-call(s32[1]{0:T(128)} %found.1.mine_ref, bf16[128,2176]{1,0:T(8,128)(2,1)S(1)} %collective-permute-done.2.near_ref, bf16[128,2176]{1,0:T(8,128)(2,1)S(1)} %collective-permute-done.3.far_ref, bf16[1,2,2048,768]{3,2,1,0:T(8,128)(2,1)S(1)} %get-tuple-element.25.in_ref, ...), custom_call_target="tpu_custom_call" | custom-call | flops 2415919104 | bytes 1572864 | tf_op jit(solution)/shard_map/visit/pallas_call | solution.py:196
  96.1 0.1 collective-permute-start.4
  96.2 0.1 add_convert_fusion.10
  96.2 1.6 %collective-permute-start.28 = (bf16[56,2048]{1,0:T(8,128)(2,1)S(1)}, bf16[56,2048]{1,0:T(8,128)(2,1)S(1)}, u32[]{:S(2)}, u32[]{:S(2)}) collective-permute-start(bf16[56,2048]{1,0:T(8,128)(2,1)S(1)} %add_convert_fusion.10), channel_id=1, source_target_pairs={{0,4},{5,1},{4,8},{9,5},{8,12},{13,9},{12,14},{15,13},{14,10},{11,... | collective-permute-start | bytes 688136 | tf_op jit(solution)/shard_map/ppermute | solution.py:257
  97.9 0.1 add_convert_fusion.7
  98.0 1.6 %collective-permute-start.30 = (bf16[72,2048]{1,0:T(8,128)(2,1)S(1)}, bf16[72,2048]{1,0:T(8,128)(2,1)S(1)}, u32[]{:S(2)}, u32[]{:S(2)}) collective-permute-start(bf16[72,2048]{1,0:T(8,128)(2,1)S(1)} %add_convert_fusion.7), channel_id=1, source_target_pairs={{0,4},{5,1},{4,8},{9,5},{8,12},{13,9},{12,14},{15,13},{14,10},{11,... | collective-permute-start | bytes 884744 | tf_op jit(solution)/shard_map/ppermute | solution.py:257
  99.6 2.7 %collective-permute-done.28 = bf16[56,2048]{1,0:T(8,128)(2,1)S(1)} collective-permute-done((bf16[56,2048]{1,0:T(8,128)(2,1)S(1)}, bf16[56,2048]{1,0:T(8,128)(2,1)S(1)}, u32[]{:S(2)}, u32[]{:S(2)}) %collective-permute-start.28) | collective-permute-done | bytes 229408 | tf_op jit(solution)/shard_map/ppermute | solution.py:257
  102.3 0.1 add_convert_fusion.9
  102.4 1.6 %collective-permute-start.29 = (bf16[56,2048]{1,0:T(8,128)(2,1)S(1)}, bf16[56,2048]{1,0:T(8,128)(2,1)S(1)}, u32[]{:S(2)}, u32[]{:S(2)}) collective-permute-start(bf16[56,2048]{1,0:T(8,128)(2,1)S(1)} %add_convert_fusion.9), channel_id=1, source_target_pairs={{0,4},{5,1},{4,8},{9,5},{8,12},{13,9},{12,14},{15,13},{14,10},{11,... | collective-permute-start | bytes 688136 | tf_op jit(solution)/shard_map/ppermute | solution.py:257
  104.0 1.4 %collective-permute-done.30 = bf16[72,2048]{1,0:T(8,128)(2,1)S(1)} collective-permute-done((bf16[72,2048]{1,0:T(8,128)(2,1)S(1)}, bf16[72,2048]{1,0:T(8,128)(2,1)S(1)}, u32[]{:S(2)}, u32[]{:S(2)}) %collective-permute-start.30) | collective-permute-done | bytes 294944 | tf_op jit(solution)/shard_map/ppermute | solution.py:257
  105.5 0.1 add_convert_fusion.6
  105.6 1.6 %collective-permute-start.31 = (bf16[72,2048]{1,0:T(8,128)(2,1)S(1)}, bf16[72,2048]{1,0:T(8,128)(2,1)S(1)}, u32[]{:S(2)}, u32[]{:S(2)}) collective-permute-start(bf16[72,2048]{1,0:T(8,128)(2,1)S(1)} %add_convert_fusion.6), channel_id=1, source_target_pairs={{0,4},{5,1},{4,8},{9,5},{8,12},{13,9},{12,14},{15,13},{14,10},{11,... | collective-permute-start | bytes 884744 | tf_op jit(solution)/shard_map/ppermute | solution.py:257
  107.2 1.3 %collective-permute-done.29 = bf16[56,2048]{1,0:T(8,128)(2,1)S(1)} collective-permute-done((bf16[56,2048]{1,0:T(8,128)(2,1)S(1)}, bf16[56,2048]{1,0:T(8,128)(2,1)S(1)}, u32[]{:S(2)}, u32[]{:S(2)}) %collective-permute-start.29) | collective-permute-done | bytes 229408 | tf_op jit(solution)/shard_map/ppermute | solution.py:257
  108.5 0.1 add_convert_fusion.8
  108.6 3.8 %collective-permute-done.31 = bf16[72,2048]{1,0:T(8,128)(2,1)S(1)} collective-permute-done((bf16[72,2048]{1,0:T(8,128)(2,1)S(1)}, bf16[72,2048]{1,0:T(8,128)(2,1)S(1)}, u32[]{:S(2)}, u32[]{:S(2)}) %collective-permute-start.31) | collective-permute-done | bytes 294944 | tf_op jit(solution)/shard_map/ppermute | solution.py:257
  112.4 0.1 add_convert_fusion.5
  112.5 0.8 pad_maximum_fusion
  (25 shorter events, 0.1 us)
Async XLA Ops:
  1.3 10.6 %collective-permute-start.5 = (bf16[128,2176]{1,0:T(8,128)(2,1)S(1)}, bf16[128,2176]{1,0:T(8,128)(2,1)S(1)}, u32[]{:S(2)}, u32[]{:S(2)}) collective-permute-start(bf16[128,2176]{1,0:T(8,128)(2,1)S(1)} %packed.1.near_ref), channel_id=1, source_target_pairs={{0,4},{5,1},{4,8},{9,5},{8,12},{13,9},{12,14},{15,13},{14,10},{11,... | collective-permute-start | bytes 1671176 | tf_op jit(solution)/shard_map/ppermute | solution.py:242
  11.9 7.8 %collective-permute-start.21 = (bf16[128,2176]{1,0:T(8,128)(2,1)S(1)}, bf16[128,2176]{1,0:T(8,128)(2,1)S(1)}, u32[]{:S(2)}, u32[]{:S(2)}) collective-permute-start(bf16[128,2176]{1,0:T(8,128)(2,1)S(1)} %collective-permute-done.5.near_ref), channel_id=1, source_target_pairs={{0,1},{1,0},{2,3},{3,2},{4,5},{5,4},{6,7},{7,6},{8,9},{9,8},{10,11... | collective-permute-start | bytes 1671176 | tf_op jit(solution)/shard_map/ppermute | solution.py:240
  11.9 0.7 copy-start
  17.6 9.6 %collective-permute-start.6 = (bf16[128,2176]{1,0:T(8,128)(2,1)S(1)}, bf16[128,2176]{1,0:T(8,128)(2,1)S(1)}, u32[]{:S(2)}, u32[]{:S(2)}) collective-permute-start(bf16[128,2176]{1,0:T(8,128)(2,1)S(1)} %collective-permute-done.5.near_ref), channel_id=1, source_target_pairs={{0,4},{5,1},{4,8},{9,5},{8,12},{13,9},{12,14},{15,13},{14,10},{11,... | collective-permute-start | bytes 1671176 | tf_op jit(solution)/shard_map/ppermute | solution.py:242
  23.0 6.2 %collective-permute-start.22 = (bf16[128,2048]{1,0:T(8,128)(2,1)S(1)}, bf16[128,2048]{1,0:T(8,128)(2,1)S(1)}, u32[]{:S(2)}, u32[]{:S(2)}) collective-permute-start(bf16[128,2048]{1,0:T(8,128)(2,1)S(1)} %get-tuple-element.44), channel_id=1, source_target_pairs={{0,1},{1,0},{2,3},{3,2},{4,5},{5,4},{6,7},{7,6},{8,9},{9,8},{10,11... | collective-permute-start | bytes 1572872 | tf_op jit(solution)/shard_map/ppermute | solution.py:244
  27.2 3.8 %collective-permute-start.19 = (bf16[128,2176]{1,0:T(8,128)(2,1)S(1)}, bf16[128,2176]{1,0:T(8,128)(2,1)S(1)}, u32[]{:S(2)}, u32[]{:S(2)}) collective-permute-start(bf16[128,2176]{1,0:T(8,128)(2,1)S(1)} %collective-permute-done.6.near_ref), channel_id=1, source_target_pairs={{0,1},{1,0},{2,3},{3,2},{4,5},{5,4},{6,7},{7,6},{8,9},{9,8},{10,11... | collective-permute-start | bytes 1671176 | tf_op jit(solution)/shard_map/ppermute | solution.py:240
  27.2 9.5 %collective-permute-start.7 = (bf16[128,2176]{1,0:T(8,128)(2,1)S(1)}, bf16[128,2176]{1,0:T(8,128)(2,1)S(1)}, u32[]{:S(2)}, u32[]{:S(2)}) collective-permute-start(bf16[128,2176]{1,0:T(8,128)(2,1)S(1)} %collective-permute-done.6.near_ref), channel_id=1, source_target_pairs={{0,4},{5,1},{4,8},{9,5},{8,12},{13,9},{12,14},{15,13},{14,10},{11,... | collective-permute-start | bytes 1671176 | tf_op jit(solution)/shard_map/ppermute | solution.py:242
  29.4 12.9 %collective-permute-start.23 = (bf16[128,2048]{1,0:T(8,128)(2,1)S(1)}, bf16[128,2048]{1,0:T(8,128)(2,1)S(1)}, u32[]{:S(2)}, u32[]{:S(2)}) collective-permute-start(bf16[128,2048]{1,0:T(8,128)(2,1)S(1)} %add_convert_fusion.4), channel_id=1, source_target_pairs={{0,4},{5,1},{4,8},{9,5},{8,12},{13,9},{12,14},{15,13},{14,10},{11,... | collective-permute-start | bytes 1572872 | tf_op jit(solution)/shard_map/ppermute | solution.py:252
  34.3 8.0 %collective-permute-start.20 = (bf16[128,2048]{1,0:T(8,128)(2,1)S(1)}, bf16[128,2048]{1,0:T(8,128)(2,1)S(1)}, u32[]{:S(2)}, u32[]{:S(2)}) collective-permute-start(bf16[128,2048]{1,0:T(8,128)(2,1)S(1)} %get-tuple-element.42), channel_id=1, source_target_pairs={{0,1},{1,0},{2,3},{3,2},{4,5},{5,4},{6,7},{7,6},{8,9},{9,8},{10,11... | collective-permute-start | bytes 1572872 | tf_op jit(solution)/shard_map/ppermute | solution.py:244
  36.7 8.0 %collective-permute-start.17 = (bf16[128,2176]{1,0:T(8,128)(2,1)S(1)}, bf16[128,2176]{1,0:T(8,128)(2,1)S(1)}, u32[]{:S(2)}, u32[]{:S(2)}) collective-permute-start(bf16[128,2176]{1,0:T(8,128)(2,1)S(1)} %collective-permute-done.7.near_ref), channel_id=1, source_target_pairs={{0,1},{1,0},{2,3},{3,2},{4,5},{5,4},{6,7},{7,6},{8,9},{9,8},{10,11... | collective-permute-start | bytes 1671176 | tf_op jit(solution)/shard_map/ppermute | solution.py:240
  36.7 11.6 %collective-permute-start.8 = (bf16[128,2176]{1,0:T(8,128)(2,1)S(1)}, bf16[128,2176]{1,0:T(8,128)(2,1)S(1)}, u32[]{:S(2)}, u32[]{:S(2)}) collective-permute-start(bf16[128,2176]{1,0:T(8,128)(2,1)S(1)} %collective-permute-done.7.near_ref), channel_id=1, source_target_pairs={{0,4},{5,1},{4,8},{9,5},{8,12},{13,9},{12,14},{15,13},{14,10},{11,... | collective-permute-start | bytes 1671176 | tf_op jit(solution)/shard_map/ppermute | solution.py:242
  42.5 11.4 %collective-permute-start.24 = (bf16[128,2048]{1,0:T(8,128)(2,1)S(1)}, bf16[128,2048]{1,0:T(8,128)(2,1)S(1)}, u32[]{:S(2)}, u32[]{:S(2)}) collective-permute-start(bf16[128,2048]{1,0:T(8,128)(2,1)S(1)} %add_convert_fusion.3), channel_id=1, source_target_pairs={{0,4},{5,1},{4,8},{9,5},{8,12},{13,9},{12,14},{15,13},{14,10},{11,... | collective-permute-start | bytes 1572872 | tf_op jit(solution)/shard_map/ppermute | solution.py:252
  48.0 5.9 %collective-permute-start.18 = (bf16[128,2048]{1,0:T(8,128)(2,1)S(1)}, bf16[128,2048]{1,0:T(8,128)(2,1)S(1)}, u32[]{:S(2)}, u32[]{:S(2)}) collective-permute-start(bf16[128,2048]{1,0:T(8,128)(2,1)S(1)} %get-tuple-element.40), channel_id=1, source_target_pairs={{0,1},{1,0},{2,3},{3,2},{4,5},{5,4},{6,7},{7,6},{8,9},{9,8},{10,11... | collective-permute-start | bytes 1572872 | tf_op jit(solution)/shard_map/ppermute | solution.py:244
  48.3 8.0 %collective-permute-start.15 = (bf16[128,2176]{1,0:T(8,128)(2,1)S(1)}, bf16[128,2176]{1,0:T(8,128)(2,1)S(1)}, u32[]{:S(2)}, u32[]{:S(2)}) collective-permute-start(bf16[128,2176]{1,0:T(8,128)(2,1)S(1)} %collective-permute-done.8.near_ref), channel_id=1, source_target_pairs={{0,1},{1,0},{2,3},{3,2},{4,5},{5,4},{6,7},{7,6},{8,9},{9,8},{10,11... | collective-permute-start | bytes 1671176 | tf_op jit(solution)/shard_map/ppermute | solution.py:240
  48.6 11.3 %collective-permute-start.9 = (bf16[128,2176]{1,0:T(8,128)(2,1)S(1)}, bf16[128,2176]{1,0:T(8,128)(2,1)S(1)}, u32[]{:S(2)}, u32[]{:S(2)}) collective-permute-start(bf16[128,2176]{1,0:T(8,128)(2,1)S(1)} %collective-permute-done.8.near_ref), channel_id=1, source_target_pairs={{0,4},{5,1},{4,8},{9,5},{8,12},{13,9},{12,14},{15,13},{14,10},{11,... | collective-permute-start | bytes 1671176 | tf_op jit(solution)/shard_map/ppermute | solution.py:242
  54.1 13.6 %collective-permute-start.25 = (bf16[128,2048]{1,0:T(8,128)(2,1)S(1)}, bf16[128,2048]{1,0:T(8,128)(2,1)S(1)}, u32[]{:S(2)}, u32[]{:S(2)}) collective-permute-start(bf16[128,2048]{1,0:T(8,128)(2,1)S(1)} %add_convert_fusion.2), channel_id=1, source_target_pairs={{0,4},{5,1},{4,8},{9,5},{8,12},{13,9},{12,14},{15,13},{14,10},{11,... | collective-permute-start | bytes 1572872 | tf_op jit(solution)/shard_map/ppermute | solution.py:252
  59.6 8.1 %collective-permute-start.16 = (bf16[128,2048]{1,0:T(8,128)(2,1)S(1)}, bf16[128,2048]{1,0:T(8,128)(2,1)S(1)}, u32[]{:S(2)}, u32[]{:S(2)}) collective-permute-start(bf16[128,2048]{1,0:T(8,128)(2,1)S(1)} %get-tuple-element.38), channel_id=1, source_target_pairs={{0,1},{1,0},{2,3},{3,2},{4,5},{5,4},{6,7},{7,6},{8,9},{9,8},{10,11... | collective-permute-start | bytes 1572872 | tf_op jit(solution)/shard_map/ppermute | solution.py:244
  59.9 10.7 %collective-permute-start.13 = (bf16[128,2176]{1,0:T(8,128)(2,1)S(1)}, bf16[128,2176]{1,0:T(8,128)(2,1)S(1)}, u32[]{:S(2)}, u32[]{:S(2)}) collective-permute-start(bf16[128,2176]{1,0:T(8,128)(2,1)S(1)} %collective-permute-done.9.near_ref), channel_id=1, source_target_pairs={{0,1},{1,0},{2,3},{3,2},{4,5},{5,4},{6,7},{7,6},{8,9},{9,8},{10,11... | collective-permute-start | bytes 1671176 | tf_op jit(solution)/shard_map/ppermute | solution.py:240
  60.2 17.8 %collective-permute-start.2 = (bf16[128,2176]{1,0:T(8,128)(2,1)S(1)}, bf16[128,2176]{1,0:T(8,128)(2,1)S(1)}, u32[]{:S(2)}, u32[]{:S(2)}) collective-permute-start(bf16[128,2176]{1,0:T(8,128)(2,1)S(1)} %packed.1.near_ref), channel_id=1, source_target_pairs={{4,0},{1,5},{8,4},{5,9},{12,8},{9,13},{14,12},{13,15},{10,14},{15,... | collective-permute-start | bytes 1671176 | tf_op jit(solution)/shard_map/ppermute | solution.py:236
  61.9 15.5 %collective-permute-start.10 = (bf16[128,2176]{1,0:T(8,128)(2,1)S(1)}, bf16[128,2176]{1,0:T(8,128)(2,1)S(1)}, u32[]{:S(2)}, u32[]{:S(2)}) collective-permute-start(bf16[128,2176]{1,0:T(8,128)(2,1)S(1)} %collective-permute-done.9.near_ref), channel_id=1, source_target_pairs={{0,4},{5,1},{4,8},{9,5},{8,12},{13,9},{12,14},{15,13},{14,10},{11,... | collective-permute-start | bytes 1671176 | tf_op jit(solution)/shard_map/ppermute | solution.py:242
  67.9 15.1 %collective-permute-start.26 = (bf16[128,2048]{1,0:T(8,128)(2,1)S(1)}, bf16[128,2048]{1,0:T(8,128)(2,1)S(1)}, u32[]{:S(2)}, u32[]{:S(2)}) collective-permute-start(bf16[128,2048]{1,0:T(8,128)(2,1)S(1)} %add_convert_fusion.1), channel_id=1, source_target_pairs={{0,4},{5,1},{4,8},{9,5},{8,12},{13,9},{12,14},{15,13},{14,10},{11,... | collective-permute-start | bytes 1572872 | tf_op jit(solution)/shard_map/ppermute | solution.py:252
  73.9 9.2 %collective-permute-start.14 = (bf16[128,2048]{1,0:T(8,128)(2,1)S(1)}, bf16[128,2048]{1,0:T(8,128)(2,1)S(1)}, u32[]{:S(2)}, u32[]{:S(2)}) collective-permute-start(bf16[128,2048]{1,0:T(8,128)(2,1)S(1)} %get-tuple-element.36), channel_id=1, source_target_pairs={{0,1},{1,0},{2,3},{3,2},{4,5},{5,4},{6,7},{7,6},{8,9},{9,8},{10,11... | collective-permute-start | bytes 1572872 | tf_op jit(solution)/shard_map/ppermute | solution.py:244
  77.4 8.0 %collective-permute-start.11 = (bf16[128,2176]{1,0:T(8,128)(2,1)S(1)}, bf16[128,2176]{1,0:T(8,128)(2,1)S(1)}, u32[]{:S(2)}, u32[]{:S(2)}) collective-permute-start(bf16[128,2176]{1,0:T(8,128)(2,1)S(1)} %collective-permute-done.10.near_ref), channel_id=1, source_target_pairs={{0,1},{1,0},{2,3},{3,2},{4,5},{5,4},{6,7},{7,6},{8,9},{9,8},{10,11... | collective-permute-start | bytes 1671176 | tf_op jit(solution)/shard_map/ppermute | solution.py:240
  77.4 11.4 %collective-permute-start = (bf16[128,2176]{1,0:T(8,128)(2,1)S(1)}, bf16[128,2176]{1,0:T(8,128)(2,1)S(1)}, u32[]{:S(2)}, u32[]{:S(2)}) collective-permute-start(bf16[128,2176]{1,0:T(8,128)(2,1)S(1)} %packed.1.near_ref), channel_id=1, source_target_pairs={{0,1},{1,0},{2,3},{3,2},{4,5},{5,4},{6,7},{7,6},{8,9},{9,8},{10,11... | collective-permute-start | bytes 1671176 | tf_op jit(solution)/shard_map/ppermute | solution.py:240
  77.9 14.8 %collective-permute-start.3 = (bf16[128,2176]{1,0:T(8,128)(2,1)S(1)}, bf16[128,2176]{1,0:T(8,128)(2,1)S(1)}, u32[]{:S(2)}, u32[]{:S(2)}) collective-permute-start(bf16[128,2176]{1,0:T(8,128)(2,1)S(1)} %collective-permute-done.2.near_ref), channel_id=1, source_target_pairs={{0,1},{1,0},{2,3},{3,2},{4,5},{5,4},{6,7},{7,6},{8,9},{9,8},{10,11... | collective-permute-start | bytes 1671176 | tf_op jit(solution)/shard_map/ppermute | solution.py:240
  83.2 12.9 %collective-permute-start.27 = (bf16[128,2048]{1,0:T(8,128)(2,1)S(1)}, bf16[128,2048]{1,0:T(8,128)(2,1)S(1)}, u32[]{:S(2)}, u32[]{:S(2)}) collective-permute-start(bf16[128,2048]{1,0:T(8,128)(2,1)S(1)} %add_convert_fusion), channel_id=1, source_target_pairs={{0,4},{5,1},{4,8},{9,5},{8,12},{13,9},{12,14},{15,13},{14,10},{11,... | collective-permute-start | bytes 1572872 | tf_op jit(solution)/shard_map/ppermute | solution.py:252
  88.7 7.4 %collective-permute-start.12 = (bf16[128,2048]{1,0:T(8,128)(2,1)S(1)}, bf16[128,2048]{1,0:T(8,128)(2,1)S(1)}, u32[]{:S(2)}, u32[]{:S(2)}) collective-permute-start(bf16[128,2048]{1,0:T(8,128)(2,1)S(1)} %get-tuple-element.34), channel_id=1, source_target_pairs={{0,1},{1,0},{2,3},{3,2},{4,5},{5,4},{6,7},{7,6},{8,9},{9,8},{10,11... | collective-permute-start | bytes 1572872 | tf_op jit(solution)/shard_map/ppermute | solution.py:244
  92.2 15.1 %collective-permute-start.1 = (bf16[128,2048]{1,0:T(8,128)(2,1)S(1)}, bf16[128,2048]{1,0:T(8,128)(2,1)S(1)}, u32[]{:S(2)}, u32[]{:S(2)}) collective-permute-start(bf16[128,2048]{1,0:T(8,128)(2,1)S(1)} %get-tuple-element.30), channel_id=1, source_target_pairs={{0,1},{1,0},{2,3},{3,2},{4,5},{5,4},{6,7},{7,6},{8,9},{9,8},{10,11... | collective-permute-start | bytes 1572872 | tf_op jit(solution)/shard_map/ppermute | solution.py:244
  96.1 3.6 %collective-permute-start.4 = (bf16[128,2048]{1,0:T(8,128)(2,1)S(1)}, bf16[128,2048]{1,0:T(8,128)(2,1)S(1)}, u32[]{:S(2)}, u32[]{:S(2)}) collective-permute-start(bf16[128,2048]{1,0:T(8,128)(2,1)S(1)} %get-tuple-element.32), channel_id=1, source_target_pairs={{0,1},{1,0},{2,3},{3,2},{4,5},{5,4},{6,7},{7,6},{8,9},{9,8},{10,11... | collective-permute-start | bytes 1572872 | tf_op jit(solution)/shard_map/ppermute | solution.py:244
  96.2 6.1 %collective-permute-start.28 = (bf16[56,2048]{1,0:T(8,128)(2,1)S(1)}, bf16[56,2048]{1,0:T(8,128)(2,1)S(1)}, u32[]{:S(2)}, u32[]{:S(2)}) collective-permute-start(bf16[56,2048]{1,0:T(8,128)(2,1)S(1)} %add_convert_fusion.10), channel_id=1, source_target_pairs={{0,4},{5,1},{4,8},{9,5},{8,12},{13,9},{12,14},{15,13},{14,10},{11,... | collective-permute-start | bytes 688136 | tf_op jit(solution)/shard_map/ppermute | solution.py:257
  98.0 7.5 %collective-permute-start.30 = (bf16[72,2048]{1,0:T(8,128)(2,1)S(1)}, bf16[72,2048]{1,0:T(8,128)(2,1)S(1)}, u32[]{:S(2)}, u32[]{:S(2)}) collective-permute-start(bf16[72,2048]{1,0:T(8,128)(2,1)S(1)} %add_convert_fusion.7), channel_id=1, source_target_pairs={{0,4},{5,1},{4,8},{9,5},{8,12},{13,9},{12,14},{15,13},{14,10},{11,... | collective-permute-start | bytes 884744 | tf_op jit(solution)/shard_map/ppermute | solution.py:257
  102.4 6.1 %collective-permute-start.29 = (bf16[56,2048]{1,0:T(8,128)(2,1)S(1)}, bf16[56,2048]{1,0:T(8,128)(2,1)S(1)}, u32[]{:S(2)}, u32[]{:S(2)}) collective-permute-start(bf16[56,2048]{1,0:T(8,128)(2,1)S(1)} %add_convert_fusion.9), channel_id=1, source_target_pairs={{0,4},{5,1},{4,8},{9,5},{8,12},{13,9},{12,14},{15,13},{14,10},{11,... | collective-permute-start | bytes 688136 | tf_op jit(solution)/shard_map/ppermute | solution.py:257
  105.6 6.8 %collective-permute-start.31 = (bf16[72,2048]{1,0:T(8,128)(2,1)S(1)}, bf16[72,2048]{1,0:T(8,128)(2,1)S(1)}, u32[]{:S(2)}, u32[]{:S(2)}) collective-permute-start(bf16[72,2048]{1,0:T(8,128)(2,1)S(1)} %add_convert_fusion.6), channel_id=1, source_target_pairs={{0,4},{5,1},{4,8},{9,5},{8,12},{13,9},{12,14},{15,13},{14,10},{11,... | collective-permute-start | bytes 884744 | tf_op jit(solution)/shard_map/ppermute | solution.py:257
